TPU v7x, 32 devices: a whole 2x2x4 slice. The times are simulated.
32 devices in a mesh: dp: 4 (over y, core), fsdp: 8 (over z, x).
Axes of the slice: x: 2, y: 2, z: 4, core: 2. Of those that a mesh axis runs over, the one named last changes fastest.
Arguments:
- tokens: bfloat16 [96, 1280, 768], P(('dp', 'fsdp')), may hold values from -6 to 6
- cotangent: bfloat16 [96, 1280, 768], P(('dp', 'fsdp')), may hold values from -6 to 6
- segment_ids: int32 [96, 1280], P(('dp', 'fsdp')), may hold values from 0 to 3, never falling along the last dimension, each value on 1 to 640 neighbouring positions
- routed: int32 [96, 160], P(('dp', 'fsdp')), may hold values from 0 to 1279, as said below
- qkv_weight: float32 [3, 768, 768], P(None, ('dp', 'fsdp')), may hold values from -0.21875 to 0.21875
- qkv_mean: float32 [3, 768, 768], P(None, ('dp', 'fsdp')), may hold values from -384 to 384
- qkv_square: float32 [3, 768, 768], P(None, ('dp', 'fsdp')), may hold values from 3840 to 15360
- qkv_average: float32 [3, 768, 768], P(None, ('dp', 'fsdp')), may hold values from -0.21875 to 0.21875
- out_weight: float32 [768, 768], P(('dp', 'fsdp')), may hold values from -0.625 to 0.625
- out_mean: float32 [768, 768], P(('dp', 'fsdp')), may hold values from -320 to 320
- out_square: float32 [768, 768], P(('dp', 'fsdp')), may hold values from 2457.6 to 9830.4
- out_average: float32 [768, 768], P(('dp', 'fsdp')), may hold values from -0.625 to 0.625
- up_weight: float32 [768, 3072], P(('dp', 'fsdp')), may hold values from -0.21875 to 0.21875
- up_mean: float32 [768, 3072], P(('dp', 'fsdp')), may hold values from -224 to 224
- up_square: float32 [768, 3072], P(('dp', 'fsdp')), may hold values from 1382.4 to 5529.6
- up_average: float32 [768, 3072], P(('dp', 'fsdp')), may hold values from -0.21875 to 0.21875
- down_weight: float32 [3072, 768], P(('dp', 'fsdp')), may hold values from -0.109375 to 0.109375
- down_mean: float32 [3072, 768], P(('dp', 'fsdp')), may hold values from -512 to 512
- down_square: float32 [3072, 768], P(('dp', 'fsdp')), may hold values from 6451.2 to 26112
- down_average: float32 [3072, 768], P(('dp', 'fsdp')), may hold values from -0.109375 to 0.109375
- router_weight: float32 [768], P(('dp', 'fsdp')), may hold values from -0.21875 to 0.21875
- router_mean: float32 [768], P(('dp', 'fsdp')), may hold values from -12288 to 12288
- router_square: float32 [768], P(('dp', 'fsdp')), may hold values from 3932160 to 15728640
- router_average: float32 [768], P(('dp', 'fsdp')), may hold values from -0.21875 to 0.21875
- norm_gains: float32 [2, 768], P(None, ('dp', 'fsdp')), may hold values from 0.5 to 1.5
- gains_mean: float32 [2, 768], P(None, ('dp', 'fsdp')), may hold values from -768 to 768
- gains_square: float32 [2, 768], P(None, ('dp', 'fsdp')), may hold values from 15360 to 61440
- gains_average: float32 [2, 768], P(None, ('dp', 'fsdp')), may hold values from 0.5 to 1.5
Outputs:
- block_out: bfloat16 [96, 1280, 768], P(('dp', 'fsdp'))
- tokens_grad: bfloat16 [96, 1280, 768], P(('dp', 'fsdp'))
- qkv_next: float32 [3, 768, 768], P(None, ('dp', 'fsdp'))
- qkv_mean_next: float32 [3, 768, 768], P(None, ('dp', 'fsdp'))
- qkv_square_next: float32 [3, 768, 768], P(None, ('dp', 'fsdp'))
- qkv_average_next: float32 [3, 768, 768], P(None, ('dp', 'fsdp'))
- out_next: float32 [768, 768], P(('dp', 'fsdp'))
- out_mean_next: float32 [768, 768], P(('dp', 'fsdp'))
- out_square_next: float32 [768, 768], P(('dp', 'fsdp'))
- out_average_next: float32 [768, 768], P(('dp', 'fsdp'))
- up_next: float32 [768, 3072], P(('dp', 'fsdp'))
- up_mean_next: float32 [768, 3072], P(('dp', 'fsdp'))
- up_square_next: float32 [768, 3072], P(('dp', 'fsdp'))
- up_average_next: float32 [768, 3072], P(('dp', 'fsdp'))
- down_next: float32 [3072, 768], P(('dp', 'fsdp'))
- down_mean_next: float32 [3072, 768], P(('dp', 'fsdp'))
- down_square_next: float32 [3072, 768], P(('dp', 'fsdp'))
- down_average_next: float32 [3072, 768], P(('dp', 'fsdp'))
- router_next: float32 [768], P(('dp', 'fsdp'))
- router_mean_next: float32 [768], P(('dp', 'fsdp'))
- router_square_next: float32 [768], P(('dp', 'fsdp'))
- router_average_next: float32 [768], P(('dp', 'fsdp'))
- gains_next: float32 [2, 768], P(None, ('dp', 'fsdp'))
- gains_mean_next: float32 [2, 768], P(None, ('dp', 'fsdp'))
- gains_square_next: float32 [2, 768], P(None, ('dp', 'fsdp'))
- gains_average_next: float32 [2, 768], P(None, ('dp', 'fsdp'))
Inputs may be any that keep to these rules, and one draw needn't show every extreme that they name: `routed`: each row holds 160 different positions of its sequence in ascending order.
All inputs are finite; a program needn't handle non-finite values.
Results may differ from a plain program's by a relative error of at most 0.012.
The roundings to bfloat16 on the way count: a program that leaves them out, or rounds other values in their place, can miss the bound.
Values may be sent and summed in bfloat16 or wider, within the bound.
No kernel may reach another device: no remote copies, remote signals or barrier semaphores. Data moves between devices by JAX's collectives and lax.ppermute only.
A program may use at most 192 MiB of HBM per device.

v0:
```python
import jax
import jax.numpy as jnp
from jax import lax
from jax.sharding import PartitionSpec as P

HEADS = 12


norm_eps = 1e-06
learn_rates = (0.03, 0.1, 0.03, 0.02, 0.03, 0.2)
beta_first = 0.5
beta_second = 0.5
adam_eps = 1e-08
decay_rate = 0.1
average_rate = 0.7
exact_mode = lax.Precision.HIGHEST


def norm_scale(values, gain):
    return values * lax.rsqrt(jnp.mean(values * values, axis=-1, keepdims=True) + norm_eps) * gain


def gelu_tanh(values):
    return jax.nn.gelu(values, approximate=True)


def gather_weights(pieces):
    return (
        lax.all_gather(pieces[0], ("dp", "fsdp"), axis=1, tiled=True),
        lax.all_gather(pieces[1], ("dp", "fsdp"), axis=0, tiled=True),
        lax.all_gather(pieces[2], ("dp", "fsdp"), axis=0, tiled=True),
        lax.all_gather(pieces[3], ("dp", "fsdp"), axis=0, tiled=True),
        lax.all_gather(pieces[4], ("dp", "fsdp"), axis=0, tiled=True),
        lax.all_gather(pieces[5], ("dp", "fsdp"), axis=1, tiled=True),
    )


def reduce_grads(terms):
    return (
        lax.psum_scatter(terms[0], ("dp", "fsdp"), scatter_dimension=1, tiled=True),
        lax.psum_scatter(terms[1], ("dp", "fsdp"), scatter_dimension=0, tiled=True),
        lax.psum_scatter(terms[2], ("dp", "fsdp"), scatter_dimension=0, tiled=True),
        lax.psum_scatter(terms[3], ("dp", "fsdp"), scatter_dimension=0, tiled=True),
        lax.psum_scatter(terms[4], ("dp", "fsdp"), scatter_dimension=0, tiled=True),
        lax.psum_scatter(terms[5], ("dp", "fsdp"), scatter_dimension=1, tiled=True),
    )


def block_mask(row_segs, row_pos, capacity):
    number = row_segs.shape[0]
    owner = jnp.arange(number, dtype=jnp.int32) // capacity
    same_seq = owner[:, None] == owner[None, :]
    same_doc = row_segs[:, None] == row_segs[None, :]
    return same_seq & same_doc & (row_pos[None, :] <= row_pos[:, None])


def adamw(weight, mean, square, grad, decay, rate):
    mean_next = beta_first * mean + (1.0 - beta_first) * grad
    square_next = beta_second * square + (1.0 - beta_second) * grad * grad
    update = mean_next / (jnp.sqrt(square_next) + adam_eps)
    weight_next = weight - rate * (update + decay * weight)
    return (weight_next, mean_next, square_next)


def body(
    tokens,
    cotangent,
    segment_ids,
    routed,
    qkv_weight,
    qkv_mean,
    qkv_square,
    qkv_average,
    out_weight,
    out_mean,
    out_square,
    out_average,
    up_weight,
    up_mean,
    up_square,
    up_average,
    down_weight,
    down_mean,
    down_square,
    down_average,
    router_weight,
    router_mean,
    router_square,
    router_average,
    norm_gains,
    gains_mean,
    gains_square,
    gains_average,
):
    seqs_here, length, model_width = tokens.shape
    capacity = routed.shape[1]
    row_count = seqs_here * capacity
    head_count = HEADS
    head_size = model_width // head_count
    scale_factor = head_size ** (-0.5)
    per_block = max(
        [
            number
            for number in range(1, seqs_here + 1)
            if seqs_here % number == 0 and number * capacity <= max(768, capacity)
        ]
    )
    block_count = seqs_here // per_block
    block_rows = per_block * capacity
    seq_index = jnp.arange(seqs_here, dtype=jnp.int32)[:, None]
    picked = tokens[seq_index, routed].reshape(row_count, model_width)
    row_segs = segment_ids[seq_index, routed].reshape(block_count, block_rows)
    row_pos = routed.reshape(block_count, block_rows)
    masters = (qkv_weight, out_weight, up_weight, down_weight, router_weight, norm_gains)
    sent = tuple((weight.astype(jnp.bfloat16) for weight in masters))
    gathered = gather_weights((sent[0], sent[1], sent[2], sent[3], sent[4], sent[5]))
    qkv_low, wout_low, wup_low, wdown_low, router_low, gains_low = gathered
    picked_f = picked.astype(jnp.float32)
    score = jnp.dot(picked, router_low, preferred_element_type=jnp.float32)
    gain_one = gains_low[0].astype(jnp.float32)
    gain_two = gains_low[1].astype(jnp.float32)
    normed_one, pull_one = jax.vjp(norm_scale, picked_f, gain_one)
    hidden_one = normed_one.astype(jnp.bfloat16)
    projected = jnp.einsum(
        "rd,cde->cre", hidden_one, qkv_low, preferred_element_type=jnp.float32
    ).astype(jnp.bfloat16)
    head_view = projected.reshape(3, block_count, block_rows, head_count, head_size)

    def attend(item):
        queries, key_heads, value_heads, segs, places = item
        logits = (
            jnp.einsum("qhd,khd->hqk", queries, key_heads, preferred_element_type=jnp.float32)
            * scale_factor
        )
        allowed = block_mask(segs, places, capacity)
        logits = jnp.where(allowed[None], logits, -1e30)
        row_max = jnp.max(logits, axis=-1, keepdims=True)
        exponent = jnp.exp(logits - row_max)
        row_total = jnp.sum(exponent, axis=-1, keepdims=True)
        probs = (exponent / row_total).astype(jnp.bfloat16)
        mixed_block = jnp.einsum(
            "hqk,khd->qhd", probs, value_heads, preferred_element_type=jnp.float32
        ).astype(jnp.bfloat16)
        return (mixed_block, row_max[..., 0] + jnp.log(row_total[..., 0]))

    mixed, log_totals = lax.map(
        attend, (head_view[0], head_view[1], head_view[2], row_segs, row_pos)
    )
    mixed = mixed.reshape(row_count, model_width)
    attended = jnp.dot(mixed, wout_low, preferred_element_type=jnp.float32)
    first = picked_f + score[:, None] * attended
    normed_two, pull_two = jax.vjp(norm_scale, first, gain_two)
    hidden_two = normed_two.astype(jnp.bfloat16)
    inner_pre = jnp.dot(hidden_two, wup_low, preferred_element_type=jnp.float32)
    activ, pull_gelu = jax.vjp(gelu_tanh, inner_pre)
    activ_low = activ.astype(jnp.bfloat16)
    down_out = jnp.dot(activ_low, wdown_low, preferred_element_type=jnp.float32)
    second = first + score[:, None] * down_out
    block_out = tokens.at[seq_index, routed].set(
        second.astype(jnp.bfloat16).reshape(seqs_here, capacity, model_width)
    )
    regathered = gather_weights((sent[0], sent[1], sent[2], sent[3], sent[4], sent[5]))
    qkv_low, wout_low, wup_low, wdown_low, router_low, gains_low = regathered
    back_cot = cotangent[seq_index, routed].reshape(row_count, model_width).astype(jnp.float32)
    grad_down_out = (score[:, None] * back_cot).astype(jnp.bfloat16)
    grad_score = jnp.sum(back_cot * down_out, axis=-1)
    grad_activ = jnp.einsum(
        "re,fe->rf", grad_down_out, wdown_low, preferred_element_type=jnp.float32
    )
    grad_pre = pull_gelu(grad_activ)[0].astype(jnp.bfloat16)
    grad_wdown = jnp.einsum(
        "rf,re->fe", activ_low, grad_down_out, preferred_element_type=jnp.float32
    )
    grad_wup = jnp.einsum("rd,rf->df", hidden_two, grad_pre, preferred_element_type=jnp.float32)
    grad_hidden_two = jnp.einsum("rf,df->rd", grad_pre, wup_low, preferred_element_type=jnp.float32)
    grad_first_norm, grad_gain_two = pull_two(grad_hidden_two)
    grad_first = back_cot + grad_first_norm
    grad_attended = (score[:, None] * grad_first).astype(jnp.bfloat16)
    grad_score = grad_score + jnp.sum(grad_first * attended, axis=-1)
    grad_mixed = jnp.einsum(
        "re,de->rd", grad_attended, wout_low, preferred_element_type=jnp.float32
    ).astype(jnp.bfloat16)
    grad_wout = jnp.einsum("rd,re->de", mixed, grad_attended, preferred_element_type=jnp.float32)

    def attend_back(item):
        queries, key_heads, value_heads, segs, places, log_block, grad_block = item
        logits = (
            jnp.einsum("qhd,khd->hqk", queries, key_heads, preferred_element_type=jnp.float32)
            * scale_factor
        )
        allowed = block_mask(segs, places, capacity)
        logits = jnp.where(allowed[None], logits, -1e30)
        probs = jnp.exp(logits - log_block[..., None])
        grad_probs = jnp.einsum(
            "qhd,khd->hqk", grad_block, value_heads, preferred_element_type=jnp.float32
        )
        inner_sum = jnp.sum(probs * grad_probs, axis=-1, keepdims=True)
        grad_logits = (probs * (grad_probs - inner_sum)).astype(jnp.bfloat16)
        grad_query = (
            jnp.einsum("hqk,khd->qhd", grad_logits, key_heads, preferred_element_type=jnp.float32)
            * scale_factor
        ).astype(jnp.bfloat16)
        grad_key = (
            jnp.einsum("hqk,qhd->khd", grad_logits, queries, preferred_element_type=jnp.float32)
            * scale_factor
        ).astype(jnp.bfloat16)
        grad_value = jnp.einsum(
            "hqk,qhd->khd",
            probs.astype(jnp.bfloat16),
            grad_block,
            preferred_element_type=jnp.float32,
        ).astype(jnp.bfloat16)
        return (grad_query, grad_key, grad_value)

    grad_mixed_view = grad_mixed.reshape(block_count, block_rows, head_count, head_size)
    grad_query, grad_key, grad_value = lax.map(
        attend_back,
        (head_view[0], head_view[1], head_view[2], row_segs, row_pos, log_totals, grad_mixed_view),
    )
    grad_projected = jnp.stack([grad_query, grad_key, grad_value]).reshape(
        3, row_count, model_width
    )
    grad_wqkv = jnp.einsum(
        "rd,cre->cde", hidden_one, grad_projected, preferred_element_type=jnp.float32
    )
    grad_hidden_one = jnp.einsum(
        "cre,cde->rd", grad_projected, qkv_low, preferred_element_type=jnp.float32
    )
    grad_picked_norm, grad_gain_one = pull_one(grad_hidden_one)
    router_f = router_low.astype(jnp.float32)
    grad_rows = grad_first + grad_picked_norm + grad_score[:, None] * router_f[None, :]
    grad_router = jnp.dot(grad_score, picked_f, precision=exact_mode)
    tokens_grad = cotangent.at[seq_index, routed].set(
        grad_rows.astype(jnp.bfloat16).reshape(seqs_here, capacity, model_width)
    )
    grad_gains = jnp.stack([grad_gain_one, grad_gain_two])
    grads = reduce_grads((grad_wqkv, grad_wout, grad_wup, grad_wdown, grad_router, grad_gains))
    states = (
        (qkv_weight, qkv_mean, qkv_square, qkv_average),
        (out_weight, out_mean, out_square, out_average),
        (up_weight, up_mean, up_square, up_average),
        (down_weight, down_mean, down_square, down_average),
        (router_weight, router_mean, router_square, router_average),
        (norm_gains, gains_mean, gains_square, gains_average),
    )
    decays = (decay_rate, decay_rate, decay_rate, decay_rate, 0.0, 0.0)
    results = [block_out, tokens_grad]
    for number in range(6):
        weight, mean, square, average = states[number]
        weight_next, mean_next, square_next = adamw(
            weight, mean, square, grads[number], decays[number], learn_rates[number]
        )
        average_next = average_rate * average + (1.0 - average_rate) * weight_next
        results = results + [weight_next, mean_next, square_next, average_next]
    return tuple(results)


def solution(mesh):
    in_specs = (
        P(("dp", "fsdp"), None, None),
        P(("dp", "fsdp"), None, None),
        P(("dp", "fsdp"), None),
        P(("dp", "fsdp"), None),
        P(None, ("dp", "fsdp"), None),
        P(None, ("dp", "fsdp"), None),
        P(None, ("dp", "fsdp"), None),
        P(None, ("dp", "fsdp"), None),
        P(("dp", "fsdp"), None),
        P(("dp", "fsdp"), None),
        P(("dp", "fsdp"), None),
        P(("dp", "fsdp"), None),
        P(("dp", "fsdp"), None),
        P(("dp", "fsdp"), None),
        P(("dp", "fsdp"), None),
        P(("dp", "fsdp"), None),
        P(("dp", "fsdp"), None),
        P(("dp", "fsdp"), None),
        P(("dp", "fsdp"), None),
        P(("dp", "fsdp"), None),
        P(("dp", "fsdp")),
        P(("dp", "fsdp")),
        P(("dp", "fsdp")),
        P(("dp", "fsdp")),
        P(None, ("dp", "fsdp")),
        P(None, ("dp", "fsdp")),
        P(None, ("dp", "fsdp")),
        P(None, ("dp", "fsdp")),
    )
    out_specs = (
        P(("dp", "fsdp"), None, None),
        P(("dp", "fsdp"), None, None),
        P(None, ("dp", "fsdp"), None),
        P(None, ("dp", "fsdp"), None),
        P(None, ("dp", "fsdp"), None),
        P(None, ("dp", "fsdp"), None),
        P(("dp", "fsdp"), None),
        P(("dp", "fsdp"), None),
        P(("dp", "fsdp"), None),
        P(("dp", "fsdp"), None),
        P(("dp", "fsdp"), None),
        P(("dp", "fsdp"), None),
        P(("dp", "fsdp"), None),
        P(("dp", "fsdp"), None),
        P(("dp", "fsdp"), None),
        P(("dp", "fsdp"), None),
        P(("dp", "fsdp"), None),
        P(("dp", "fsdp"), None),
        P(("dp", "fsdp")),
        P(("dp", "fsdp")),
        P(("dp", "fsdp")),
        P(("dp", "fsdp")),
        P(None, ("dp", "fsdp")),
        P(None, ("dp", "fsdp")),
        P(None, ("dp", "fsdp")),
        P(None, ("dp", "fsdp")),
    )
    return jax.shard_map(body, mesh=mesh, in_specs=in_specs, out_specs=out_specs, check_vma=False)
```

profile of v0, /device:TPU:0, one launch (start us, length us, event | category | flops | bytes accessed | tf_op | source)
XLA Modules:
  0.0 905.1 jit_solution(17557903869245385194)
XLA Ops:
  7.3 5.8 copy.152
  13.1 2.6 copy.153
  18.3 42.1 %all-reduce = bf16[768]{0:T(1024)(128)(2,1)S(1)} all-reduce(bf16[768]{0:T(1024)(128)(2,1)S(1)} %dynamic-update-slice), channel_id=1, replica_groups=mesh['dp'=4,'fsdp'=8] {'dp','fsdp'}, use_global_device_ids=true, to_apply=%add | all-reduce | flops 768 | bytes 3072
  60.5 65.5 %all-gather = bf16[32,24,2]{1,2,0:T(2,128)(2,1)S(1)} all-gather(bf16[1,24,2]{1,2,0:T(2,128)(2,1)S(1)} %convert_bitcast_fusion.1), channel_id=1, replica_groups=mesh['dp'=4,'fsdp'=8] {'dp','fsdp'}, dimensions={0}, use_global_device_ids=true | all-gather | bytes 3168 | tf_op jit(solution)/shard_map/all_gather | solution.py:34
  126.1 4.8 gather_fusion.1
  131.0 9.8 %gather_fusion = bf16[480,768]{1,0:T(8,128)(2,1)S(1)} fusion(bf16[3,1280,768]{2,1,0:T(8,128)(2,1)} %copy.152, s32[480]{0:T(512)S(1)} %reshape.292), kind=kCustom, calls=%fused_computation | custom fusion | bytes 1478400 | tf_op jit(solution)/shard_map/gather | solution.py:111
  140.8 12.4 %gather_fusion.2 = bf16[480,768]{1,0:T(8,128)(2,1)} fusion(bf16[3,1280,768]{2,1,0:T(8,128)(2,1)} %copy.153, s32[480]{0:T(512)S(1)} %reshape.292), kind=kCustom, calls=%fused_computation.2 | custom fusion | bytes 1478400 | tf_op jit(solution)/shard_map/gather | solution.py:164
  154.1 4.0 convert_bitcast_fusion
  159.7 1.4 copy.122
  161.1 2.2 fusion.13
  163.2 2.5 fusion
  165.7 1.8 copy-done.2
  167.6 4.4 fusion.25
  172.0 3.9 multiply_reduce_fusion.4
  175.9 26.3 %all-gather.10.cloned.1.call-done = bf16[768,3072]{1,0:T(8,128)(2,1)} async-done(((bf16[24,3072]{1,0:T(8,128)(2,1)}), bf16[768,3072]{1,0:T(8,128)(2,1)}) %all-gather.10.cloned.1.call-update) | async-done | bytes 4718608 | tf_op jit(solution)/shard_map/all_gather | solution.py:31
  202.3 5.4 fusion.65
  207.7 2.5 copy-done.42
  210.2 5.6 fusion.33
  215.9 134.4 %reduce-scatter.9.cloned.1.call-done = f32[96,768]{1,0:T(8,128)} async-done(((f32[3072,768]{1,0:T(8,128)}), f32[96,768]{1,0:T(8,128)}) %reduce-scatter.9.cloned.1.call-update) | async-done | bytes 294928 | tf_op jit(solution)/shard_map/reduce_scatter | solution.py:43
  350.3 2.6 multiply_add_fusion.3
  353.0 63.9 %all-gather.12.cloned.1.call-done = bf16[3072,768]{1,0:T(8,128)(2,1)} async-done(((bf16[96,768]{1,0:T(8,128)(2,1)}), bf16[3072,768]{1,0:T(8,128)(2,1)}) %all-gather.12.cloned.1.call-update) | async-done | bytes 4718608 | tf_op jit(solution)/shard_map/all_gather | solution.py:32
  416.9 8.7 fusion.8
  425.7 6.1 multiply_reduce_fusion.1
  431.9 7.6 fusion.21
  440.7 2.4 fusion.63
  443.1 3.4 convolution_convert_fusion
  446.5 2.3 copy.126
  448.7 8.4 fusion.26
  457.1 2.3 copy.132
  459.5 7.8 multiply_reduce_fusion
  467.3 7.0 multiply_convert_fusion
  474.4 2.5 copy-done.3
  478.0 1.1 copy.130
  479.1 4.7 multiply_convert_fusion.2
  484.1 6.4 convolution_bitcast_fusion
  490.5 11.1 %copy.133 = f32[3,768,768]{2,0,1:T(4,128)} copy(f32[3,768,768]{1,2,0:T(8,128)} %convolution_bitcast_fusion) | data formatting | bytes 14155776 | tf_op jit(solution)/shard_map/rd,cre->cde/transpose | solution.py:223
  501.7 1.3 copy-done.5
  503.0 7.3 fusion.64
  511.6 5.4 fusion.17
  517.1 65.6 %scatter_fusion = bf16[3,1280,768]{2,1,0:T(8,128)(2,1)} fusion(bf16[3,1280,768]{2,1,0:T(8,128)(2,1)} %copy.152, s32[480]{0:T(512)S(1)} %reshape.310, bf16[480,768]{1,0:T(8,128)(2,1)S(1)} %copy-done.16), kind=kCustom, calls=%fused_computation.3 | custom fusion | bytes 2215680 | tf_op jit(solution)/shard_map/scatter | solution.py:159
  582.7 1.9 fusion.20
  584.8 65.9 %scatter_fusion.1 = bf16[3,1280,768]{2,1,0:T(8,128)(2,1)} fusion(bf16[3,1280,768]{2,1,0:T(8,128)(2,1)} %copy.153, s32[480]{0:T(512)S(1)} %reshape.310, bf16[480,768]{1,0:T(8,128)(2,1)S(1)} %fusion.20), kind=kCustom, calls=%fused_computation.4 | custom fusion | bytes 2215680 | tf_op jit(solution)/shard_map/scatter | solution.py:233
  651.1 40.3 %all-reduce.4 = (f32[768]{0:T(1024)S(1)}, f32[2,768]{1,0:T(2,128)S(1)}) all-reduce(f32[768]{0:T(1024)S(1)} %convolution_reduce_fusion, f32[2,768]{1,0:T(2,128)S(1)} %pad_maximum_fusion.3), channel_id=6, replica_groups=mesh['dp'=4,'fsdp'=8] {'dp','fsdp'}, use_global_device_ids=true, to_apply=%region_15.16.clone | all-reduce | flops 2304 | bytes 18432
  692.8 1.6 multiply_add_fusion.7
  694.4 59.1 %all-reduce.7.cloned.1.call-done = f32[3,768,768]{2,0,1:T(4,128)} async-done(((f32[3,768,768]{2,0,1:T(4,128)}), f32[3,768,768]{2,0,1:T(4,128)}) %all-reduce.7.cloned.1.call-update) | async-done | bytes 7077904
  754.6 2.1 multiply_add_fusion.5
  756.6 139.3 %reduce-scatter.7.cloned.1.call-done = f32[24,3072]{1,0:T(8,128)} async-done(((f32[768,3072]{1,0:T(8,128)}), f32[24,3072]{1,0:T(8,128)}) %reduce-scatter.7.cloned.1.call-update) | async-done | bytes 294928 | tf_op jit(solution)/shard_map/reduce_scatter | solution.py:42
  895.9 2.1 multiply_add_fusion.4
  (139 shorter events, 12.2 us)
Async XLA Ops:
  7.2 118.9 %copy-start = (s32[3,1280]{1,0:T(4,128)S(1)}, s32[3,1280]{1,0:T(4,128)}, u32[]{:S(2)}) copy-start(s32[3,1280]{1,0:T(4,128)} %param.30) | copy-start | bytes 46084
  7.2 146.8 %all-gather.6.cloned.1.call-start = ((), (), s32[]{:S(2)}) async-start(), calls=%async_computation.3 | async-start | bytes 3649536 | tf_op jit(solution)/shard_map/all_gather | solution.py:29
  7.3 5.8 copy-start.6
  13.1 2.6 copy-start.14
  13.1 3.4 copy-start.23
  13.1 4.1 copy-start.12
  13.1 4.9 copy-start.36
  13.1 4.9 copy-start.31
  13.1 47.4 %copy-start.32 = (f32[2,24]{1,0:T(2,128)S(1)}, f32[2,24]{1,0:T(2,128)}, u32[]{:S(2)}) copy-start(f32[2,24]{1,0:T(2,128)} %param.52) | copy-start | bytes 580
  16.4 155.6 %all-gather.8.cloned.1.call-start = ((), (), s32[]{:S(2)}) async-start(), calls=%async_computation.4 | async-start | bytes 1216512 | tf_op jit(solution)/shard_map/all_gather | solution.py:30
  17.1 185.2 %all-gather.10.cloned.1.call-start = ((), (), s32[]{:S(2)}) async-start(), calls=%async_computation.5 | async-start | bytes 4866048 | tf_op jit(solution)/shard_map/all_gather | solution.py:31
  17.9 332.4 %reduce-scatter.9.cloned.1.call-start = ((), (), s32[]{:S(2)}) async-start(), calls=%async_computation.9 | async-start | bytes 9732096 | tf_op jit(solution)/shard_map/reduce_scatter | solution.py:43
  163.2 4.4 copy-start.2
  202.3 7.9 copy-start.17
  207.7 2.5 copy-start.42
  215.8 201.1 %all-gather.12.cloned.1.call-start = ((), (), s32[]{:S(2)}) async-start(), calls=%async_computation.6 | async-start | bytes 4866048 | tf_op jit(solution)/shard_map/all_gather | solution.py:32
  352.9 339.9 %reduce-scatter.5.cloned.1.call-start = ((), (), s32[]{:S(2)}) async-start(), calls=%async_computation.7 | async-start | bytes 2433024 | tf_op jit(solution)/shard_map/reduce_scatter | solution.py:41
  416.9 8.7 copy-start.4
  425.7 6.2 copy-start.10
  425.7 6.2 copy-start.11
  425.7 6.2 copy-start.18
  425.7 6.2 copy-start.41
  431.9 8.8 copy-start.9
  459.5 294.0 %all-reduce.7.cloned.1.call-start = ((), (), s32[]{:S(2)}) async-start(), calls=%async_computation.10 | async-start | bytes 18874368
  474.4 2.5 copy-start.3
  479.1 4.9 copy-start.19
  484.1 6.4 copy-start.22
  501.6 1.4 copy-start.5
  501.6 394.3 %reduce-scatter.7.cloned.1.call-start = ((), (), s32[]{:S(2)}) async-start(), calls=%async_computation.8 | async-start | bytes 9732096 | tf_op jit(solution)/shard_map/reduce_scatter | solution.py:42
  511.6 5.5 copy-start.16
  517.1 65.6 %copy-start.8 = (f32[480,768]{1,0:T(8,128)S(1)}, f32[480,768]{1,0:T(8,128)}, u32[]{:S(2)}) copy-start(f32[480,768]{1,0:T(8,128)} %copy-done.7) | copy-start | bytes 4423684
  584.6 106.8 %copy-start.37 = (f32[24]{0:T(128)S(1)}, f32[24]{0:T(128)}, u32[]{:S(2)}) copy-start(f32[24]{0:T(128)} %param.48) | copy-start | bytes 292
  584.7 106.8 %copy-start.38 = (f32[24]{0:T(128)S(1)}, f32[24]{0:T(128)}, u32[]{:S(2)}) copy-start(f32[24]{0:T(128)} %param.51) | copy-start | bytes 292
  584.7 106.8 %copy-start.39 = (f32[24]{0:T(128)S(1)}, f32[24]{0:T(128)}, u32[]{:S(2)}) copy-start(f32[24]{0:T(128)} %param.50) | copy-start | bytes 292
  584.7 106.8 %copy-start.40 = (f32[24]{0:T(128)S(1)}, f32[24]{0:T(128)}, u32[]{:S(2)}) copy-start(f32[24]{0:T(128)} %param.49) | copy-start | bytes 292
  584.7 107.4 %copy-start.33 = (f32[2,24]{1,0:T(2,128)S(1)}, f32[2,24]{1,0:T(2,128)}, u32[]{:S(2)}) copy-start(f32[2,24]{1,0:T(2,128)} %param.55) | copy-start | bytes 580
  584.7 107.4 %copy-start.34 = (f32[2,24]{1,0:T(2,128)S(1)}, f32[2,24]{1,0:T(2,128)}, u32[]{:S(2)}) copy-start(f32[2,24]{1,0:T(2,128)} %param.54) | copy-start | bytes 580
  584.7 107.4 %copy-start.35 = (f32[2,24]{1,0:T(2,128)S(1)}, f32[2,24]{1,0:T(2,128)}, u32[]{:S(2)}) copy-start(f32[2,24]{1,0:T(2,128)} %param.53) | copy-start | bytes 580
  584.7 108.1 %copy-start.28 = (f32[24,768]{1,0:T(8,128)S(1)}, f32[24,768]{1,0:T(8,128)}, u32[]{:S(2)}) copy-start(f32[24,768]{1,0:T(8,128)} %param.39) | copy-start | bytes 221188
  584.7 108.1 %copy-start.29 = (f32[24,768]{1,0:T(8,128)S(1)}, f32[24,768]{1,0:T(8,128)}, u32[]{:S(2)}) copy-start(f32[24,768]{1,0:T(8,128)} %param.38) | copy-start | bytes 221188
  584.8 108.1 %copy-start.30 = (f32[24,768]{1,0:T(8,128)S(1)}, f32[24,768]{1,0:T(8,128)}, u32[]{:S(2)}) copy-start(f32[24,768]{1,0:T(8,128)} %param.37) | copy-start | bytes 221188
  584.8 169.8 %copy-start.15 = (f32[3,24,768]{2,1,0:T(8,128)S(1)}, f32[3,24,768]{2,1,0:T(8,128)}, u32[]{:S(2)}) copy-start(f32[3,24,768]{2,1,0:T(8,128)} %param.32) | copy-start | bytes 663556
  584.8 169.8 %copy-start.27 = (f32[3,24,768]{2,1,0:T(8,128)S(1)}, f32[3,24,768]{2,1,0:T(8,128)}, u32[]{:S(2)}) copy-start(f32[3,24,768]{2,1,0:T(8,128)} %param.35) | copy-start | bytes 663556
  584.8 311.1 %copy-start.13 = (f32[24,3072]{1,0:T(8,128)S(1)}, f32[24,3072]{1,0:T(8,128)}, u32[]{:S(2)}) copy-start(f32[24,3072]{1,0:T(8,128)} %param.40) | copy-start | bytes 884740
  584.8 311.1 %copy-start.24 = (f32[24,3072]{1,0:T(8,128)S(1)}, f32[24,3072]{1,0:T(8,128)}, u32[]{:S(2)}) copy-start(f32[24,3072]{1,0:T(8,128)} %param.43) | copy-start | bytes 884740
  584.8 311.1 %copy-start.25 = (f32[24,3072]{1,0:T(8,128)S(1)}, f32[24,3072]{1,0:T(8,128)}, u32[]{:S(2)}) copy-start(f32[24,3072]{1,0:T(8,128)} %param.42) | copy-start | bytes 884740
  584.8 311.1 %copy-start.26 = (f32[24,3072]{1,0:T(8,128)S(1)}, f32[24,3072]{1,0:T(8,128)}, u32[]{:S(2)}) copy-start(f32[24,3072]{1,0:T(8,128)} %param.41) | copy-start | bytes 884740
  584.8 313.2 %copy-start.1 = (s32[3,1280]{1,0:T(4,128)S(1)}, s32[3,1280]{1,0:T(4,128)}, u32[]{:S(2)}) copy-start(s32[3,1280]{1,0:T(4,128)} %param.30) | copy-start | bytes 46084
  (3 other events, 3.6 us)
Sparse Core Ops, SparseCore 0:
  16.5 62.9 all-gather.5
  83.1 52.9 all-gather.7
  139.6 62.6 all-gather.9
  216.0 134.2 reduce-scatter.8
  354.1 62.7 all-gather.11
  459.6 97.8 reduce-scatter.4
  563.2 190.2 all-reduce.6
  760.4 135.4 reduce-scatter.6
where the time goes:
time: 920 us; the launch traced here: 905 us
  waiting for transfers between devices  423 us (46%)
  local copies, waits for them, and re-layouts  199 us (22%)
  blocking collectives  148 us (16%)
  matrix products  95.6 us (10%)
  other arithmetic  23.8 us (3%)
  between operations  15 us (2%)
    reduce_scatter x1, waiting for transfers between devices, reduce_grads(): lax.psum_scatter(terms[2], ('dp', 'fsdp'), scatter_dimension=0, tiled=True)  139 us
    reduce_scatter x1, waiting for transfers between devices, reduce_grads(): lax.psum_scatter(terms[3], ('dp', 'fsdp'), scatter_dimension=0, tiled=True)  134 us
    unnamed x2, blocking collectives  82.4 us
    scatter x1, local copies, waits for them, and re-layouts, body(): cotangent.at[seq_index, routed]  65.9 us
    scatter x1, local copies, waits for them, and re-layouts, body(): tokens.at[seq_index, routed]  65.6 us
    all_gather x1, blocking collectives, gather_weights(): lax.all_gather(pieces[5], ('dp', 'fsdp'), axis=1, tiled=True)  65.5 us
    all_gather x1, waiting for transfers between devices, gather_weights(): lax.all_gather(pieces[3], ('dp', 'fsdp'), axis=0, tiled=True)  63.9 us
    unnamed x9, waiting for transfers between devices  59.3 us
  transfers between devices with their start and end apart: 8, of which 5 were waited for; matrix products, arithmetic and copies ran while one was open for 27% of the time, Pallas kernels for 0%

commit v1 on v0

v1 whole, which is shorter than its diff:
```python
import functools

import jax
import jax.numpy as jnp
from jax import lax
from jax.experimental import pallas as pl
from jax.experimental.pallas import tpu as pltpu
from jax.sharding import Mesh, PartitionSpec as P

HEADS = 12
SMALL = 256

norm_eps = 1e-06
learn_rates = (0.03, 0.1, 0.03, 0.02, 0.03, 0.2)
beta_first = 0.5
beta_second = 0.5
adam_eps = 1e-08
decay_rate = 0.1
average_rate = 0.7
exact_mode = lax.Precision.HIGHEST
f32 = jnp.float32
bf16 = jnp.bfloat16


def shifted(value, axis, sizes, step):
    n = sizes[axis]
    return lax.ppermute(value, axis, [(i, (i + step) % n) for i in range(n)])


def gather_axis(value, axis, sizes):
    return [value] + [shifted(value, axis, sizes, k) for k in range(1, sizes[axis])]


def gather_piece(block, sizes):
    along = gather_axis(block, "a", sizes)
    half = len(along) // 2
    first, second = jnp.stack(along[:half]), jnp.stack(along[half:])
    first = gather_axis(jnp.stack(gather_axis(first, "b", sizes)), "y", sizes)
    second = gather_axis(jnp.stack(gather_axis(second, "y", sizes)), "b", sizes)
    here = first + second
    return here, [shifted(v, "c", sizes, 1) for v in here]


def sum_axis(pieces, axis, sizes):
    total = pieces[0]
    for k in range(1, sizes[axis]):
        total = total + shifted(pieces[k].astype(bf16), axis, sizes, -k).astype(f32)
    return total


def scatter_piece(own, other, sizes):
    came = [shifted(v, "c", sizes, 1) for v in other]
    first = own[0].astype(f32) + came[0].astype(f32)
    second = own[1].astype(f32) + came[1].astype(f32)
    first = sum_axis([first[k] for k in range(sizes["b"])], "b", sizes)
    second = sum_axis([second[k] for k in range(sizes["y"])], "y", sizes)
    first = sum_axis([first[k] for k in range(sizes["y"])], "y", sizes)
    second = sum_axis([second[k] for k in range(sizes["b"])], "b", sizes)
    half = sizes["a"] // 2
    return sum_axis([first[k] for k in range(half)] + [second[k] for k in range(half)], "a", sizes)


def places(sizes):
    half = sizes["a"] // 2
    out = []
    for kc in range(2):
        for ky in range(sizes["y"]):
            for kb in range(sizes["b"]):
                for ka in range(sizes["a"]):
                    part = 0 if ka < half else 1
                    out.append((kc, part, ky, kb, ka % half, (ky, kc, ka, kb)))
    return out


def owner(pos_ref, steps, sizes):
    ky, kc, ka, kb = steps
    y = lax.rem(pos_ref[0] + (sizes["y"] - ky), sizes["y"])
    c = lax.rem(pos_ref[1] + (2 - kc), 2)
    a = lax.rem(pos_ref[2] + (sizes["a"] - ka), sizes["a"])
    b = lax.rem(pos_ref[3] + (sizes["b"] - kb), sizes["b"])
    return ((y * 2 + c) * sizes["a"] + a) * sizes["b"] + b


def assemble(here, there, pos, sizes, cuts):
    ny, nb = sizes["y"], sizes["b"]
    rows = here[0].shape[-2]
    devices = 2 * ny * nb * sizes["a"]
    sources = here + there
    blocks = places(sizes)

    def kernel(pos_ref, *refs):
        ins, outs, sems = refs[: len(sources)], refs[len(sources) : -1], refs[-1]
        copies = []
        for kc, part, ky, kb, ka, steps in blocks:
            base = kc * (ny + nb)
            ref = ins[base + ky].at[kb, ka] if part == 0 else ins[base + ny + kb].at[ky, ka]
            where = owner(pos_ref, steps, sizes)
            for (start, width), out in zip(cuts, outs):
                copies.append((ref.at[:, pl.ds(start, width)], out.at[where]))
        started = []
        for i, (src, dst) in enumerate(copies):
            copy = pltpu.make_async_copy(src, dst, sems.at[i])
            copy.start()
            started.append(copy)
        for copy in started:
            copy.wait()

    return pl.pallas_call(
        kernel,
        out_shape=[jax.ShapeDtypeStruct((devices, rows, width), bf16) for _, width in cuts],
        in_specs=[pl.BlockSpec(memory_space=pltpu.SMEM)] + [pl.BlockSpec(memory_space=pl.ANY)] * len(sources),
        out_specs=[pl.BlockSpec(memory_space=pl.ANY)] * len(cuts),
        scratch_shapes=[pltpu.SemaphoreType.DMA((len(blocks) * len(cuts),))],
        cost_estimate=pl.CostEstimate(flops=0, transcendentals=0, bytes_accessed=2 * devices * rows * sum(w for _, w in cuts) * 2),
        name="assemble",
    )(pos, *sources)


def disassemble(parts, pos, sizes):
    ny, nb, half = sizes["y"], sizes["b"], sizes["a"] // 2
    rows = parts[0].shape[1]
    widths = [p.shape[2] for p in parts]
    total = sum(widths)
    blocks = places(sizes)

    def kernel(pos_ref, *refs):
        ins, outs, sems = refs[: len(parts)], refs[len(parts) : -1], refs[-1]
        started = []
        for kc, part, ky, kb, ka, steps in blocks:
            ref = outs[kc * 2 + part]
            ref = ref.at[kb, ky, ka] if part == 0 else ref.at[ky, kb, ka]
            where = owner(pos_ref, steps, sizes)
            start = 0
            for width, src in zip(widths, ins):
                copy = pltpu.make_async_copy(src.at[where], ref.at[:, pl.ds(start, width)], sems.at[len(started)])
                copy.start()
                started.append(copy)
                start += width
        for copy in started:
            copy.wait()

    first = jax.ShapeDtypeStruct((nb, ny, half, rows, total), bf16)
    second = jax.ShapeDtypeStruct((ny, nb, half, rows, total), bf16)
    outs = pl.pallas_call(
        kernel,
        out_shape=[first, second, first, second],
        in_specs=[pl.BlockSpec(memory_space=pltpu.SMEM)] + [pl.BlockSpec(memory_space=pl.ANY)] * len(parts),
        out_specs=[pl.BlockSpec(memory_space=pl.ANY)] * 4,
        scratch_shapes=[pltpu.SemaphoreType.DMA((len(blocks) * len(parts),))],
        cost_estimate=pl.CostEstimate(flops=0, transcendentals=0, bytes_accessed=4 * 2 * ny * nb * 2 * half * rows * total),
        name="disassemble",
    )(pos, *parts)
    return outs[:2], outs[2:]


def norm_scale(values, gain):
    return values * lax.rsqrt(jnp.mean(values * values, axis=-1, keepdims=True) + norm_eps) * gain


def gelu_tanh(values):
    return jax.nn.gelu(values, approximate=True)


def adamw(state, grad, decay, rate):
    weight, mean, square, average = state
    mean_next = beta_first * mean + (1.0 - beta_first) * grad
    square_next = beta_second * square + (1.0 - beta_second) * grad * grad
    update = mean_next / (jnp.sqrt(square_next) + adam_eps)
    weight_next = weight - rate * (update + decay * weight)
    average_next = average_rate * average + (1.0 - average_rate) * weight_next
    return [weight_next, mean_next, square_next, average_next]


def dot(a, b, spec):
    return jnp.einsum(spec, a, b, preferred_element_type=f32)


def body(sizes, *args):
    tokens, cotangent, segment_ids, routed = args[:4]
    states = [args[4 + 4 * i : 8 + 4 * i] for i in range(6)]
    qkv_state, out_state, up_state, down_state, router_state, gains_state = states
    seqs, length, width = tokens.shape
    capacity = routed.shape[1]
    count = seqs * capacity
    rows = out_state[0].shape[0]
    hidden = up_state[0].shape[1]
    fold = down_state[0].shape[0] // rows
    head_size = width // HEADS
    scale = head_size ** (-0.5)
    pos = jnp.stack([lax.axis_index(n) for n in ("y", "c", "a", "b")]).astype(jnp.int32)

    low = lambda v: v.astype(bf16)
    small = jnp.concatenate([router_state[0][:, None], gains_state[0].T, jnp.zeros((rows, SMALL - 3), f32)], axis=1)
    send_qkv = low(jnp.concatenate([qkv_state[0][0], qkv_state[0][1], qkv_state[0][2], small], axis=1))
    send_up = low(jnp.concatenate([out_state[0], up_state[0]], axis=1))
    send_down = low(down_state[0]).reshape(fold, rows, width).transpose(1, 0, 2).reshape(rows, fold * width)
    got = gather_piece(send_qkv, sizes)
    got_up = gather_piece(send_up, sizes)
    got_down = gather_piece(send_down, sizes)

    here = routed[:, :, None] == jnp.arange(length, dtype=jnp.int32)[None, None, :]
    pick = here.astype(bf16)
    is_routed = jnp.any(here, axis=1)
    picked = dot(pick, tokens, "sct,std->scd").astype(bf16).reshape(count, width)
    back_cot = dot(pick, cotangent, "sct,std->scd").reshape(count, width)
    segs = jnp.sum(jnp.where(here, segment_ids[:, None, :], 0), axis=-1)

    w_qkv, w_small = assemble(*got, pos, sizes, [(0, 3 * width), (3 * width, SMALL)])
    w_qkv = w_qkv.reshape(width, 3 * width)
    w_small = w_small.reshape(width, SMALL)
    router_low = w_small[:, 0]
    gain_one = w_small[:, 1].astype(f32)
    gain_two = w_small[:, 2].astype(f32)

    picked_f = picked.astype(f32)
    score = jnp.dot(picked, router_low, preferred_element_type=f32)
    normed_one, pull_one = jax.vjp(norm_scale, picked_f, gain_one)
    hidden_one = low(normed_one)
    projected = low(dot(hidden_one, w_qkv, "rd,de->re"))
    heads = projected.reshape(seqs, capacity, 3, HEADS, head_size)
    queries, keys, values = heads[:, :, 0], heads[:, :, 1], heads[:, :, 2]
    allowed = (segs[:, :, None] == segs[:, None, :]) & (routed[:, None, :] <= routed[:, :, None])
    logits = dot(queries, keys, "sqhd,skhd->shqk") * scale
    logits = jnp.where(allowed[:, None], logits, -1e30)
    probs = jax.nn.softmax(logits, axis=-1)
    probs_low = low(probs)
    mixed = low(dot(probs_low, values, "shqk,skhd->sqhd")).reshape(count, width)

    w_out, w_up = assemble(*got_up, pos, sizes, [(0, width), (width, hidden)])
    w_out = w_out.reshape(width, width)
    w_up = w_up.reshape(width, hidden)
    attended = dot(mixed, w_out, "rd,de->re")
    first = picked_f + score[:, None] * attended
    normed_two, pull_two = jax.vjp(norm_scale, first, gain_two)
    hidden_two = low(normed_two)
    inner_pre = dot(hidden_two, w_up, "rd,df->rf")
    activ, pull_gelu = jax.vjp(gelu_tanh, inner_pre)
    activ_low = low(activ)
    grad_down_out = low(score[:, None] * back_cot)

    grad_wdown = low(dot(activ_low, grad_down_out, "rf,re->fe"))
    grad_wdown = grad_wdown.reshape(-1, fold, rows, width)
    own, other = disassemble([grad_wdown[:, i] for i in range(fold)], pos, sizes)
    sum_down = scatter_piece(own, other, sizes)

    (w_down,) = assemble_down(*got_down, pos, sizes, fold, width)
    w_down = w_down.reshape(hidden, width)
    down_out = dot(activ_low, w_down, "rf,fe->re")
    second = first + score[:, None] * down_out
    second = low(second).reshape(seqs, capacity, width)
    block_out = jnp.where(is_routed[:, :, None], low(dot(pick, second, "sct,scd->std")), tokens)

    grad_score = jnp.sum(back_cot * down_out, axis=-1)
    grad_activ = dot(grad_down_out, w_down, "re,fe->rf")
    grad_pre = low(pull_gelu(grad_activ)[0])
    grad_wup = low(dot(hidden_two, grad_pre, "rd,rf->df")).reshape(-1, rows, hidden)
    own, other = disassemble([grad_wup], pos, sizes)
    sum_up = scatter_piece(own, other, sizes)

    grad_hidden_two = dot(grad_pre, w_up, "rf,df->rd")
    grad_first_norm, grad_gain_two = pull_two(grad_hidden_two)
    grad_first = back_cot + grad_first_norm
    grad_attended = low(score[:, None] * grad_first)
    grad_score = grad_score + jnp.sum(grad_first * attended, axis=-1)
    grad_mixed = low(dot(grad_attended, w_out, "re,de->rd")).reshape(seqs, capacity, HEADS, head_size)
    grad_wout = low(dot(mixed, grad_attended, "rd,re->de"))

    grad_probs = dot(grad_mixed, values, "sqhd,skhd->shqk")
    inner_sum = jnp.sum(probs * grad_probs, axis=-1, keepdims=True)
    grad_logits = low(probs * (grad_probs - inner_sum))
    grad_query = low(dot(grad_logits, keys, "shqk,skhd->sqhd") * scale)
    grad_key = low(dot(grad_logits, queries, "shqk,sqhd->skhd") * scale)
    grad_value = low(dot(probs_low, grad_mixed, "shqk,sqhd->skhd"))
    grad_projected = jnp.concatenate([g.reshape(count, width) for g in (grad_query, grad_key, grad_value)], axis=1)
    grad_wqkv = low(dot(hidden_one, grad_projected, "rd,re->de"))
    grad_hidden_one = dot(grad_projected, w_qkv, "re,de->rd")
    grad_picked_norm, grad_gain_one = pull_one(grad_hidden_one)
    grad_rows = grad_first + grad_picked_norm + grad_score[:, None] * router_low.astype(f32)[None, :]
    grad_router = jnp.sum(grad_score[:, None] * picked_f, axis=0)
    grad_small = jnp.stack([grad_router, grad_gain_one, grad_gain_two], axis=1)
    grad_small = low(jnp.pad(grad_small, ((0, 0), (0, SMALL - 3))))
    parts = [grad_wqkv.reshape(-1, rows, 3 * width), grad_wout.reshape(-1, rows, width), grad_small.reshape(-1, rows, SMALL)]
    own, other = disassemble(parts, pos, sizes)
    sum_rest = scatter_piece(own, other, sizes)

    grad_rows = low(grad_rows).reshape(seqs, capacity, width)
    tokens_grad = jnp.where(is_routed[:, :, None], low(dot(pick, grad_rows, "sct,scd->std")), cotangent)

    grad_small = sum_rest[:, 4 * width :]
    grads = (
        jnp.stack([sum_rest[:, i * width : (i + 1) * width] for i in range(3)]),
        sum_rest[:, 3 * width : 4 * width],
        sum_up,
        sum_down.reshape(rows, fold, width).transpose(1, 0, 2).reshape(fold * rows, width),
        grad_small[:, 0],
        grad_small[:, 1:3].T,
    )
    decays = (decay_rate, decay_rate, decay_rate, decay_rate, 0.0, 0.0)
    results = [block_out, tokens_grad]
    for state, grad, decay, rate in zip(states, grads, decays, learn_rates):
        results = results + adamw(state, grad, decay, rate)
    return tuple(results)


def assemble_down(here, there, pos, sizes, fold, width):
    ny, nb = sizes["y"], sizes["b"]
    rows = here[0].shape[-2]
    devices = 2 * ny * nb * sizes["a"]
    sources = here + there
    blocks = places(sizes)

    def kernel(pos_ref, *refs):
        ins, out, sems = refs[: len(sources)], refs[-2], refs[-1]
        started = []
        for kc, part, ky, kb, ka, steps in blocks:
            base = kc * (ny + nb)
            ref = ins[base + ky].at[kb, ka] if part == 0 else ins[base + ny + kb].at[ky, ka]
            where = owner(pos_ref, steps, sizes)
            for j in range(fold):
                copy = pltpu.make_async_copy(ref.at[:, pl.ds(j * width, width)], out.at[where, j], sems.at[len(started)])
                copy.start()
                started.append(copy)
        for copy in started:
            copy.wait()

    return pl.pallas_call(
        kernel,
        out_shape=[jax.ShapeDtypeStruct((devices, fold, rows, width), bf16)],
        in_specs=[pl.BlockSpec(memory_space=pltpu.SMEM)] + [pl.BlockSpec(memory_space=pl.ANY)] * len(sources),
        out_specs=[pl.BlockSpec(memory_space=pl.ANY)],
        scratch_shapes=[pltpu.SemaphoreType.DMA((len(blocks) * fold,))],
        cost_estimate=pl.CostEstimate(flops=0, transcendentals=0, bytes_accessed=4 * devices * fold * rows * width),
        name="assemble_down",
    )(pos, *sources)


def solution(mesh):
    lead = mesh.shape["dp"] // 2
    inner = mesh.shape["fsdp"] // 4
    names = ("y", "c", "a", "b")
    fine = Mesh(mesh.devices.reshape(lead, 2, 4, inner), names)
    sizes = dict(zip(names, (lead, 2, 4, inner)))
    head, second, only = P(names, None, None), P(None, names, None), P(names, None)
    weights = (second,) * 4 + (only,) * 12 + (P(names),) * 4 + (P(None, names),) * 4
    return jax.shard_map(
        functools.partial(body, sizes),
        mesh=fine,
        in_specs=(head, head, only, only) + weights,
        out_specs=(head, head) + weights,
        check_vma=False,
    )
```

time: 920 us -> 1290 us (1.40)
  Pallas kernels: 0 us -> 897 us
  waiting for transfers between devices: 423 us -> 131 us
  blocking collectives: 148 us -> 0 us
  local copies, waits for them, and re-layouts: 199 us -> 71.3 us
  starting transfers between devices: 0.33 us -> 62.9 us
    pallas_call x0 -> x6, Pallas kernels: none -> 897 us  [the longest x3 448 us: disassemble(): pl.pallas_call(kernel, out_shape=[first, second, first, second], in_specs...]
    reduce_scatter x3 -> x0, waiting for transfers between devices: 274 us -> none  [the longest x1 139 us: reduce_grads(): lax.psum_scatter(terms[2], ('dp', 'fsdp'), scatter_dimension=0, tiled=True)]
    scatter x2 -> x0, local copies, waits for them, and re-layouts: 131 us -> none  [the longest x1 65.9 us: body(): cotangent.at[seq_index, routed]]
    ppermute x0 -> x60, waiting for transfers between devices: none -> 131 us  [shifted(): return lax.ppermute(value, axis, [(i, (i + step) % n) for i in range(n)])]
    all_gather x4 -> x0, waiting for transfers between devices: 90.3 us -> none  [the longest x1 63.9 us: gather_weights(): lax.all_gather(pieces[3], ('dp', 'fsdp'), axis=0, tiled=True)]
    unnamed x2 -> x0, blocking collectives: 82.4 us -> none
    all_gather x1 -> x0, blocking collectives: 65.5 us -> none  [gather_weights(): lax.all_gather(pieces[5], ('dp', 'fsdp'), axis=1, tiled=True)]
    ppermute x0 -> x60, starting transfers between devices: none -> 62.9 us  [shifted(): return lax.ppermute(value, axis, [(i, (i + step) % n) for i in range(n)])]
  transfers between devices with their start and end apart: 8 -> 60, of which waited for: 5 -> 26; matrix products, arithmetic and copies ran while one was open for 27% -> 6% of each run, Pallas kernels for 0% -> 21%
where the time goes in v1:
time: 1290 us
  Pallas kernels  897 us (70%)
  waiting for transfers between devices  131 us (10%)
  matrix products  90 us (7%)
  local copies, waits for them, and re-layouts  71.3 us (6%)
  starting transfers between devices  62.9 us (5%)
  other arithmetic  30.7 us (2%)
    pallas_call x3, Pallas kernels, disassemble(): pl.pallas_call(kernel, out_shape=[first, second, first, second], in_specs...  448 us
    pallas_call x2, Pallas kernels, assemble(): pl.pallas_call(kernel, out_shape=[jax.ShapeDtypeStruct((devices, rows, wi...  303 us
    pallas_call x1, Pallas kernels, assemble_down(): pl.pallas_call(kernel, out_shape=[jax.ShapeDtypeStruct((devices, fold, ro...  146 us
    ppermute x60, waiting for transfers between devices, shifted(): return lax.ppermute(value, axis, [(i, (i + step) % n) for i in range(n)])  131 us
    dot_general x22, matrix products, dot(): return jnp.einsum(spec, a, b, preferred_element_type=f32)  89.7 us
    ppermute x60, starting transfers between devices, shifted(): return lax.ppermute(value, axis, [(i, (i + step) % n) for i in range(n)])  62.9 us
  transfers between devices with their start and end apart: 60, of which 26 were waited for; matrix products, arithmetic and copies ran while one was open for 6% of the time, Pallas kernels for 21%

profile of v1, /device:TPU:0, one launch (start us, length us, event | category | flops | bytes accessed | tf_op | source)
XLA Modules:
  0.0 1285.6 jit_solution(18099508061456566424)
XLA Ops:
  3.3 3.1 collective-permute-start
  16.3 4.0 fusion.19
  27.0 8.5 collective-permute-done.14
  41.9 5.2 collective-permute-done.16
  50.0 7.6 collective-permute-done.2.refs_1_
  59.6 13.0 %collective-permute-done.13.refs_1_ = bf16[2,2,24,3840]{3,2,1,0:T(8,128)(2,1)} collective-permute-done((bf16[2,2,24,3840]{3,2,1,0:T(8,128)(2,1)}, bf16[2,2,24,3840]{3,2,1,0:T(8,128)(2,1)}, u32[]{:S(2)}, u32[]{:S(2)}) %collective-permute-start.13) | collective-permute-done | bytes 737312 | tf_op jit(solution)/shard_map/ppermute | solution.py:27
  73.9 121.5 %assemble.2 = (bf16[32,24,2304]{2,1,0:T(8,128)(2,1)}, bf16[32,24,256]{2,1,0:T(8,128)(2,1)}) custom-call(s32[4]{0:T(128)} %pad_add_fusion.pos_ref, bf16[2,2,24,2560]{3,2,1,0:T(8,128)(2,1)} %copy-done.13, bf16[2,2,24,2560]{3,2,1,0:T(8,128)(2,1)} %copy-done.29, bf16[2,2,24,2560]{3,2,1,0:T(8,128)(2,1)} %copy-done.14, bf16[2,2,24,2560]{3,2,1,0:T(8,128)(2,1)} %copy-done.31, ...), custom_call_target="tpu_custom_call" | custom-call | bytes 7864320 | tf_op jit(solution)/shard_map/assemble/pallas_call | solution.py:108
  197.2 3.9 convolution_convert_fusion.3
  201.1 5.4 reshape.386
  206.5 5.9 fusion.120
  214.8 3.0 copy.184
  217.9 3.0 copy.183
  232.3 5.4 multiply_convert_fusion.6
  237.7 181.0 %assemble.3 = (bf16[32,24,768]{2,1,0:T(8,128)(2,1)}, bf16[32,24,3072]{2,1,0:T(8,128)(2,1)}) custom-call(s32[4]{0:T(128)} %pad_add_fusion.pos_ref, bf16[2,2,24,3840]{3,2,1,0:T(8,128)(2,1)} %pad_maximum_fusion.refs_0_, bf16[2,2,24,3840]{3,2,1,0:T(8,128)(2,1)} %collective-permute-done.13.refs_1_, bf16[2,2,24,3840]{3,2,1,0:T(8,128)(2,1)} %pad_maximum_fusion.1.refs_2_, ...), custom_call_target="tpu_custom_call" | custom-call | bytes 11796480 | tf_op jit(solution)/shard_map/assemble/pallas_call | solution.py:108
  418.7 3.4 convert_add_fusion
  424.9 3.9 convolution_convert_fusion
  431.0 145.9 %disassemble.5 = (bf16[2,2,2,24,3072]{4,3,2,1,0:T(8,128)(2,1)}, bf16[2,2,2,24,3072]{4,3,2,1,0:T(8,128)(2,1)}, bf16[2,2,2,24,3072]{4,3,2,1,0:T(8,128)(2,1)}, bf16[2,2,2,24,3072]{4,3,2,1,0:T(8,128)(2,1)}) custom-call(s32[4]{0:T(128)} %pad_add_fusion.pos_ref, bf16[32,24,768]{2,1,0:T(8,128)(2,1)} %get-tuple-element.171.refs_0_, ...), custom_call_target="tpu_custom_call" | custom-call | bytes 9437184 | tf_op jit(solution)/shard_map/disassemble/pallas_call | solution.py:144
  585.3 11.9 collective-permute-done.56
  600.7 5.0 collective-permute-done.57
  609.8 4.7 collective-permute-done.59
  614.5 3.8 collective-permute-done.58
  625.3 4.3 collective-permute-done.22
  631.2 5.2 collective-permute-done.25
  638.7 7.8 collective-permute-done.27
  648.8 8.2 collective-permute-done.24.refs_1_
  660.2 145.9 %assemble_down.1 = bf16[32,4,24,768]{3,2,1,0:T(8,128)(2,1)} custom-call(s32[4]{0:T(128)} %pad_add_fusion.pos_ref, bf16[2,2,24,3072]{3,2,1,0:T(8,128)(2,1)} %copy-done.11, bf16[2,2,24,3072]{3,2,1,0:T(8,128)(2,1)} %collective-permute-done.24.refs_1_, bf16[2,2,24,3072]{3,2,1,0:T(8,128)(2,1)} %copy-done.12, ...), custom_call_target="tpu_custom_call" | custom-call | bytes 9437184 | tf_op jit(solution)/shard_map/assemble_down/pallas_call | solution.py:326
  806.1 8.5 fusion.7
  814.6 6.1 multiply_reduce_fusion.1
  820.8 7.5 multiply_reduce_fusion.3
  830.0 3.5 reshape.387
  833.5 4.1 copy.146
  837.7 4.9 multiply_reduce_fusion
  842.6 4.6 multiply_convert_fusion
  854.0 4.0 reshape.370
  865.2 3.4 copy.153
  868.7 4.2 reshape.372
  875.9 6.2 fusion.18
  882.1 4.1 convolution_convert_fusion.2
  888.1 4.5 convolution_convert_fusion.1
  894.2 157.5 %disassemble.3 = (bf16[2,2,2,24,3328]{4,3,2,1,0:T(8,128)(2,1)}, bf16[2,2,2,24,3328]{4,3,2,1,0:T(8,128)(2,1)}, bf16[2,2,2,24,3328]{4,3,2,1,0:T(8,128)(2,1)}, bf16[2,2,2,24,3328]{4,3,2,1,0:T(8,128)(2,1)}) custom-call(s32[4]{0:T(128)} %pad_add_fusion.pos_ref, bf16[32,24,2304]{2,1,0:T(8,128)(2,1)} %bitcast.302, bf16[32,24,768]{2,1,0:T(8,128)(2,1)} %bitcast.301, ...), custom_call_target="tpu_custom_call" | custom-call | bytes 10223616 | tf_op jit(solution)/shard_map/disassemble/pallas_call | solution.py:144
  1052.3 145.0 %disassemble.4 = (bf16[2,2,2,24,3072]{4,3,2,1,0:T(8,128)(2,1)}, bf16[2,2,2,24,3072]{4,3,2,1,0:T(8,128)(2,1)}, bf16[2,2,2,24,3072]{4,3,2,1,0:T(8,128)(2,1)}, bf16[2,2,2,24,3072]{4,3,2,1,0:T(8,128)(2,1)}) custom-call(s32[4]{0:T(128)} %pad_add_fusion.pos_ref, bf16[32,24,3072]{2,1,0:T(8,128)(2,1)} %bitcast.297), custom_call_target="tpu_custom_call" | custom-call | bytes 9437184 | tf_op jit(solution)/shard_map/disassemble/pallas_call | solution.py:144
  1199.8 7.7 convert_select_fusion.1
  1207.5 8.1 convert_select_fusion
  1224.8 7.5 collective-permute-done.47
  1235.8 12.2 collective-permute-done.34
  1250.7 3.6 collective-permute-done.48
  1264.3 6.4 collective-permute-done.49
  1272.2 7.5 collective-permute-done.40
  (377 shorter events, 141.5 us)
Async XLA Ops:
  3.3 17.1 %collective-permute-start = (bf16[24,2560]{1,0:T(8,128)(2,1)S(1)}, bf16[24,2560]{1,0:T(8,128)(2,1)S(1)}, u32[]{:S(2)}, u32[]{:S(2)}) collective-permute-start(bf16[24,2560]{1,0:T(8,128)(2,1)S(1)} %concatenate.42), channel_id=1, source_target_pairs={{0,2},{2,4},{4,6},{6,0},{1,3},{3,5},{5,7},{7,1},{8,10},{10,12},{12... | collective-permute-start | bytes 368648 | tf_op jit(solution)/shard_map/ppermute | solution.py:27
  6.4 14.3 %collective-permute-start.4 = (bf16[24,2560]{1,0:T(8,128)(2,1)S(1)}, bf16[24,2560]{1,0:T(8,128)(2,1)S(1)}, u32[]{:S(2)}, u32[]{:S(2)}) collective-permute-start(bf16[24,2560]{1,0:T(8,128)(2,1)S(1)} %concatenate.42), channel_id=1, source_target_pairs={{0,6},{2,0},{4,2},{6,4},{1,7},{3,1},{5,3},{7,5},{8,14},{10,8},{12,... | collective-permute-start | bytes 368648 | tf_op jit(solution)/shard_map/ppermute | solution.py:27
  8.5 15.2 %collective-permute-start.3 = (bf16[24,2560]{1,0:T(8,128)(2,1)S(1)}, bf16[24,2560]{1,0:T(8,128)(2,1)S(1)}, u32[]{:S(2)}, u32[]{:S(2)}) collective-permute-start(bf16[24,2560]{1,0:T(8,128)(2,1)S(1)} %concatenate.42), channel_id=1, source_target_pairs={{0,4},{2,6},{4,0},{6,2},{1,5},{3,7},{5,1},{7,3},{8,12},{10,14},{12... | collective-permute-start | bytes 368648 | tf_op jit(solution)/shard_map/ppermute | solution.py:27
  11.3 14.1 %collective-permute-start.11 = (bf16[24,3840]{1,0:T(8,128)(2,1)S(1)}, bf16[24,3840]{1,0:T(8,128)(2,1)S(1)}, u32[]{:S(2)}, u32[]{:S(2)}) collective-permute-start(bf16[24,3840]{1,0:T(8,128)(2,1)S(1)} %pad_maximum_fusion.13), channel_id=1, source_target_pairs={{0,2},{2,4},{4,6},{6,0},{1,3},{3,5},{5,7},{7,1},{8,10},{10,12},{12... | collective-permute-start | bytes 552968 | tf_op jit(solution)/shard_map/ppermute | solution.py:27
  12.9 14.1 %collective-permute-start.15 = (bf16[24,3840]{1,0:T(8,128)(2,1)S(1)}, bf16[24,3840]{1,0:T(8,128)(2,1)S(1)}, u32[]{:S(2)}, u32[]{:S(2)}) collective-permute-start(bf16[24,3840]{1,0:T(8,128)(2,1)S(1)} %pad_maximum_fusion.13), channel_id=1, source_target_pairs={{0,6},{2,0},{4,2},{6,4},{1,7},{3,1},{5,3},{7,5},{8,14},{10,8},{12,... | collective-permute-start | bytes 552968 | tf_op jit(solution)/shard_map/ppermute | solution.py:27
  20.4 15.1 %collective-permute-start.14 = (bf16[24,3840]{1,0:T(8,128)(2,1)S(1)}, bf16[24,3840]{1,0:T(8,128)(2,1)S(1)}, u32[]{:S(2)}, u32[]{:S(2)}) collective-permute-start(bf16[24,3840]{1,0:T(8,128)(2,1)S(1)} %pad_maximum_fusion.13), channel_id=1, source_target_pairs={{0,4},{2,6},{4,0},{6,2},{1,5},{3,7},{5,1},{7,3},{8,12},{10,14},{12... | collective-permute-start | bytes 552968 | tf_op jit(solution)/shard_map/ppermute | solution.py:27
  20.7 16.4 %collective-permute-start.1 = (bf16[2,24,2560]{2,1,0:T(8,128)(2,1)S(1)}, bf16[2,24,2560]{2,1,0:T(8,128)(2,1)S(1)}, u32[]{:S(2)}, u32[]{:S(2)}) collective-permute-start(bf16[2,24,2560]{2,1,0:T(8,128)(2,1)S(1)} %get-tuple-element.199), channel_id=1, source_target_pairs={{0,1},{1,0},{2,3},{3,2},{4,5},{5,4},{6,7},{7,6},{8,9},{9,8},{10,11... | collective-permute-start | bytes 737288 | tf_op jit(solution)/shard_map/ppermute | solution.py:27
  23.7 14.0 %collective-permute-start.5 = (bf16[2,24,2560]{2,1,0:T(8,128)(2,1)S(1)}, bf16[2,24,2560]{2,1,0:T(8,128)(2,1)S(1)}, u32[]{:S(2)}, u32[]{:S(2)}) collective-permute-start(bf16[2,24,2560]{2,1,0:T(8,128)(2,1)S(1)} %get-tuple-element.197), channel_id=1, source_target_pairs={{0,16},{16,0},{1,17},{17,1},{2,18},{18,2},{3,19},{19,3},{4,20},{20... | collective-permute-start | bytes 737288 | tf_op jit(solution)/shard_map/ppermute | solution.py:27
  25.4 13.9 %collective-permute-start.12 = (bf16[2,24,3840]{2,1,0:T(8,128)(2,1)S(1)}, bf16[2,24,3840]{2,1,0:T(8,128)(2,1)S(1)}, u32[]{:S(2)}, u32[]{:S(2)}) collective-permute-start(bf16[2,24,3840]{2,1,0:T(8,128)(2,1)S(1)} %get-tuple-element.181), channel_id=1, source_target_pairs={{0,1},{1,0},{2,3},{3,2},{4,5},{5,4},{6,7},{7,6},{8,9},{9,8},{10,11... | collective-permute-start | bytes 1105928 | tf_op jit(solution)/shard_map/ppermute | solution.py:27
  35.5 11.5 collective-permute-start.16
  37.2 20.4 %collective-permute-start.2 = (bf16[2,2,24,2560]{3,2,1,0:T(8,128)(2,1)S(1)}, bf16[2,2,24,2560]{3,2,1,0:T(8,128)(2,1)S(1)}, u32[]{:S(2)}, u32[]{:S(2)}) collective-permute-start(bf16[2,2,24,2560]{3,2,1,0:T(8,128)(2,1)S(1)} %pad_maximum_fusion.4.refs_0_), channel_id=1, source_target_pairs={{0,16},{16,0},{1,17},{17,1},{2,18},{18,2},{3,19},{19,3},{4,20},{20... | collective-permute-start | bytes 1474568 | tf_op jit(solution)/shard_map/ppermute | solution.py:27
  37.7 20.3 %collective-permute-start.7 = (bf16[2,2,24,2560]{3,2,1,0:T(8,128)(2,1)S(1)}, bf16[2,2,24,2560]{3,2,1,0:T(8,128)(2,1)S(1)}, u32[]{:S(2)}, u32[]{:S(2)}) collective-permute-start(bf16[2,2,24,2560]{3,2,1,0:T(8,128)(2,1)S(1)} %pad_maximum_fusion.4.refs_0_), channel_id=1, source_target_pairs={{0,8},{8,0},{1,9},{9,1},{2,10},{10,2},{3,11},{11,3},{4,12},{12,4},... | collective-permute-start | bytes 1474568 | tf_op jit(solution)/shard_map/ppermute | solution.py:27
  37.8 19.8 %collective-permute-start.6 = (bf16[2,2,24,2560]{3,2,1,0:T(8,128)(2,1)S(1)}, bf16[2,2,24,2560]{3,2,1,0:T(8,128)(2,1)S(1)}, u32[]{:S(2)}, u32[]{:S(2)}) collective-permute-start(bf16[2,2,24,2560]{3,2,1,0:T(8,128)(2,1)S(1)} %pad_maximum_fusion.5.refs_2_), channel_id=1, source_target_pairs={{0,1},{1,0},{2,3},{3,2},{4,5},{5,4},{6,7},{7,6},{8,9},{9,8},{10,11... | collective-permute-start | bytes 1474568 | tf_op jit(solution)/shard_map/ppermute | solution.py:27
  40.3 32.2 %collective-permute-start.13 = (bf16[2,2,24,3840]{3,2,1,0:T(8,128)(2,1)}, bf16[2,2,24,3840]{3,2,1,0:T(8,128)(2,1)}, u32[]{:S(2)}, u32[]{:S(2)}) collective-permute-start(bf16[2,2,24,3840]{3,2,1,0:T(8,128)(2,1)} %pad_maximum_fusion.refs_0_), channel_id=1, source_target_pairs={{0,16},{16,0},{1,17},{17,1},{2,18},{18,2},{3,19},{19,3},{4,20},{20... | collective-permute-start | bytes 2211848 | tf_op jit(solution)/shard_map/ppermute | solution.py:27
  48.0 24.6 %collective-permute-start.17 = (bf16[2,2,24,3840]{3,2,1,0:T(8,128)(2,1)}, bf16[2,2,24,3840]{3,2,1,0:T(8,128)(2,1)}, u32[]{:S(2)}, u32[]{:S(2)}) collective-permute-start(bf16[2,2,24,3840]{3,2,1,0:T(8,128)(2,1)} %pad_maximum_fusion.1.refs_2_), channel_id=1, source_target_pairs={{0,1},{1,0},{2,3},{3,2},{4,5},{5,4},{6,7},{7,6},{8,9},{9,8},{10,11... | collective-permute-start | bytes 2211848 | tf_op jit(solution)/shard_map/ppermute | solution.py:27
  57.6 15.5 %collective-permute-start.8 = (bf16[2,2,24,2560]{3,2,1,0:T(8,128)(2,1)S(1)}, bf16[2,2,24,2560]{3,2,1,0:T(8,128)(2,1)S(1)}, u32[]{:S(2)}, u32[]{:S(2)}) collective-permute-start(bf16[2,2,24,2560]{3,2,1,0:T(8,128)(2,1)S(1)} %collective-permute-done.2.refs_1_), channel_id=1, source_target_pairs={{0,8},{8,0},{1,9},{9,1},{2,10},{10,2},{3,11},{11,3},{4,12},{12,4},... | collective-permute-start | bytes 1474568 | tf_op jit(solution)/shard_map/ppermute | solution.py:27
  58.1 15.7 %collective-permute-start.10 = (bf16[2,2,24,2560]{3,2,1,0:T(8,128)(2,1)S(1)}, bf16[2,2,24,2560]{3,2,1,0:T(8,128)(2,1)}, u32[]{:S(2)}, u32[]{:S(2)}) collective-permute-start(bf16[2,2,24,2560]{3,2,1,0:T(8,128)(2,1)S(1)} %collective-permute-done.6.refs_3_), channel_id=1, source_target_pairs={{0,8},{8,0},{1,9},{9,1},{2,10},{10,2},{3,11},{11,3},{4,12},{12,4},... | collective-permute-start | bytes 1474568 | tf_op jit(solution)/shard_map/ppermute | solution.py:27
  59.4 178.2 %collective-permute-start.18 = (bf16[2,2,24,3840]{3,2,1,0:T(8,128)(2,1)}, bf16[2,2,24,3840]{3,2,1,0:T(8,128)(2,1)}, u32[]{:S(2)}, u32[]{:S(2)}) collective-permute-start(bf16[2,2,24,3840]{3,2,1,0:T(8,128)(2,1)} %pad_maximum_fusion.refs_0_), channel_id=1, source_target_pairs={{0,8},{8,0},{1,9},{9,1},{2,10},{10,2},{3,11},{11,3},{4,12},{12,4},... | collective-permute-start | bytes 2211848 | tf_op jit(solution)/shard_map/ppermute | solution.py:27
  72.5 165.1 %collective-permute-start.20 = (bf16[2,2,24,3840]{3,2,1,0:T(8,128)(2,1)}, bf16[2,2,24,3840]{3,2,1,0:T(8,128)(2,1)}, u32[]{:S(2)}, u32[]{:S(2)}) collective-permute-start(bf16[2,2,24,3840]{3,2,1,0:T(8,128)(2,1)} %pad_maximum_fusion.1.refs_2_), channel_id=1, source_target_pairs={{0,8},{8,0},{1,9},{9,1},{2,10},{10,2},{3,11},{11,3},{4,12},{12,4},... | collective-permute-start | bytes 2211848 | tf_op jit(solution)/shard_map/ppermute | solution.py:27
  72.5 165.1 %collective-permute-start.19 = (bf16[2,2,24,3840]{3,2,1,0:T(8,128)(2,1)}, bf16[2,2,24,3840]{3,2,1,0:T(8,128)(2,1)}, u32[]{:S(2)}, u32[]{:S(2)}) collective-permute-start(bf16[2,2,24,3840]{3,2,1,0:T(8,128)(2,1)} %collective-permute-done.13.refs_1_), channel_id=1, source_target_pairs={{0,8},{8,0},{1,9},{9,1},{2,10},{10,2},{3,11},{11,3},{4,12},{12,4},... | collective-permute-start | bytes 2211848 | tf_op jit(solution)/shard_map/ppermute | solution.py:27
  73.0 164.6 %collective-permute-start.21 = (bf16[2,2,24,3840]{3,2,1,0:T(8,128)(2,1)}, bf16[2,2,24,3840]{3,2,1,0:T(8,128)(2,1)}, u32[]{:S(2)}, u32[]{:S(2)}) collective-permute-start(bf16[2,2,24,3840]{3,2,1,0:T(8,128)(2,1)} %collective-permute-done.17.refs_3_), channel_id=1, source_target_pairs={{0,8},{8,0},{1,9},{9,1},{2,10},{10,2},{3,11},{11,3},{4,12},{12,4},... | collective-permute-start | bytes 2211848 | tf_op jit(solution)/shard_map/ppermute | solution.py:27
  581.8 15.4 %collective-permute-start.56 = (bf16[2,2,24,3072]{3,2,1,0:T(8,128)(2,1)S(1)}, bf16[2,2,24,3072]{3,2,1,0:T(8,128)(2,1)S(1)}, u32[]{:S(2)}, u32[]{:S(2)}) collective-permute-start(bf16[2,2,24,3072]{3,2,1,0:T(8,128)(2,1)S(1)} %fusion.69), channel_id=1, source_target_pairs={{0,16},{16,0},{1,17},{17,1},{2,18},{18,2},{3,19},{19,3},{4,20},{20... | collective-permute-start | bytes 1769480 | tf_op jit(solution)/shard_map/ppermute | solution.py:27
  583.7 15.2 %collective-permute-start.52 = (bf16[2,2,24,3072]{3,2,1,0:T(8,128)(2,1)S(1)}, bf16[2,2,24,3072]{3,2,1,0:T(8,128)(2,1)S(1)}, u32[]{:S(2)}, u32[]{:S(2)}) collective-permute-start(bf16[2,2,24,3072]{3,2,1,0:T(8,128)(2,1)S(1)} %fusion.68), channel_id=1, source_target_pairs={{0,1},{1,0},{2,3},{3,2},{4,5},{5,4},{6,7},{7,6},{8,9},{9,8},{10,11... | collective-permute-start | bytes 1769480 | tf_op jit(solution)/shard_map/ppermute | solution.py:27
  605.9 12.4 collective-permute-start.58
  607.9 10.5 collective-permute-start.54
  624.8 11.6 collective-permute-start.25
  636.5 10.0 collective-permute-start.27
  638.1 18.9 %collective-permute-start.24 = (bf16[2,2,24,3072]{3,2,1,0:T(8,128)(2,1)S(1)}, bf16[2,2,24,3072]{3,2,1,0:T(8,128)(2,1)}, u32[]{:S(2)}, u32[]{:S(2)}) collective-permute-start(bf16[2,2,24,3072]{3,2,1,0:T(8,128)(2,1)S(1)} %pad_maximum_fusion.2.refs_0_), channel_id=1, source_target_pairs={{0,16},{16,0},{1,17},{17,1},{2,18},{18,2},{3,19},{19,3},{4,20},{20... | collective-permute-start | bytes 1769480 | tf_op jit(solution)/shard_map/ppermute | solution.py:27
  646.5 11.0 collective-permute-start.28
  648.3 9.9 collective-permute-start.29
  648.3 9.9 collective-permute-start.31
  1051.7 167.9 %collective-permute-start.33 = (bf16[2,2,2,24,3328]{4,3,2,1,0:T(8,128)(2,1)}, bf16[2,2,2,24,3328]{4,3,2,1,0:T(8,128)(2,1)}, u32[]{:S(2)}, u32[]{:S(2)}) collective-permute-start(bf16[2,2,2,24,3328]{4,3,2,1,0:T(8,128)(2,1)} %get-tuple-element.47), channel_id=1, source_target_pairs={{0,8},{8,0},{1,9},{9,1},{2,10},{10,2},{3,11},{11,3},{4,12},{12,4},... | collective-permute-start | bytes 3833864 | tf_op jit(solution)/shard_map/ppermute | solution.py:27
  1051.9 170.3 %collective-permute-start.37 = (bf16[2,2,2,24,3328]{4,3,2,1,0:T(8,128)(2,1)}, bf16[2,2,2,24,3328]{4,3,2,1,0:T(8,128)(2,1)}, u32[]{:S(2)}, u32[]{:S(2)}) collective-permute-start(bf16[2,2,2,24,3328]{4,3,2,1,0:T(8,128)(2,1)} %get-tuple-element.49), channel_id=1, source_target_pairs={{0,8},{8,0},{1,9},{9,1},{2,10},{10,2},{3,11},{11,3},{4,12},{12,4},... | collective-permute-start | bytes 3833864 | tf_op jit(solution)/shard_map/ppermute | solution.py:27
  1197.3 18.3 %collective-permute-start.46 = (bf16[2,2,2,24,3072]{4,3,2,1,0:T(8,128)(2,1)}, bf16[2,2,2,24,3072]{4,3,2,1,0:T(8,128)(2,1)S(1)}, u32[]{:S(2)}, u32[]{:S(2)}) collective-permute-start(bf16[2,2,2,24,3072]{4,3,2,1,0:T(8,128)(2,1)} %get-tuple-element.53), channel_id=1, source_target_pairs={{0,8},{8,0},{1,9},{9,1},{2,10},{10,2},{3,11},{11,3},{4,12},{12,4},... | collective-permute-start | bytes 3538952 | tf_op jit(solution)/shard_map/ppermute | solution.py:27
  1197.5 20.1 %collective-permute-start.42 = (bf16[2,2,2,24,3072]{4,3,2,1,0:T(8,128)(2,1)}, bf16[2,2,2,24,3072]{4,3,2,1,0:T(8,128)(2,1)S(1)}, u32[]{:S(2)}, u32[]{:S(2)}) collective-permute-start(bf16[2,2,2,24,3072]{4,3,2,1,0:T(8,128)(2,1)} %get-tuple-element.51), channel_id=1, source_target_pairs={{0,8},{8,0},{1,9},{9,1},{2,10},{10,2},{3,11},{11,3},{4,12},{12,4},... | collective-permute-start | bytes 3538952 | tf_op jit(solution)/shard_map/ppermute | solution.py:27
  1216.1 16.2 %collective-permute-start.47 = (bf16[2,2,24,3072]{3,2,1,0:T(8,128)(2,1)S(1)}, bf16[2,2,24,3072]{3,2,1,0:T(8,128)(2,1)S(1)}, u32[]{:S(2)}, u32[]{:S(2)}) collective-permute-start(bf16[2,2,24,3072]{3,2,1,0:T(8,128)(2,1)S(1)} %fusion.67), channel_id=1, source_target_pairs={{0,16},{16,0},{1,17},{17,1},{2,18},{18,2},{3,19},{19,3},{4,20},{20... | collective-permute-start | bytes 1769480 | tf_op jit(solution)/shard_map/ppermute | solution.py:27
  1218.0 16.3 %collective-permute-start.43 = (bf16[2,2,24,3072]{3,2,1,0:T(8,128)(2,1)S(1)}, bf16[2,2,24,3072]{3,2,1,0:T(8,128)(2,1)S(1)}, u32[]{:S(2)}, u32[]{:S(2)}) collective-permute-start(bf16[2,2,24,3072]{3,2,1,0:T(8,128)(2,1)S(1)} %fusion.66), channel_id=1, source_target_pairs={{0,1},{1,0},{2,3},{3,2},{4,5},{5,4},{6,7},{7,6},{8,9},{9,8},{10,11... | collective-permute-start | bytes 1769480 | tf_op jit(solution)/shard_map/ppermute | solution.py:27
  1221.3 26.6 %collective-permute-start.34 = (bf16[2,2,24,3328]{3,2,1,0:T(8,128)(2,1)S(1)}, bf16[2,2,24,3328]{3,2,1,0:T(8,128)(2,1)S(1)}, u32[]{:S(2)}, u32[]{:S(2)}) collective-permute-start(bf16[2,2,24,3328]{3,2,1,0:T(8,128)(2,1)S(1)} %fusion.61), channel_id=1, source_target_pairs={{0,1},{1,0},{2,3},{3,2},{4,5},{5,4},{6,7},{7,6},{8,9},{9,8},{10,11... | collective-permute-start | bytes 1916936 | tf_op jit(solution)/shard_map/ppermute | solution.py:27
  1223.9 25.0 %collective-permute-start.38 = (bf16[2,2,24,3328]{3,2,1,0:T(8,128)(2,1)S(1)}, bf16[2,2,24,3328]{3,2,1,0:T(8,128)(2,1)S(1)}, u32[]{:S(2)}, u32[]{:S(2)}) collective-permute-start(bf16[2,2,24,3328]{3,2,1,0:T(8,128)(2,1)S(1)} %fusion.62), channel_id=1, source_target_pairs={{0,16},{16,0},{1,17},{17,1},{2,18},{18,2},{3,19},{19,3},{4,20},{20... | collective-permute-start | bytes 1916936 | tf_op jit(solution)/shard_map/ppermute | solution.py:27
  1232.5 21.8 %collective-permute-start.48 = (bf16[2,24,3072]{2,1,0:T(8,128)(2,1)S(1)}, bf16[2,24,3072]{2,1,0:T(8,128)(2,1)S(1)}, u32[]{:S(2)}, u32[]{:S(2)}) collective-permute-start(bf16[2,24,3072]{2,1,0:T(8,128)(2,1)S(1)} %fusion.84), channel_id=1, source_target_pairs={{0,1},{1,0},{2,3},{3,2},{4,5},{5,4},{6,7},{7,6},{8,9},{9,8},{10,11... | collective-permute-start | bytes 884744 | tf_op jit(solution)/shard_map/ppermute | solution.py:27
  1234.5 22.8 %collective-permute-start.44 = (bf16[2,24,3072]{2,1,0:T(8,128)(2,1)S(1)}, bf16[2,24,3072]{2,1,0:T(8,128)(2,1)S(1)}, u32[]{:S(2)}, u32[]{:S(2)}) collective-permute-start(bf16[2,24,3072]{2,1,0:T(8,128)(2,1)S(1)} %fusion.83), channel_id=1, source_target_pairs={{0,16},{16,0},{1,17},{17,1},{2,18},{18,2},{3,19},{19,3},{4,20},{20... | collective-permute-start | bytes 884744 | tf_op jit(solution)/shard_map/ppermute | solution.py:27
  1248.1 12.0 collective-permute-start.35
  1249.1 10.9 collective-permute-start.39
  1254.4 16.2 %collective-permute-start.49 = (bf16[24,3072]{1,0:T(8,128)(2,1)S(1)}, bf16[24,3072]{1,0:T(8,128)(2,1)S(1)}, u32[]{:S(2)}, u32[]{:S(2)}) collective-permute-start(bf16[24,3072]{1,0:T(8,128)(2,1)S(1)} %get-tuple-element.190), channel_id=1, source_target_pairs={{0,4},{2,6},{4,0},{6,2},{1,5},{3,7},{5,1},{7,3},{8,12},{10,14},{12... | collective-permute-start | bytes 442376 | tf_op jit(solution)/shard_map/ppermute | solution.py:27
  1257.4 13.3 %collective-permute-start.45 = (bf16[24,3072]{1,0:T(8,128)(2,1)S(1)}, bf16[24,3072]{1,0:T(8,128)(2,1)S(1)}, u32[]{:S(2)}, u32[]{:S(2)}) collective-permute-start(bf16[24,3072]{1,0:T(8,128)(2,1)S(1)} %fusion.97), channel_id=1, source_target_pairs={{0,6},{2,0},{4,2},{6,4},{1,7},{3,1},{5,3},{7,5},{8,14},{10,8},{12,... | collective-permute-start | bytes 442376 | tf_op jit(solution)/shard_map/ppermute | solution.py:27
  1260.1 12.1 collective-permute-start.41
  1260.2 19.6 %collective-permute-start.40 = (bf16[24,3328]{1,0:T(8,128)(2,1)S(1)}, bf16[24,3328]{1,0:T(8,128)(2,1)S(1)}, u32[]{:S(2)}, u32[]{:S(2)}) collective-permute-start(bf16[24,3328]{1,0:T(8,128)(2,1)S(1)} %get-tuple-element.185), channel_id=1, source_target_pairs={{0,4},{2,6},{4,0},{6,2},{1,5},{3,7},{5,1},{7,3},{8,12},{10,14},{12... | collective-permute-start | bytes 479240 | tf_op jit(solution)/shard_map/ppermute | solution.py:27
  1263.2 16.5 %collective-permute-start.36 = (bf16[24,3328]{1,0:T(8,128)(2,1)S(1)}, bf16[24,3328]{1,0:T(8,128)(2,1)S(1)}, u32[]{:S(2)}, u32[]{:S(2)}) collective-permute-start(bf16[24,3328]{1,0:T(8,128)(2,1)S(1)} %fusion.96), channel_id=1, source_target_pairs={{0,6},{2,0},{4,2},{6,4},{1,7},{3,1},{5,3},{7,5},{8,14},{10,8},{12,... | collective-permute-start | bytes 479240 | tf_op jit(solution)/shard_map/ppermute | solution.py:27
  (78 other events, 1056.2 us)

commit v2 on v1

--- a/solution.py
+++ b/solution.py
@@ -81,72 +81,75 @@
     return ((y * 2 + c) * sizes["a"] + a) * sizes["b"] + b
 
 
-def assemble(here, there, pos, sizes, cuts):
-    ny, nb = sizes["y"], sizes["b"]
+VMEM = pltpu.CompilerParams(vmem_limit_bytes=60 * 1024 * 1024)
+
+
+def source(ins, block, sizes):
+    kc, part, ky, kb, ka, _ = block
+    base = kc * (sizes["y"] + sizes["b"])
+    return ins[base + ky][kb, ka] if part == 0 else ins[base + sizes["y"] + kb][ky, ka]
+
+
+def assemble(here, there, pos, sizes, cuts, fold=1):
     rows = here[0].shape[-2]
-    devices = 2 * ny * nb * sizes["a"]
+    devices = 2 * sizes["y"] * sizes["b"] * sizes["a"]
     sources = here + there
     blocks = places(sizes)
 
     def kernel(pos_ref, *refs):
-        ins, outs, sems = refs[: len(sources)], refs[len(sources) : -1], refs[-1]
-        copies = []
-        for kc, part, ky, kb, ka, steps in blocks:
-            base = kc * (ny + nb)
-            ref = ins[base + ky].at[kb, ka] if part == 0 else ins[base + ny + kb].at[ky, ka]
-            where = owner(pos_ref, steps, sizes)
-            for (start, width), out in zip(cuts, outs):
-                copies.append((ref.at[:, pl.ds(start, width)], out.at[where]))
-        started = []
-        for i, (src, dst) in enumerate(copies):
-            copy = pltpu.make_async_copy(src, dst, sems.at[i])
-            copy.start()
-            started.append(copy)
-        for copy in started:
-            copy.wait()
-
+        ins, outs = refs[: len(sources)], refs[len(sources) :]
+        for block in blocks:
+            where = owner(pos_ref, block[-1], sizes)
+            value = source(ins, block, sizes)
+            for i, (start, width) in enumerate(cuts):
+                if fold == 1:
+                    outs[i][where] = value[:, start : start + width]
+                else:
+                    outs[0][where * fold + i] = value[:, start : start + width]
+
+    shapes = [jax.ShapeDtypeStruct((devices, rows, width), bf16) for _, width in cuts]
+    if fold > 1:
+        shapes = [jax.ShapeDtypeStruct((devices * fold, rows, cuts[0][1]), bf16)]
+    vmem = pl.BlockSpec(memory_space=pltpu.VMEM)
     return pl.pallas_call(
         kernel,
-        out_shape=[jax.ShapeDtypeStruct((devices, rows, width), bf16) for _, width in cuts],
-        in_specs=[pl.BlockSpec(memory_space=pltpu.SMEM)] + [pl.BlockSpec(memory_space=pl.ANY)] * len(sources),
-        out_specs=[pl.BlockSpec(memory_space=pl.ANY)] * len(cuts),
-        scratch_shapes=[pltpu.SemaphoreType.DMA((len(blocks) * len(cuts),))],
+        out_shape=shapes,
+        in_specs=[pl.BlockSpec(memory_space=pltpu.SMEM)] + [vmem] * len(sources),
+        out_specs=[vmem] * len(shapes),
+        compiler_params=VMEM,
         cost_estimate=pl.CostEstimate(flops=0, transcendentals=0, bytes_accessed=2 * devices * rows * sum(w for _, w in cuts) * 2),
         name="assemble",
     )(pos, *sources)
 
 
-def disassemble(parts, pos, sizes):
+def disassemble(parts, pos, sizes, fold=1):
     ny, nb, half = sizes["y"], sizes["b"], sizes["a"] // 2
     rows = parts[0].shape[1]
-    widths = [p.shape[2] for p in parts]
-    total = sum(widths)
+    total = sum(p.shape[2] for p in parts) * fold
     blocks = places(sizes)
 
     def kernel(pos_ref, *refs):
-        ins, outs, sems = refs[: len(parts)], refs[len(parts) : -1], refs[-1]
-        started = []
+        ins, outs = refs[: len(parts)], refs[len(parts) :]
         for kc, part, ky, kb, ka, steps in blocks:
             ref = outs[kc * 2 + part]
             ref = ref.at[kb, ky, ka] if part == 0 else ref.at[ky, kb, ka]
             where = owner(pos_ref, steps, sizes)
             start = 0
-            for width, src in zip(widths, ins):
-                copy = pltpu.make_async_copy(src.at[where], ref.at[:, pl.ds(start, width)], sems.at[len(started)])
-                copy.start()
-                started.append(copy)
-                start += width
-        for copy in started:
-            copy.wait()
+            for src in ins:
+                for j in range(fold):
+                    width = src.shape[2]
+                    ref[:, start : start + width] = src[where * fold + j]
+                    start += width
 
     first = jax.ShapeDtypeStruct((nb, ny, half, rows, total), bf16)
     second = jax.ShapeDtypeStruct((ny, nb, half, rows, total), bf16)
+    vmem = pl.BlockSpec(memory_space=pltpu.VMEM)
     outs = pl.pallas_call(
         kernel,
         out_shape=[first, second, first, second],
-        in_specs=[pl.BlockSpec(memory_space=pltpu.SMEM)] + [pl.BlockSpec(memory_space=pl.ANY)] * len(parts),
-        out_specs=[pl.BlockSpec(memory_space=pl.ANY)] * 4,
-        scratch_shapes=[pltpu.SemaphoreType.DMA((len(blocks) * len(parts),))],
+        in_specs=[pl.BlockSpec(memory_space=pltpu.SMEM)] + [vmem] * len(parts),
+        out_specs=[vmem] * 4,
+        compiler_params=VMEM,
         cost_estimate=pl.CostEstimate(flops=0, transcendentals=0, bytes_accessed=4 * 2 * ny * nb * 2 * half * rows * total),
         name="disassemble",
     )(pos, *parts)
@@ -239,11 +242,10 @@
     grad_down_out = low(score[:, None] * back_cot)
 
     grad_wdown = low(dot(activ_low, grad_down_out, "rf,re->fe"))
-    grad_wdown = grad_wdown.reshape(-1, fold, rows, width)
-    own, other = disassemble([grad_wdown[:, i] for i in range(fold)], pos, sizes)
+    own, other = disassemble([grad_wdown.reshape(-1, rows, width)], pos, sizes, fold)
     sum_down = scatter_piece(own, other, sizes)
 
-    (w_down,) = assemble_down(*got_down, pos, sizes, fold, width)
+    (w_down,) = assemble(*got_down, pos, sizes, [(i * width, width) for i in range(fold)], fold)
     w_down = w_down.reshape(hidden, width)
     down_out = dot(activ_low, w_down, "rf,fe->re")
     second = first + score[:, None] * down_out
@@ -302,38 +304,6 @@
     return tuple(results)
 
 
-def assemble_down(here, there, pos, sizes, fold, width):
-    ny, nb = sizes["y"], sizes["b"]
-    rows = here[0].shape[-2]
-    devices = 2 * ny * nb * sizes["a"]
-    sources = here + there
-    blocks = places(sizes)
-
-    def kernel(pos_ref, *refs):
-        ins, out, sems = refs[: len(sources)], refs[-2], refs[-1]
-        started = []
-        for kc, part, ky, kb, ka, steps in blocks:
-            base = kc * (ny + nb)
-            ref = ins[base + ky].at[kb, ka] if part == 0 else ins[base + ny + kb].at[ky, ka]
-            where = owner(pos_ref, steps, sizes)
-            for j in range(fold):
-                copy = pltpu.make_async_copy(ref.at[:, pl.ds(j * width, width)], out.at[where, j], sems.at[len(started)])
-                copy.start()
-                started.append(copy)
-        for copy in started:
-            copy.wait()
-
-    return pl.pallas_call(
-        kernel,
-        out_shape=[jax.ShapeDtypeStruct((devices, fold, rows, width), bf16)],
-        in_specs=[pl.BlockSpec(memory_space=pltpu.SMEM)] + [pl.BlockSpec(memory_space=pl.ANY)] * len(sources),
-        out_specs=[pl.BlockSpec(memory_space=pl.ANY)],
-        scratch_shapes=[pltpu.SemaphoreType.DMA((len(blocks) * fold,))],
-        cost_estimate=pl.CostEstimate(flops=0, transcendentals=0, bytes_accessed=4 * devices * fold * rows * width),
-        name="assemble_down",
-    )(pos, *sources)
-
-
 def solution(mesh):
     lead = mesh.shape["dp"] // 2
     inner = mesh.shape["fsdp"] // 4

time: 1290 us -> 419 us (0.32)
  Pallas kernels: 897 us -> 29.9 us
    pallas_call x3, Pallas kernels: 448 us -> 14.9 us  [disassemble(): pl.pallas_call(kernel, out_shape=[first, second, first, second], in_specs...]
    pallas_call x3, Pallas kernels: 448 us -> 14.9 us  [assemble(): pl.pallas_call(kernel, out_shape=shapes, in_specs=[pl.BlockSpec(memory_sp...]
  transfers between devices with their start and end apart: 60 -> 60, of which waited for: 26 -> 26; matrix products, arithmetic and copies ran while one was open for 6% -> 18% of each run, Pallas kernels for 21% -> 2%
where the time goes in v2:
time: 419 us; the launch traced here: 412 us
  waiting for transfers between devices  132 us (32%)
  matrix products  85.2 us (20%)
  local copies, waits for them, and re-layouts  70.1 us (17%)
  starting transfers between devices  62.2 us (15%)
  other arithmetic  30.7 us (7%)
  Pallas kernels  29.9 us (7%)
    ppermute x60, waiting for transfers between devices, shifted(): return lax.ppermute(value, axis, [(i, (i + step) % n) for i in range(n)])  132 us
    dot_general x22, matrix products, dot(): return jnp.einsum(spec, a, b, preferred_element_type=f32)  84.9 us
    ppermute x60, starting transfers between devices, shifted(): return lax.ppermute(value, axis, [(i, (i + step) % n) for i in range(n)])  62.2 us
    unnamed x154, local copies, waits for them, and re-layouts  19.6 us
    pallas_call x3, Pallas kernels, assemble(): pl.pallas_call(kernel, out_shape=shapes, in_specs=[pl.BlockSpec(memory_sp...  14.9 us
    pallas_call x3, Pallas kernels, disassemble(): pl.pallas_call(kernel, out_shape=[first, second, first, second], in_specs...  14.9 us
    reshape x3, local copies, waits for them, and re-layouts, body(): g.reshape(count, width)  11.2 us
    convert_element_type x4, local copies, waits for them, and re-layouts, body(): low = lambda v: v.astype(bf16)  9.95 us
  transfers between devices with their start and end apart: 60, of which 26 were waited for; matrix products, arithmetic and copies ran while one was open for 18% of the time, Pallas kernels for 2%

profile of v2, /device:TPU:0, one launch (start us, length us, event | category | flops | bytes accessed | tf_op | source)
XLA Modules:
  0.0 412.2 jit_solution(13644223010232178132)
XLA Ops:
  3.3 3.1 collective-permute-start
  16.3 4.0 fusion.19
  27.0 8.5 %collective-permute-done.14 = bf16[24,3840]{1,0:T(8,128)(2,1)S(1)} collective-permute-done((bf16[24,3840]{1,0:T(8,128)(2,1)S(1)}, bf16[24,3840]{1,0:T(8,128)(2,1)S(1)}, u32[]{:S(2)}, u32[]{:S(2)}) %collective-permute-start.14) | collective-permute-done | bytes 184352 | tf_op jit(solution)/shard_map/ppermute | solution.py:27
  41.8 5.2 %collective-permute-done.16 = bf16[2,24,3840]{2,1,0:T(8,128)(2,1)S(1)} collective-permute-done((bf16[2,24,3840]{2,1,0:T(8,128)(2,1)S(1)}, bf16[2,24,3840]{2,1,0:T(8,128)(2,1)S(1)}, u32[]{:S(2)}, u32[]{:S(2)}) %collective-permute-start.16) | collective-permute-done | bytes 368672 | tf_op jit(solution)/shard_map/ppermute | solution.py:27
  50.0 7.6 %collective-permute-done.2.refs_1_ = bf16[2,2,24,2560]{3,2,1,0:T(8,128)(2,1)S(1)} collective-permute-done((bf16[2,2,24,2560]{3,2,1,0:T(8,128)(2,1)S(1)}, bf16[2,2,24,2560]{3,2,1,0:T(8,128)(2,1)S(1)}, u32[]{:S(2)}, u32[]{:S(2)}) %collective-permute-start.2) | collective-permute-done | bytes 491552 | tf_op jit(solution)/shard_map/ppermute | solution.py:27
  59.6 13.0 %collective-permute-done.13.refs_1_ = bf16[2,2,24,3840]{3,2,1,0:T(8,128)(2,1)} collective-permute-done((bf16[2,2,24,3840]{3,2,1,0:T(8,128)(2,1)}, bf16[2,2,24,3840]{3,2,1,0:T(8,128)(2,1)}, u32[]{:S(2)}, u32[]{:S(2)}) %collective-permute-start.13) | collective-permute-done | bytes 737312 | tf_op jit(solution)/shard_map/ppermute | solution.py:27
  73.9 4.4 %assemble.3 = (bf16[32,24,2304]{2,1,0:T(8,128)(2,1)}, bf16[32,24,256]{2,1,0:T(8,128)(2,1)}) custom-call(s32[4]{0:T(128)} %pad_add_fusion.pos_ref, bf16[2,2,24,2560]{3,2,1,0:T(8,128)(2,1)} %copy-done.13, bf16[2,2,24,2560]{3,2,1,0:T(8,128)(2,1)} %copy-done.29, bf16[2,2,24,2560]{3,2,1,0:T(8,128)(2,1)} %copy-done.14, bf16[2,2,24,2560]{3,2,1,0:T(8,128)(2,1)} %copy-done.31, ...), custom_call_target="tpu_custom_call" | custom-call | bytes 7864320 | tf_op jit(solution)/shard_map/assemble/pallas_call | solution.py:114
  80.1 3.9 convolution_convert_fusion.3
  84.0 5.4 %reshape.386 = bf16[3,160,3,12,64]{4,3,2,1,0:T(8,128)(2,1)} reshape(bf16[480,2304]{1,0:T(8,128)(2,1)S(1)} %convolution_convert_fusion.3) | data formatting | bytes 4423680 | tf_op jit(solution)/shard_map/reshape | solution.py:223
  89.3 5.8 %fusion.120 = (bf16[3,160,1,12,64]{4,3,2,1,0:T(8,128)(2,1)}, bf16[3,160,1,12,64]{4,3,2,1,0:T(8,128)(2,1)S(1)}, bf16[3,160,1,12,64]{4,3,2,1,0:T(8,128)(2,1)}) fusion(bf16[3,160,3,12,64]{4,3,2,1,0:T(8,128)(2,1)} %reshape.386), kind=kLoop, calls=%fused_computation.258 | loop fusion | bytes 4423680 | tf_op jit(solution)/shard_map/slice | solution.py:224
  100.6 3.0 copy.175
  115.0 5.4 %multiply_convert_fusion.6 = (bf16[3,160,768]{2,1,0:T(8,128)(2,1)}, f32[3,160,768]{2,1,0:T(8,128)}) fusion(f32[3,160]{1,0:T(4,128)S(1)} %mul.465, bf16[3,1280,768]{2,1,0:T(8,128)(2,1)} %param.29, s32[3,160]{1,0:T(4,128)S(1)} %copy-done.44), kind=kOutput, calls=%fused_computation.70 | convolution fusion | flops 945070080 | bytes 8113920 | tf_op jit(solution)/shard_map/sct,std->scd/dot_general | solution.py:178
  120.4 5.7 %assemble.4 = (bf16[32,24,768]{2,1,0:T(8,128)(2,1)}, bf16[32,24,3072]{2,1,0:T(8,128)(2,1)}) custom-call(s32[4]{0:T(128)} %pad_add_fusion.pos_ref, bf16[2,2,24,3840]{3,2,1,0:T(8,128)(2,1)} %pad_maximum_fusion.refs_0_, bf16[2,2,24,3840]{3,2,1,0:T(8,128)(2,1)} %collective-permute-done.13.refs_1_, bf16[2,2,24,3840]{3,2,1,0:T(8,128)(2,1)} %pad_maximum_fusion.1.refs_2_, ...), custom_call_target="tpu_custom_call" | custom-call | bytes 11796480 | tf_op jit(solution)/shard_map/assemble/pallas_call | solution.py:114
  126.1 3.3 convert_add_fusion
  132.2 5.2 %convolution_convert_fusion = bf16[3072,768]{1,0:T(8,128)(2,1)} fusion(f32[480,768]{1,0:T(8,128)S(1)} %bitcast.292, f32[480]{0:T(512)S(1)} %bitcast.328, f32[480,3072]{1,0:T(8,128)S(1)} %fusion.111), kind=kOutput, calls=%fused_computation.17 | convolution fusion | flops 2281291776 | bytes 12093312 | tf_op jit(solution)/shard_map/rf,re->fe/dot_general | solution.py:178
  137.3 4.9 %disassemble.5 = (bf16[2,2,2,24,3072]{4,3,2,1,0:T(8,128)(2,1)}, bf16[2,2,2,24,3072]{4,3,2,1,0:T(8,128)(2,1)}, bf16[2,2,2,24,3072]{4,3,2,1,0:T(8,128)(2,1)}, bf16[2,2,2,24,3072]{4,3,2,1,0:T(8,128)(2,1)}) custom-call(s32[4]{0:T(128)} %pad_add_fusion.pos_ref, bf16[128,24,768]{2,1,0:T(8,128)(2,1)} %bitcast.286), custom_call_target="tpu_custom_call" | custom-call | bytes 9437184 | tf_op jit(solution)/shard_map/disassemble/pallas_call | solution.py:147
  150.7 12.2 %collective-permute-done.56 = bf16[2,2,24,3072]{3,2,1,0:T(8,128)(2,1)S(1)} collective-permute-done((bf16[2,2,24,3072]{3,2,1,0:T(8,128)(2,1)S(1)}, bf16[2,2,24,3072]{3,2,1,0:T(8,128)(2,1)S(1)}, u32[]{:S(2)}, u32[]{:S(2)}) %collective-permute-start.56) | collective-permute-done | bytes 589856 | tf_op jit(solution)/shard_map/ppermute | solution.py:27
  166.3 5.3 %collective-permute-done.57 = bf16[2,24,3072]{2,1,0:T(8,128)(2,1)S(1)} collective-permute-done((bf16[2,24,3072]{2,1,0:T(8,128)(2,1)S(1)}, bf16[2,24,3072]{2,1,0:T(8,128)(2,1)S(1)}, u32[]{:S(2)}, u32[]{:S(2)}) %collective-permute-start.57) | collective-permute-done | bytes 294944 | tf_op jit(solution)/shard_map/ppermute | solution.py:27
  175.7 4.7 %collective-permute-done.59 = bf16[24,3072]{1,0:T(8,128)(2,1)S(1)} collective-permute-done((bf16[24,3072]{1,0:T(8,128)(2,1)S(1)}, bf16[24,3072]{1,0:T(8,128)(2,1)S(1)}, u32[]{:S(2)}, u32[]{:S(2)}) %collective-permute-start.59) | collective-permute-done | bytes 147488 | tf_op jit(solution)/shard_map/ppermute | solution.py:27
  180.4 4.1 collective-permute-done.58
  191.5 4.0 collective-permute-done.22
  197.0 5.3 %collective-permute-done.25 = bf16[24,3072]{1,0:T(8,128)(2,1)S(1)} collective-permute-done((bf16[24,3072]{1,0:T(8,128)(2,1)S(1)}, bf16[24,3072]{1,0:T(8,128)(2,1)S(1)}, u32[]{:S(2)}, u32[]{:S(2)}) %collective-permute-start.25) | collective-permute-done | bytes 147488 | tf_op jit(solution)/shard_map/ppermute | solution.py:27
  204.6 7.8 %collective-permute-done.27 = bf16[2,24,3072]{2,1,0:T(8,128)(2,1)S(1)} collective-permute-done((bf16[2,24,3072]{2,1,0:T(8,128)(2,1)S(1)}, bf16[2,24,3072]{2,1,0:T(8,128)(2,1)S(1)}, u32[]{:S(2)}, u32[]{:S(2)}) %collective-permute-start.27) | collective-permute-done | bytes 294944 | tf_op jit(solution)/shard_map/ppermute | solution.py:27
  214.7 7.9 %collective-permute-done.24.refs_1_ = bf16[2,2,24,3072]{3,2,1,0:T(8,128)(2,1)} collective-permute-done((bf16[2,2,24,3072]{3,2,1,0:T(8,128)(2,1)S(1)}, bf16[2,2,24,3072]{3,2,1,0:T(8,128)(2,1)}, u32[]{:S(2)}, u32[]{:S(2)}) %collective-permute-start.24) | collective-permute-done | bytes 589856 | tf_op jit(solution)/shard_map/ppermute | solution.py:27
  225.8 4.9 %assemble.5 = bf16[128,24,768]{2,1,0:T(8,128)(2,1)} custom-call(s32[4]{0:T(128)} %pad_add_fusion.pos_ref, bf16[2,2,24,3072]{3,2,1,0:T(8,128)(2,1)} %copy-done.11, bf16[2,2,24,3072]{3,2,1,0:T(8,128)(2,1)} %collective-permute-done.24.refs_1_, bf16[2,2,24,3072]{3,2,1,0:T(8,128)(2,1)} %copy-done.12, bf16[2,2,24,3072]{3,2,1,0:T(8,128)(2,1)} %collective-permute-done.28.refs_3_, ...), custom_call_target="tpu_custom_call" | custom-call | bytes 9437184 | tf_op jit(solution)/shard_map/assemble/pallas_call | solution.py:114
  230.7 8.8 %fusion.7 = bf16[480,3072]{1,0:T(8,128)(2,1)S(1)} fusion(f32[480,3072]{1,0:T(8,128)} %copy-done.61, bf16[480,768]{1,0:T(8,128)(2,1)} %bitcast.300, bf16[3072,768]{1,0:T(8,128)(2,1)} %bitcast.284), kind=kOutput, calls=%fused_computation.9 | convolution fusion | flops 2294415360 | bytes 14303232 | tf_op jit(solution)/shard_map/re,fe->rf/dot_general | solution.py:178
  243.5 7.6 %multiply_reduce_fusion.3 = (f32[480]{0:T(512)S(1)}, bf16[480,768]{1,0:T(8,128)(2,1)}, f32[480,768]{1,0:T(8,128)S(1)}) fusion(f32[480,768]{1,0:T(8,128)S(1)} %bitcast.293, f32[480,768]{1,0:T(8,128)S(1)} %copy-done.7, f32[480]{0:T(512)S(1)} %bitcast.329, f32[480]{0:T(512)S(1)} %multiply_multiply_fusion.8, f32[480]{0:T(512)S(1)} %fusion.101, ...), kind=kOutput, calls=%fused_computation.67 | convolution fusion | flops 2282249728 | bytes 18737664 | tf_op jit(solution)/shard_map/rf,fe->re/dot_general | solution.py:178
  252.7 3.5 reshape.387
  256.3 4.0 copy.142
  260.4 4.9 %multiply_reduce_fusion = (f32[3,12,160]{2,1,0:T(8,128)S(1)}, f32[3,12,160,160]{2,3,1,0:T(8,128)S(1)}) fusion(f32[3,12,160,160]{2,3,1,0:T(8,128)} %copy-done.5, f32[3,12,160]{2,1,0:T(8,128)S(1)} %copy-done.49, bf16[3,160,12,64]{1,3,2,0:T(8,128)(2,1)} %copy.142, bf16[3,160,1,12,64]{1,4,3,0,2:T(8,128)(2,1)} %copy.174), kind=kOutput, calls=%fused_computation.12 | convolution fusion | flops 120723840 | bytes 8893440 | tf_op jit(solution)/shard_map/sqhd,skhd->shqk/dot_general | solution.py:178
  265.2 4.6 %multiply_convert_fusion = bf16[3,12,160,160]{2,3,1,0:T(8,128)(2,1)S(1)} fusion(f32[3,12,160,160]{2,3,1,0:T(8,128)S(1)} %get-tuple-element.215, f32[3,12,160]{2,1,0:T(8,128)S(1)} %get-tuple-element.214, f32[3,12,160,160]{2,3,1,0:T(8,128)} %copy-done.5, f32[3,12,160]{2,1,0:T(8,128)S(1)} %copy-done.49), kind=kLoop, calls=%fused_computation.11 | loop fusion | flops 3686400 | bytes 9262080 | tf_op jit(solution)/shard_map/convert_element_type | solution.py:195
  276.7 4.0 reshape.370
  287.9 3.4 copy.149
  291.4 4.2 %reshape.372 = bf16[480,768]{0,1:T(8,128)(2,1)} reshape(bf16[3,160,12,64]{1,0,3,2:T(4,128)(2,1)} %copy.149) | data formatting | bytes 1474560 | tf_op jit(solution)/shard_map/reshape | solution.py:276
  298.5 6.2 %fusion.18 = (bf16[768]{0:T(1024)(128)(2,1)S(1)}, f32[480]{0:T(512)S(1)}, f32[480,768]{1,0:T(8,128)}) fusion(f32[480]{0:T(512)S(1)} %rsqrt.25, bf16[3,160,768]{2,1,0:T(8,128)(2,1)S(1)} %get-tuple-element.206, f32[768]{0:T(1024)S(1)} %convert_reduce_fusion.1, bf16[480,768]{1,0:T(8,128)(2,1)S(1)} %bitcast.277, ...), kind=kOutput, calls=%fused_computation.54 | convolution fusion | flops 1701640960 | bytes 8708352 | tf_op jit(solution)/shard_map/re,de->rd/dot_general | solution.py:178
  304.7 4.1 convolution_convert_fusion.2
  310.8 4.5 %convolution_convert_fusion.1 = bf16[768,3072]{1,0:T(8,128)(2,1)} fusion(bf16[480,3072]{1,0:T(8,128)(2,1)S(1)} %copy-done.63, f32[480,768]{1,0:T(8,128)S(1)} %copy-done.8, f32[768]{0:T(1024)S(1)} %convert_reduce_fusion, f32[480]{0:T(512)S(1)} %fusion.101), kind=kOutput, calls=%fused_computation.18 | convolution fusion | flops 2268389376 | bytes 9147264 | tf_op jit(solution)/shard_map/rd,rf->df/dot_general | solution.py:178
  316.9 5.1 %disassemble.3 = (bf16[2,2,2,24,3328]{4,3,2,1,0:T(8,128)(2,1)}, bf16[2,2,2,24,3328]{4,3,2,1,0:T(8,128)(2,1)}, bf16[2,2,2,24,3328]{4,3,2,1,0:T(8,128)(2,1)}, bf16[2,2,2,24,3328]{4,3,2,1,0:T(8,128)(2,1)}) custom-call(s32[4]{0:T(128)} %pad_add_fusion.pos_ref, bf16[32,24,2304]{2,1,0:T(8,128)(2,1)} %bitcast.288, bf16[32,24,768]{2,1,0:T(8,128)(2,1)} %bitcast.287, ...), custom_call_target="tpu_custom_call" | custom-call | bytes 10223616 | tf_op jit(solution)/shard_map/disassemble/pallas_call | solution.py:147
  322.5 4.9 %disassemble.4 = (bf16[2,2,2,24,3072]{4,3,2,1,0:T(8,128)(2,1)}, bf16[2,2,2,24,3072]{4,3,2,1,0:T(8,128)(2,1)}, bf16[2,2,2,24,3072]{4,3,2,1,0:T(8,128)(2,1)}, bf16[2,2,2,24,3072]{4,3,2,1,0:T(8,128)(2,1)}) custom-call(s32[4]{0:T(128)} %pad_add_fusion.pos_ref, bf16[32,24,3072]{2,1,0:T(8,128)(2,1)} %bitcast.283), custom_call_target="tpu_custom_call" | custom-call | bytes 9437184 | tf_op jit(solution)/shard_map/disassemble/pallas_call | solution.py:147
  329.9 7.9 %convert_select_fusion.1 = bf16[3,1280,768]{2,1,0:T(8,128)(2,1)} fusion(bf16[3,1280,768]{2,1,0:T(8,128)(2,1)} %param.28, pred[3,1280]{1,0:T(4,128)(4,1)S(1)} %fusion.14, bf16[3,160,768]{2,1,0:T(8,128)(2,1)S(1)} %bitcast.338, s32[3,160]{1,0:T(4,128)S(1)} %copy-done.44), kind=kOutput, calls=%fused_computation.13 | convolution fusion | flops 950231040 | bytes 12539520 | tf_op jit(solution)/shard_map/sct,scd->std/dot_general | solution.py:178
  337.8 4.9 %convert_select_fusion = bf16[3,1280,768]{2,1,0:T(8,128)(2,1)} fusion(bf16[3,1280,768]{2,1,0:T(8,128)(2,1)S(1)} %bitcast.282, pred[3,1280]{1,0:T(4,128)(4,1)S(1)} %fusion.14, bf16[3,160,768]{2,1,0:T(8,128)(2,1)S(1)} %bitcast.299, s32[3,160]{1,0:T(4,128)S(1)} %copy-done.44), kind=kOutput, calls=%fused_computation.10 | convolution fusion | flops 950231040 | bytes 12539520 | tf_op jit(solution)/shard_map/sct,scd->std/dot_general | solution.py:178
  351.5 7.9 %collective-permute-done.47 = bf16[2,2,24,3072]{3,2,1,0:T(8,128)(2,1)S(1)} collective-permute-done((bf16[2,2,24,3072]{3,2,1,0:T(8,128)(2,1)S(1)}, bf16[2,2,24,3072]{3,2,1,0:T(8,128)(2,1)S(1)}, u32[]{:S(2)}, u32[]{:S(2)}) %collective-permute-start.47) | collective-permute-done | bytes 589856 | tf_op jit(solution)/shard_map/ppermute | solution.py:27
  362.5 12.2 %collective-permute-done.34 = bf16[2,2,24,3328]{3,2,1,0:T(8,128)(2,1)S(1)} collective-permute-done((bf16[2,2,24,3328]{3,2,1,0:T(8,128)(2,1)S(1)}, bf16[2,2,24,3328]{3,2,1,0:T(8,128)(2,1)S(1)}, u32[]{:S(2)}, u32[]{:S(2)}) %collective-permute-start.34) | collective-permute-done | bytes 639008 | tf_op jit(solution)/shard_map/ppermute | solution.py:27
  377.4 3.6 collective-permute-done.48
  381.1 3.1 collective-permute-start.49
  386.9 3.1 collective-permute-start.40
  391.1 6.3 %collective-permute-done.49 = bf16[24,3072]{1,0:T(8,128)(2,1)S(1)} collective-permute-done((bf16[24,3072]{1,0:T(8,128)(2,1)S(1)}, bf16[24,3072]{1,0:T(8,128)(2,1)S(1)}, u32[]{:S(2)}, u32[]{:S(2)}) %collective-permute-start.49) | collective-permute-done | bytes 147488 | tf_op jit(solution)/shard_map/ppermute | solution.py:27
  399.0 7.5 %collective-permute-done.40 = bf16[24,3328]{1,0:T(8,128)(2,1)S(1)} collective-permute-done((bf16[24,3328]{1,0:T(8,128)(2,1)S(1)}, bf16[24,3328]{1,0:T(8,128)(2,1)S(1)}, u32[]{:S(2)}, u32[]{:S(2)}) %collective-permute-start.40) | collective-permute-done | bytes 159776 | tf_op jit(solution)/shard_map/ppermute | solution.py:27
  (386 shorter events, 139.2 us)
Async XLA Ops:
  3.3 17.1 %collective-permute-start = (bf16[24,2560]{1,0:T(8,128)(2,1)S(1)}, bf16[24,2560]{1,0:T(8,128)(2,1)S(1)}, u32[]{:S(2)}, u32[]{:S(2)}) collective-permute-start(bf16[24,2560]{1,0:T(8,128)(2,1)S(1)} %concatenate.42), channel_id=1, source_target_pairs={{0,2},{2,4},{4,6},{6,0},{1,3},{3,5},{5,7},{7,1},{8,10},{10,12},{12... | collective-permute-start | bytes 368648 | tf_op jit(solution)/shard_map/ppermute | solution.py:27
  6.4 14.3 %collective-permute-start.4 = (bf16[24,2560]{1,0:T(8,128)(2,1)S(1)}, bf16[24,2560]{1,0:T(8,128)(2,1)S(1)}, u32[]{:S(2)}, u32[]{:S(2)}) collective-permute-start(bf16[24,2560]{1,0:T(8,128)(2,1)S(1)} %concatenate.42), channel_id=1, source_target_pairs={{0,6},{2,0},{4,2},{6,4},{1,7},{3,1},{5,3},{7,5},{8,14},{10,8},{12,... | collective-permute-start | bytes 368648 | tf_op jit(solution)/shard_map/ppermute | solution.py:27
  8.5 15.2 %collective-permute-start.3 = (bf16[24,2560]{1,0:T(8,128)(2,1)S(1)}, bf16[24,2560]{1,0:T(8,128)(2,1)S(1)}, u32[]{:S(2)}, u32[]{:S(2)}) collective-permute-start(bf16[24,2560]{1,0:T(8,128)(2,1)S(1)} %concatenate.42), channel_id=1, source_target_pairs={{0,4},{2,6},{4,0},{6,2},{1,5},{3,7},{5,1},{7,3},{8,12},{10,14},{12... | collective-permute-start | bytes 368648 | tf_op jit(solution)/shard_map/ppermute | solution.py:27
  11.3 14.1 %collective-permute-start.11 = (bf16[24,3840]{1,0:T(8,128)(2,1)S(1)}, bf16[24,3840]{1,0:T(8,128)(2,1)S(1)}, u32[]{:S(2)}, u32[]{:S(2)}) collective-permute-start(bf16[24,3840]{1,0:T(8,128)(2,1)S(1)} %pad_maximum_fusion.13), channel_id=1, source_target_pairs={{0,2},{2,4},{4,6},{6,0},{1,3},{3,5},{5,7},{7,1},{8,10},{10,12},{12... | collective-permute-start | bytes 552968 | tf_op jit(solution)/shard_map/ppermute | solution.py:27
  12.9 14.1 %collective-permute-start.15 = (bf16[24,3840]{1,0:T(8,128)(2,1)S(1)}, bf16[24,3840]{1,0:T(8,128)(2,1)S(1)}, u32[]{:S(2)}, u32[]{:S(2)}) collective-permute-start(bf16[24,3840]{1,0:T(8,128)(2,1)S(1)} %pad_maximum_fusion.13), channel_id=1, source_target_pairs={{0,6},{2,0},{4,2},{6,4},{1,7},{3,1},{5,3},{7,5},{8,14},{10,8},{12,... | collective-permute-start | bytes 552968 | tf_op jit(solution)/shard_map/ppermute | solution.py:27
  20.4 15.1 %collective-permute-start.14 = (bf16[24,3840]{1,0:T(8,128)(2,1)S(1)}, bf16[24,3840]{1,0:T(8,128)(2,1)S(1)}, u32[]{:S(2)}, u32[]{:S(2)}) collective-permute-start(bf16[24,3840]{1,0:T(8,128)(2,1)S(1)} %pad_maximum_fusion.13), channel_id=1, source_target_pairs={{0,4},{2,6},{4,0},{6,2},{1,5},{3,7},{5,1},{7,3},{8,12},{10,14},{12... | collective-permute-start | bytes 552968 | tf_op jit(solution)/shard_map/ppermute | solution.py:27
  20.7 16.4 %collective-permute-start.1 = (bf16[2,24,2560]{2,1,0:T(8,128)(2,1)S(1)}, bf16[2,24,2560]{2,1,0:T(8,128)(2,1)S(1)}, u32[]{:S(2)}, u32[]{:S(2)}) collective-permute-start(bf16[2,24,2560]{2,1,0:T(8,128)(2,1)S(1)} %get-tuple-element.195), channel_id=1, source_target_pairs={{0,1},{1,0},{2,3},{3,2},{4,5},{5,4},{6,7},{7,6},{8,9},{9,8},{10,11... | collective-permute-start | bytes 737288 | tf_op jit(solution)/shard_map/ppermute | solution.py:27
  23.7 14.0 %collective-permute-start.5 = (bf16[2,24,2560]{2,1,0:T(8,128)(2,1)S(1)}, bf16[2,24,2560]{2,1,0:T(8,128)(2,1)S(1)}, u32[]{:S(2)}, u32[]{:S(2)}) collective-permute-start(bf16[2,24,2560]{2,1,0:T(8,128)(2,1)S(1)} %get-tuple-element.193), channel_id=1, source_target_pairs={{0,16},{16,0},{1,17},{17,1},{2,18},{18,2},{3,19},{19,3},{4,20},{20... | collective-permute-start | bytes 737288 | tf_op jit(solution)/shard_map/ppermute | solution.py:27
  25.4 13.9 %collective-permute-start.12 = (bf16[2,24,3840]{2,1,0:T(8,128)(2,1)S(1)}, bf16[2,24,3840]{2,1,0:T(8,128)(2,1)S(1)}, u32[]{:S(2)}, u32[]{:S(2)}) collective-permute-start(bf16[2,24,3840]{2,1,0:T(8,128)(2,1)S(1)} %get-tuple-element.177), channel_id=1, source_target_pairs={{0,1},{1,0},{2,3},{3,2},{4,5},{5,4},{6,7},{7,6},{8,9},{9,8},{10,11... | collective-permute-start | bytes 1105928 | tf_op jit(solution)/shard_map/ppermute | solution.py:27
  35.5 11.5 %collective-permute-start.16 = (bf16[2,24,3840]{2,1,0:T(8,128)(2,1)S(1)}, bf16[2,24,3840]{2,1,0:T(8,128)(2,1)S(1)}, u32[]{:S(2)}, u32[]{:S(2)}) collective-permute-start(bf16[2,24,3840]{2,1,0:T(8,128)(2,1)S(1)} %get-tuple-element.175), channel_id=1, source_target_pairs={{0,16},{16,0},{1,17},{17,1},{2,18},{18,2},{3,19},{19,3},{4,20},{20... | collective-permute-start | bytes 1105928 | tf_op jit(solution)/shard_map/ppermute | solution.py:27
  37.2 20.4 %collective-permute-start.2 = (bf16[2,2,24,2560]{3,2,1,0:T(8,128)(2,1)S(1)}, bf16[2,2,24,2560]{3,2,1,0:T(8,128)(2,1)S(1)}, u32[]{:S(2)}, u32[]{:S(2)}) collective-permute-start(bf16[2,2,24,2560]{3,2,1,0:T(8,128)(2,1)S(1)} %pad_maximum_fusion.4.refs_0_), channel_id=1, source_target_pairs={{0,16},{16,0},{1,17},{17,1},{2,18},{18,2},{3,19},{19,3},{4,20},{20... | collective-permute-start | bytes 1474568 | tf_op jit(solution)/shard_map/ppermute | solution.py:27
  37.7 20.3 %collective-permute-start.7 = (bf16[2,2,24,2560]{3,2,1,0:T(8,128)(2,1)S(1)}, bf16[2,2,24,2560]{3,2,1,0:T(8,128)(2,1)S(1)}, u32[]{:S(2)}, u32[]{:S(2)}) collective-permute-start(bf16[2,2,24,2560]{3,2,1,0:T(8,128)(2,1)S(1)} %pad_maximum_fusion.4.refs_0_), channel_id=1, source_target_pairs={{0,8},{8,0},{1,9},{9,1},{2,10},{10,2},{3,11},{11,3},{4,12},{12,4},... | collective-permute-start | bytes 1474568 | tf_op jit(solution)/shard_map/ppermute | solution.py:27
  37.8 19.8 %collective-permute-start.6 = (bf16[2,2,24,2560]{3,2,1,0:T(8,128)(2,1)S(1)}, bf16[2,2,24,2560]{3,2,1,0:T(8,128)(2,1)S(1)}, u32[]{:S(2)}, u32[]{:S(2)}) collective-permute-start(bf16[2,2,24,2560]{3,2,1,0:T(8,128)(2,1)S(1)} %pad_maximum_fusion.5.refs_2_), channel_id=1, source_target_pairs={{0,1},{1,0},{2,3},{3,2},{4,5},{5,4},{6,7},{7,6},{8,9},{9,8},{10,11... | collective-permute-start | bytes 1474568 | tf_op jit(solution)/shard_map/ppermute | solution.py:27
  40.3 32.2 %collective-permute-start.13 = (bf16[2,2,24,3840]{3,2,1,0:T(8,128)(2,1)}, bf16[2,2,24,3840]{3,2,1,0:T(8,128)(2,1)}, u32[]{:S(2)}, u32[]{:S(2)}) collective-permute-start(bf16[2,2,24,3840]{3,2,1,0:T(8,128)(2,1)} %pad_maximum_fusion.refs_0_), channel_id=1, source_target_pairs={{0,16},{16,0},{1,17},{17,1},{2,18},{18,2},{3,19},{19,3},{4,20},{20... | collective-permute-start | bytes 2211848 | tf_op jit(solution)/shard_map/ppermute | solution.py:27
  48.0 24.6 %collective-permute-start.17 = (bf16[2,2,24,3840]{3,2,1,0:T(8,128)(2,1)}, bf16[2,2,24,3840]{3,2,1,0:T(8,128)(2,1)}, u32[]{:S(2)}, u32[]{:S(2)}) collective-permute-start(bf16[2,2,24,3840]{3,2,1,0:T(8,128)(2,1)} %pad_maximum_fusion.1.refs_2_), channel_id=1, source_target_pairs={{0,1},{1,0},{2,3},{3,2},{4,5},{5,4},{6,7},{7,6},{8,9},{9,8},{10,11... | collective-permute-start | bytes 2211848 | tf_op jit(solution)/shard_map/ppermute | solution.py:27
  57.6 15.5 %collective-permute-start.8 = (bf16[2,2,24,2560]{3,2,1,0:T(8,128)(2,1)S(1)}, bf16[2,2,24,2560]{3,2,1,0:T(8,128)(2,1)S(1)}, u32[]{:S(2)}, u32[]{:S(2)}) collective-permute-start(bf16[2,2,24,2560]{3,2,1,0:T(8,128)(2,1)S(1)} %collective-permute-done.2.refs_1_), channel_id=1, source_target_pairs={{0,8},{8,0},{1,9},{9,1},{2,10},{10,2},{3,11},{11,3},{4,12},{12,4},... | collective-permute-start | bytes 1474568 | tf_op jit(solution)/shard_map/ppermute | solution.py:27
  58.1 15.8 %collective-permute-start.10 = (bf16[2,2,24,2560]{3,2,1,0:T(8,128)(2,1)S(1)}, bf16[2,2,24,2560]{3,2,1,0:T(8,128)(2,1)}, u32[]{:S(2)}, u32[]{:S(2)}) collective-permute-start(bf16[2,2,24,2560]{3,2,1,0:T(8,128)(2,1)S(1)} %collective-permute-done.6.refs_3_), channel_id=1, source_target_pairs={{0,8},{8,0},{1,9},{9,1},{2,10},{10,2},{3,11},{11,3},{4,12},{12,4},... | collective-permute-start | bytes 1474568 | tf_op jit(solution)/shard_map/ppermute | solution.py:27
  59.4 60.9 %collective-permute-start.18 = (bf16[2,2,24,3840]{3,2,1,0:T(8,128)(2,1)}, bf16[2,2,24,3840]{3,2,1,0:T(8,128)(2,1)}, u32[]{:S(2)}, u32[]{:S(2)}) collective-permute-start(bf16[2,2,24,3840]{3,2,1,0:T(8,128)(2,1)} %pad_maximum_fusion.refs_0_), channel_id=1, source_target_pairs={{0,8},{8,0},{1,9},{9,1},{2,10},{10,2},{3,11},{11,3},{4,12},{12,4},... | collective-permute-start | bytes 2211848 | tf_op jit(solution)/shard_map/ppermute | solution.py:27
  72.5 47.8 %collective-permute-start.20 = (bf16[2,2,24,3840]{3,2,1,0:T(8,128)(2,1)}, bf16[2,2,24,3840]{3,2,1,0:T(8,128)(2,1)}, u32[]{:S(2)}, u32[]{:S(2)}) collective-permute-start(bf16[2,2,24,3840]{3,2,1,0:T(8,128)(2,1)} %pad_maximum_fusion.1.refs_2_), channel_id=1, source_target_pairs={{0,8},{8,0},{1,9},{9,1},{2,10},{10,2},{3,11},{11,3},{4,12},{12,4},... | collective-permute-start | bytes 2211848 | tf_op jit(solution)/shard_map/ppermute | solution.py:27
  72.5 47.8 %collective-permute-start.19 = (bf16[2,2,24,3840]{3,2,1,0:T(8,128)(2,1)}, bf16[2,2,24,3840]{3,2,1,0:T(8,128)(2,1)}, u32[]{:S(2)}, u32[]{:S(2)}) collective-permute-start(bf16[2,2,24,3840]{3,2,1,0:T(8,128)(2,1)} %collective-permute-done.13.refs_1_), channel_id=1, source_target_pairs={{0,8},{8,0},{1,9},{9,1},{2,10},{10,2},{3,11},{11,3},{4,12},{12,4},... | collective-permute-start | bytes 2211848 | tf_op jit(solution)/shard_map/ppermute | solution.py:27
  73.8 46.5 %collective-permute-start.21 = (bf16[2,2,24,3840]{3,2,1,0:T(8,128)(2,1)}, bf16[2,2,24,3840]{3,2,1,0:T(8,128)(2,1)}, u32[]{:S(2)}, u32[]{:S(2)}) collective-permute-start(bf16[2,2,24,3840]{3,2,1,0:T(8,128)(2,1)} %collective-permute-done.17.refs_3_), channel_id=1, source_target_pairs={{0,8},{8,0},{1,9},{9,1},{2,10},{10,2},{3,11},{11,3},{4,12},{12,4},... | collective-permute-start | bytes 2211848 | tf_op jit(solution)/shard_map/ppermute | solution.py:27
  147.2 15.7 %collective-permute-start.56 = (bf16[2,2,24,3072]{3,2,1,0:T(8,128)(2,1)S(1)}, bf16[2,2,24,3072]{3,2,1,0:T(8,128)(2,1)S(1)}, u32[]{:S(2)}, u32[]{:S(2)}) collective-permute-start(bf16[2,2,24,3072]{3,2,1,0:T(8,128)(2,1)S(1)} %fusion.69), channel_id=1, source_target_pairs={{0,16},{16,0},{1,17},{17,1},{2,18},{18,2},{3,19},{19,3},{4,20},{20... | collective-permute-start | bytes 1769480 | tf_op jit(solution)/shard_map/ppermute | solution.py:27
  149.1 15.4 %collective-permute-start.52 = (bf16[2,2,24,3072]{3,2,1,0:T(8,128)(2,1)S(1)}, bf16[2,2,24,3072]{3,2,1,0:T(8,128)(2,1)S(1)}, u32[]{:S(2)}, u32[]{:S(2)}) collective-permute-start(bf16[2,2,24,3072]{3,2,1,0:T(8,128)(2,1)S(1)} %fusion.68), channel_id=1, source_target_pairs={{0,1},{1,0},{2,3},{3,2},{4,5},{5,4},{6,7},{7,6},{8,9},{9,8},{10,11... | collective-permute-start | bytes 1769480 | tf_op jit(solution)/shard_map/ppermute | solution.py:27
  171.8 12.7 %collective-permute-start.58 = (bf16[24,3072]{1,0:T(8,128)(2,1)S(1)}, bf16[24,3072]{1,0:T(8,128)(2,1)S(1)}, u32[]{:S(2)}, u32[]{:S(2)}) collective-permute-start(bf16[24,3072]{1,0:T(8,128)(2,1)S(1)} %get-tuple-element.184), channel_id=1, source_target_pairs={{0,4},{2,6},{4,0},{6,2},{1,5},{3,7},{5,1},{7,3},{8,12},{10,14},{12... | collective-permute-start | bytes 442376 | tf_op jit(solution)/shard_map/ppermute | solution.py:27
  173.7 10.7 %collective-permute-start.54 = (bf16[24,3072]{1,0:T(8,128)(2,1)S(1)}, bf16[24,3072]{1,0:T(8,128)(2,1)S(1)}, u32[]{:S(2)}, u32[]{:S(2)}) collective-permute-start(bf16[24,3072]{1,0:T(8,128)(2,1)S(1)} %fusion.98), channel_id=1, source_target_pairs={{0,6},{2,0},{4,2},{6,4},{1,7},{3,1},{5,3},{7,5},{8,14},{10,8},{12,... | collective-permute-start | bytes 442376 | tf_op jit(solution)/shard_map/ppermute | solution.py:27
  190.9 11.3 %collective-permute-start.25 = (bf16[24,3072]{1,0:T(8,128)(2,1)S(1)}, bf16[24,3072]{1,0:T(8,128)(2,1)S(1)}, u32[]{:S(2)}, u32[]{:S(2)}) collective-permute-start(bf16[24,3072]{1,0:T(8,128)(2,1)S(1)} %bitcast.320), channel_id=1, source_target_pairs={{0,4},{2,6},{4,0},{6,2},{1,5},{3,7},{5,1},{7,3},{8,12},{10,14},{12... | collective-permute-start | bytes 442376 | tf_op jit(solution)/shard_map/ppermute | solution.py:27
  202.3 10.0 %collective-permute-start.27 = (bf16[2,24,3072]{2,1,0:T(8,128)(2,1)S(1)}, bf16[2,24,3072]{2,1,0:T(8,128)(2,1)S(1)}, u32[]{:S(2)}, u32[]{:S(2)}) collective-permute-start(bf16[2,24,3072]{2,1,0:T(8,128)(2,1)S(1)} %get-tuple-element.189), channel_id=1, source_target_pairs={{0,16},{16,0},{1,17},{17,1},{2,18},{18,2},{3,19},{19,3},{4,20},{20... | collective-permute-start | bytes 884744 | tf_op jit(solution)/shard_map/ppermute | solution.py:27
  203.9 18.7 %collective-permute-start.24 = (bf16[2,2,24,3072]{3,2,1,0:T(8,128)(2,1)S(1)}, bf16[2,2,24,3072]{3,2,1,0:T(8,128)(2,1)}, u32[]{:S(2)}, u32[]{:S(2)}) collective-permute-start(bf16[2,2,24,3072]{3,2,1,0:T(8,128)(2,1)S(1)} %pad_maximum_fusion.2.refs_0_), channel_id=1, source_target_pairs={{0,16},{16,0},{1,17},{17,1},{2,18},{18,2},{3,19},{19,3},{4,20},{20... | collective-permute-start | bytes 1769480 | tf_op jit(solution)/shard_map/ppermute | solution.py:27
  212.4 10.5 %collective-permute-start.28 = (bf16[2,2,24,3072]{3,2,1,0:T(8,128)(2,1)S(1)}, bf16[2,2,24,3072]{3,2,1,0:T(8,128)(2,1)}, u32[]{:S(2)}, u32[]{:S(2)}) collective-permute-start(bf16[2,2,24,3072]{3,2,1,0:T(8,128)(2,1)S(1)} %pad_maximum_fusion.3.refs_2_), channel_id=1, source_target_pairs={{0,1},{1,0},{2,3},{3,2},{4,5},{5,4},{6,7},{7,6},{8,9},{9,8},{10,11... | collective-permute-start | bytes 1769480 | tf_op jit(solution)/shard_map/ppermute | solution.py:27
  214.2 9.6 %collective-permute-start.29 = (bf16[2,2,24,3072]{3,2,1,0:T(8,128)(2,1)S(1)}, bf16[2,2,24,3072]{3,2,1,0:T(8,128)(2,1)}, u32[]{:S(2)}, u32[]{:S(2)}) collective-permute-start(bf16[2,2,24,3072]{3,2,1,0:T(8,128)(2,1)S(1)} %pad_maximum_fusion.2.refs_0_), channel_id=1, source_target_pairs={{0,8},{8,0},{1,9},{9,1},{2,10},{10,2},{3,11},{11,3},{4,12},{12,4},... | collective-permute-start | bytes 1769480 | tf_op jit(solution)/shard_map/ppermute | solution.py:27
  214.2 9.6 %collective-permute-start.31 = (bf16[2,2,24,3072]{3,2,1,0:T(8,128)(2,1)S(1)}, bf16[2,2,24,3072]{3,2,1,0:T(8,128)(2,1)}, u32[]{:S(2)}, u32[]{:S(2)}) collective-permute-start(bf16[2,2,24,3072]{3,2,1,0:T(8,128)(2,1)S(1)} %pad_maximum_fusion.3.refs_2_), channel_id=1, source_target_pairs={{0,8},{8,0},{1,9},{9,1},{2,10},{10,2},{3,11},{11,3},{4,12},{12,4},... | collective-permute-start | bytes 1769480 | tf_op jit(solution)/shard_map/ppermute | solution.py:27
  322.0 24.3 %collective-permute-start.33 = (bf16[2,2,2,24,3328]{4,3,2,1,0:T(8,128)(2,1)}, bf16[2,2,2,24,3328]{4,3,2,1,0:T(8,128)(2,1)}, u32[]{:S(2)}, u32[]{:S(2)}) collective-permute-start(bf16[2,2,2,24,3328]{4,3,2,1,0:T(8,128)(2,1)} %get-tuple-element.47), channel_id=1, source_target_pairs={{0,8},{8,0},{1,9},{9,1},{2,10},{10,2},{3,11},{11,3},{4,12},{12,4},... | collective-permute-start | bytes 3833864 | tf_op jit(solution)/shard_map/ppermute | solution.py:27
  322.2 26.8 %collective-permute-start.37 = (bf16[2,2,2,24,3328]{4,3,2,1,0:T(8,128)(2,1)}, bf16[2,2,2,24,3328]{4,3,2,1,0:T(8,128)(2,1)}, u32[]{:S(2)}, u32[]{:S(2)}) collective-permute-start(bf16[2,2,2,24,3328]{4,3,2,1,0:T(8,128)(2,1)} %get-tuple-element.49), channel_id=1, source_target_pairs={{0,8},{8,0},{1,9},{9,1},{2,10},{10,2},{3,11},{11,3},{4,12},{12,4},... | collective-permute-start | bytes 3833864 | tf_op jit(solution)/shard_map/ppermute | solution.py:27
  327.5 15.2 %collective-permute-start.46 = (bf16[2,2,2,24,3072]{4,3,2,1,0:T(8,128)(2,1)}, bf16[2,2,2,24,3072]{4,3,2,1,0:T(8,128)(2,1)S(1)}, u32[]{:S(2)}, u32[]{:S(2)}) collective-permute-start(bf16[2,2,2,24,3072]{4,3,2,1,0:T(8,128)(2,1)} %get-tuple-element.53), channel_id=1, source_target_pairs={{0,8},{8,0},{1,9},{9,1},{2,10},{10,2},{3,11},{11,3},{4,12},{12,4},... | collective-permute-start | bytes 3538952 | tf_op jit(solution)/shard_map/ppermute | solution.py:27
  327.6 16.7 %collective-permute-start.42 = (bf16[2,2,2,24,3072]{4,3,2,1,0:T(8,128)(2,1)}, bf16[2,2,2,24,3072]{4,3,2,1,0:T(8,128)(2,1)S(1)}, u32[]{:S(2)}, u32[]{:S(2)}) collective-permute-start(bf16[2,2,2,24,3072]{4,3,2,1,0:T(8,128)(2,1)} %get-tuple-element.51), channel_id=1, source_target_pairs={{0,8},{8,0},{1,9},{9,1},{2,10},{10,2},{3,11},{11,3},{4,12},{12,4},... | collective-permute-start | bytes 3538952 | tf_op jit(solution)/shard_map/ppermute | solution.py:27
  343.2 16.2 %collective-permute-start.47 = (bf16[2,2,24,3072]{3,2,1,0:T(8,128)(2,1)S(1)}, bf16[2,2,24,3072]{3,2,1,0:T(8,128)(2,1)S(1)}, u32[]{:S(2)}, u32[]{:S(2)}) collective-permute-start(bf16[2,2,24,3072]{3,2,1,0:T(8,128)(2,1)S(1)} %fusion.67), channel_id=1, source_target_pairs={{0,16},{16,0},{1,17},{17,1},{2,18},{18,2},{3,19},{19,3},{4,20},{20... | collective-permute-start | bytes 1769480 | tf_op jit(solution)/shard_map/ppermute | solution.py:27
  344.7 16.3 %collective-permute-start.43 = (bf16[2,2,24,3072]{3,2,1,0:T(8,128)(2,1)S(1)}, bf16[2,2,24,3072]{3,2,1,0:T(8,128)(2,1)S(1)}, u32[]{:S(2)}, u32[]{:S(2)}) collective-permute-start(bf16[2,2,24,3072]{3,2,1,0:T(8,128)(2,1)S(1)} %fusion.66), channel_id=1, source_target_pairs={{0,1},{1,0},{2,3},{3,2},{4,5},{5,4},{6,7},{7,6},{8,9},{9,8},{10,11... | collective-permute-start | bytes 1769480 | tf_op jit(solution)/shard_map/ppermute | solution.py:27
  348.1 26.6 %collective-permute-start.34 = (bf16[2,2,24,3328]{3,2,1,0:T(8,128)(2,1)S(1)}, bf16[2,2,24,3328]{3,2,1,0:T(8,128)(2,1)S(1)}, u32[]{:S(2)}, u32[]{:S(2)}) collective-permute-start(bf16[2,2,24,3328]{3,2,1,0:T(8,128)(2,1)S(1)} %fusion.61), channel_id=1, source_target_pairs={{0,1},{1,0},{2,3},{3,2},{4,5},{5,4},{6,7},{7,6},{8,9},{9,8},{10,11... | collective-permute-start | bytes 1916936 | tf_op jit(solution)/shard_map/ppermute | solution.py:27
  350.6 25.2 %collective-permute-start.38 = (bf16[2,2,24,3328]{3,2,1,0:T(8,128)(2,1)S(1)}, bf16[2,2,24,3328]{3,2,1,0:T(8,128)(2,1)S(1)}, u32[]{:S(2)}, u32[]{:S(2)}) collective-permute-start(bf16[2,2,24,3328]{3,2,1,0:T(8,128)(2,1)S(1)} %fusion.62), channel_id=1, source_target_pairs={{0,16},{16,0},{1,17},{17,1},{2,18},{18,2},{3,19},{19,3},{4,20},{20... | collective-permute-start | bytes 1916936 | tf_op jit(solution)/shard_map/ppermute | solution.py:27
  359.6 21.4 %collective-permute-start.48 = (bf16[2,24,3072]{2,1,0:T(8,128)(2,1)S(1)}, bf16[2,24,3072]{2,1,0:T(8,128)(2,1)S(1)}, u32[]{:S(2)}, u32[]{:S(2)}) collective-permute-start(bf16[2,24,3072]{2,1,0:T(8,128)(2,1)S(1)} %fusion.84), channel_id=1, source_target_pairs={{0,1},{1,0},{2,3},{3,2},{4,5},{5,4},{6,7},{7,6},{8,9},{9,8},{10,11... | collective-permute-start | bytes 884744 | tf_op jit(solution)/shard_map/ppermute | solution.py:27
  361.2 23.1 %collective-permute-start.44 = (bf16[2,24,3072]{2,1,0:T(8,128)(2,1)S(1)}, bf16[2,24,3072]{2,1,0:T(8,128)(2,1)S(1)}, u32[]{:S(2)}, u32[]{:S(2)}) collective-permute-start(bf16[2,24,3072]{2,1,0:T(8,128)(2,1)S(1)} %fusion.83), channel_id=1, source_target_pairs={{0,16},{16,0},{1,17},{17,1},{2,18},{18,2},{3,19},{19,3},{4,20},{20... | collective-permute-start | bytes 884744 | tf_op jit(solution)/shard_map/ppermute | solution.py:27
  374.8 12.1 %collective-permute-start.35 = (bf16[2,24,3328]{2,1,0:T(8,128)(2,1)S(1)}, bf16[2,24,3328]{2,1,0:T(8,128)(2,1)S(1)}, u32[]{:S(2)}, u32[]{:S(2)}) collective-permute-start(bf16[2,24,3328]{2,1,0:T(8,128)(2,1)S(1)} %fusion.76), channel_id=1, source_target_pairs={{0,16},{16,0},{1,17},{17,1},{2,18},{18,2},{3,19},{19,3},{4,20},{20... | collective-permute-start | bytes 958472 | tf_op jit(solution)/shard_map/ppermute | solution.py:27
  376.0 10.7 %collective-permute-start.39 = (bf16[2,24,3328]{2,1,0:T(8,128)(2,1)S(1)}, bf16[2,24,3328]{2,1,0:T(8,128)(2,1)S(1)}, u32[]{:S(2)}, u32[]{:S(2)}) collective-permute-start(bf16[2,24,3328]{2,1,0:T(8,128)(2,1)S(1)} %fusion.77), channel_id=1, source_target_pairs={{0,1},{1,0},{2,3},{3,2},{4,5},{5,4},{6,7},{7,6},{8,9},{9,8},{10,11... | collective-permute-start | bytes 958472 | tf_op jit(solution)/shard_map/ppermute | solution.py:27
  381.1 16.3 %collective-permute-start.49 = (bf16[24,3072]{1,0:T(8,128)(2,1)S(1)}, bf16[24,3072]{1,0:T(8,128)(2,1)S(1)}, u32[]{:S(2)}, u32[]{:S(2)}) collective-permute-start(bf16[24,3072]{1,0:T(8,128)(2,1)S(1)} %get-tuple-element.186), channel_id=1, source_target_pairs={{0,4},{2,6},{4,0},{6,2},{1,5},{3,7},{5,1},{7,3},{8,12},{10,14},{12... | collective-permute-start | bytes 442376 | tf_op jit(solution)/shard_map/ppermute | solution.py:27
  384.4 13.1 %collective-permute-start.45 = (bf16[24,3072]{1,0:T(8,128)(2,1)S(1)}, bf16[24,3072]{1,0:T(8,128)(2,1)S(1)}, u32[]{:S(2)}, u32[]{:S(2)}) collective-permute-start(bf16[24,3072]{1,0:T(8,128)(2,1)S(1)} %fusion.97), channel_id=1, source_target_pairs={{0,6},{2,0},{4,2},{6,4},{1,7},{3,1},{5,3},{7,5},{8,14},{10,8},{12,... | collective-permute-start | bytes 442376 | tf_op jit(solution)/shard_map/ppermute | solution.py:27
  386.8 12.2 %collective-permute-start.41 = (bf16[24,3328]{1,0:T(8,128)(2,1)S(1)}, bf16[24,3328]{1,0:T(8,128)(2,1)S(1)}, u32[]{:S(2)}, u32[]{:S(2)}) collective-permute-start(bf16[24,3328]{1,0:T(8,128)(2,1)S(1)} %get-tuple-element.182), channel_id=1, source_target_pairs={{0,2},{2,4},{4,6},{6,0},{1,3},{3,5},{5,7},{7,1},{8,10},{10,12},{12... | collective-permute-start | bytes 479240 | tf_op jit(solution)/shard_map/ppermute | solution.py:27
  386.9 19.6 %collective-permute-start.40 = (bf16[24,3328]{1,0:T(8,128)(2,1)S(1)}, bf16[24,3328]{1,0:T(8,128)(2,1)S(1)}, u32[]{:S(2)}, u32[]{:S(2)}) collective-permute-start(bf16[24,3328]{1,0:T(8,128)(2,1)S(1)} %get-tuple-element.181), channel_id=1, source_target_pairs={{0,4},{2,6},{4,0},{6,2},{1,5},{3,7},{5,1},{7,3},{8,12},{10,14},{12... | collective-permute-start | bytes 479240 | tf_op jit(solution)/shard_map/ppermute | solution.py:27
  390.3 16.3 %collective-permute-start.36 = (bf16[24,3328]{1,0:T(8,128)(2,1)S(1)}, bf16[24,3328]{1,0:T(8,128)(2,1)S(1)}, u32[]{:S(2)}, u32[]{:S(2)}) collective-permute-start(bf16[24,3328]{1,0:T(8,128)(2,1)S(1)} %fusion.96), channel_id=1, source_target_pairs={{0,6},{2,0},{4,2},{6,4},{1,7},{3,1},{5,3},{7,5},{8,14},{10,8},{12,... | collective-permute-start | bytes 479240 | tf_op jit(solution)/shard_map/ppermute | solution.py:27
  (82 other events, 912.4 us)

commit v3 on v2

v3 whole, which is shorter than its diff:
```python
import functools

import jax
import jax.numpy as jnp
from jax import lax
from jax.experimental import pallas as pl
from jax.experimental.pallas import tpu as pltpu
from jax.sharding import Mesh, PartitionSpec as P

HEADS = 12
SMALL = 256

norm_eps = 1e-06
learn_rates = (0.03, 0.1, 0.03, 0.02, 0.03, 0.2)
beta_first = 0.5
beta_second = 0.5
adam_eps = 1e-08
decay_rate = 0.1
average_rate = 0.7
exact_mode = lax.Precision.HIGHEST
f32 = jnp.float32
bf16 = jnp.bfloat16


def shifted(value, axis, sizes, step):
    n = sizes[axis]
    return lax.ppermute(value, axis, [(i, (i + step) % n) for i in range(n)])


def after(value, *others):
    return lax.optimization_barrier((value, others))[0]


def gather_axis(value, axis, sizes):
    return [value] + [shifted(value, axis, sizes, k) for k in range(1, sizes[axis])]


def gather_first(block, sizes):
    along = gather_axis(block, "a", sizes)
    half = len(along) // 2
    return jnp.stack(along[:half]), jnp.stack(along[half:])


def gather_second(halves, sizes):
    first, second = halves
    return jnp.stack(gather_axis(first, "b", sizes)), jnp.stack(gather_axis(second, "y", sizes))


def gather_third(halves, sizes):
    first, second = halves
    return gather_axis(first, "y", sizes) + gather_axis(second, "b", sizes)


def gather_last(here, sizes):
    return here, [shifted(v, "c", sizes, 1) for v in here]


def join_cores(mine, theirs, sizes):
    split = lambda v: v.reshape((sizes["y"], 1, -1) + v.shape[1:])
    mine, theirs = split(mine), split(theirs)
    core = lax.axis_index("c")
    low_core = jnp.where(core == 0, mine, theirs)
    high_core = jnp.where(core == 0, theirs, mine)
    return jnp.concatenate([low_core, high_core], axis=1).reshape((-1,) + mine.shape[3:])


def take(value, index, axis):
    return lax.dynamic_index_in_dim(value, index, axis, keepdims=False)


def parts_of(value, axis, at, sizes):
    n, me = sizes[axis], lax.axis_index(axis)
    return take(value, me, at), [take(value, lax.rem(me + k, n), at).astype(bf16) for k in range(1, n)]


def send_parts(parts, axis, sizes):
    return [shifted(part, axis, sizes, k + 1) for k, part in enumerate(parts)]


def add_up(own, came):
    for part in came:
        own = own + part.astype(f32)
    return own


def sum_start(grad, sizes):
    core = lax.axis_index("c")
    grad = grad.reshape((sizes["y"], 2, sizes["a"], sizes["b"]) + grad.shape[1:])
    return take(grad, core, 1), take(grad, 1 - core, 1)


def sum_first(own, came, sizes):
    total = own.astype(f32) + came.astype(f32)
    half = total.shape[-1] // 2
    return parts_of(total[..., :half], "b", 2, sizes), parts_of(total[..., half:], "y", 0, sizes)


def sum_second(owns, cames, sizes):
    first, second = add_up(owns[0], cames[0]), add_up(owns[1], cames[1])
    return parts_of(first, "y", 0, sizes), parts_of(second, "b", 1, sizes)


def sum_third(owns, cames, sizes):
    first, second = add_up(owns[0], cames[0]), add_up(owns[1], cames[1])
    return parts_of(jnp.concatenate([first, second], axis=-1), "a", 0, sizes)


def places(sizes):
    half = sizes["a"] // 2
    out = []
    for kc in range(2):
        for ky in range(sizes["y"]):
            for kb in range(sizes["b"]):
                for ka in range(sizes["a"]):
                    part = 0 if ka < half else 1
                    out.append((kc, part, ky, kb, ka % half, (ky, kc, ka, kb)))
    return out


def owner(pos_ref, steps, sizes):
    ky, kc, ka, kb = steps
    y = lax.rem(pos_ref[0] + (sizes["y"] - ky), sizes["y"])
    c = lax.rem(pos_ref[1] + (2 - kc), 2)
    a = lax.rem(pos_ref[2] + (sizes["a"] - ka), sizes["a"])
    b = lax.rem(pos_ref[3] + (sizes["b"] - kb), sizes["b"])
    return ((y * 2 + c) * sizes["a"] + a) * sizes["b"] + b


VMEM = pltpu.CompilerParams(vmem_limit_bytes=60 * 1024 * 1024)


def source(ins, block, sizes):
    kc, part, ky, kb, ka, _ = block
    base = kc * (sizes["y"] + sizes["b"])
    return ins[base + ky][kb, ka] if part == 0 else ins[base + sizes["y"] + kb][ky, ka]


def assemble(here, there, pos, sizes, cuts, fold=1):
    rows = here[0].shape[-2]
    devices = 2 * sizes["y"] * sizes["b"] * sizes["a"]
    sources = here + there
    blocks = places(sizes)

    def kernel(pos_ref, *refs):
        ins, outs = refs[: len(sources)], refs[len(sources) :]
        for block in blocks:
            where = owner(pos_ref, block[-1], sizes)
            value = source(ins, block, sizes)
            for i, (start, width) in enumerate(cuts):
                if fold == 1:
                    outs[i][where] = value[:, start : start + width]
                else:
                    outs[0][where * fold + i] = value[:, start : start + width]

    shapes = [jax.ShapeDtypeStruct((devices, rows, width), bf16) for _, width in cuts]
    if fold > 1:
        shapes = [jax.ShapeDtypeStruct((devices * fold, rows, cuts[0][1]), bf16)]
    vmem = pl.BlockSpec(memory_space=pltpu.VMEM)
    return pl.pallas_call(
        kernel,
        out_shape=shapes,
        in_specs=[pl.BlockSpec(memory_space=pltpu.SMEM)] + [vmem] * len(sources),
        out_specs=[vmem] * len(shapes),
        compiler_params=VMEM,
        cost_estimate=pl.CostEstimate(flops=0, transcendentals=0, bytes_accessed=2 * devices * rows * sum(w for _, w in cuts) * 2),
        name="assemble",
    )(pos, *sources)


def norm_scale(values, gain):
    return values * lax.rsqrt(jnp.mean(values * values, axis=-1, keepdims=True) + norm_eps) * gain


def gelu_tanh(values):
    return jax.nn.gelu(values, approximate=True)


def adamw(state, grad, decay, rate):
    weight, mean, square, average = state
    mean_next = beta_first * mean + (1.0 - beta_first) * grad
    square_next = beta_second * square + (1.0 - beta_second) * grad * grad
    update = mean_next / (jnp.sqrt(square_next) + adam_eps)
    weight_next = weight - rate * (update + decay * weight)
    average_next = average_rate * average + (1.0 - average_rate) * weight_next
    return [weight_next, mean_next, square_next, average_next]


def dot(a, b, spec):
    return jnp.einsum(spec, a, b, preferred_element_type=f32)


NT = (((1,), (1,)), ((), ()))
TN = (((0,), (0,)), ((), ()))
NN = (((1,), (0,)), ((), ()))


def mm(a, b, dims):
    return lax.dot_general(a, b, dims, preferred_element_type=f32)


def softmax_of(q2, k2, own, allowed, scale):
    logits = mm(jnp.where(own, q2, 0.0).astype(bf16), k2, NT) * scale
    logits = jnp.where(allowed, logits, -1e30)
    exponent = jnp.exp(logits - jnp.max(logits, axis=-1, keepdims=True))
    return exponent / jnp.sum(exponent, axis=-1, keepdims=True)


def mask_of(col_ref, row_ref, n):
    query = lax.broadcasted_iota(jnp.int32, (n, n), 0)
    key = lax.broadcasted_iota(jnp.int32, (n, n), 1)
    return (col_ref[0] == row_ref[0]) & (key <= query)


def attend_kernel(scale, col_ref, row_ref, qkv_ref, out_ref):
    n, width = out_ref.shape
    allowed = mask_of(col_ref, row_ref, n)
    lane = lax.broadcasted_iota(jnp.int32, (n, 128), 1)
    owns = (lane < 64, lane >= 64)
    for p in range(width // 128):
        q2, k2, v2 = (qkv_ref[:, i * width + p * 128 : i * width + (p + 1) * 128] for i in range(3))
        total = jnp.zeros((n, 128), f32)
        for own in owns:
            probs = softmax_of(q2, k2, own, allowed, scale).astype(bf16)
            total += mm(probs, jnp.where(own, v2, 0.0).astype(bf16), NN)
        out_ref[:, p * 128 : (p + 1) * 128] = total.astype(bf16)


def attend_back_kernel(scale, col_ref, row_ref, qkv_ref, grad_ref, out_ref):
    n, width = grad_ref.shape
    allowed = mask_of(col_ref, row_ref, n)
    lane = lax.broadcasted_iota(jnp.int32, (n, 128), 1)
    owns = (lane < 64, lane >= 64)
    for p in range(width // 128):
        q2, k2, v2 = (qkv_ref[:, i * width + p * 128 : i * width + (p + 1) * 128] for i in range(3))
        g2 = grad_ref[:, p * 128 : (p + 1) * 128]
        grads = [jnp.zeros((n, 128), f32) for _ in range(3)]
        for own in owns:
            only = lambda v: jnp.where(own, v, 0.0).astype(bf16)
            probs = softmax_of(q2, k2, own, allowed, scale)
            grad_probs = mm(only(g2), v2, NT)
            inner = jnp.sum(probs * grad_probs, axis=-1, keepdims=True)
            grad_logits = (probs * (grad_probs - inner)).astype(bf16)
            grads[0] += mm(grad_logits, only(k2), NN)
            grads[1] += mm(grad_logits, only(q2), TN)
            grads[2] += mm(probs.astype(bf16), only(g2), TN)
        for i, factor in enumerate((scale, scale, 1.0)):
            out_ref[:, i * width + p * 128 : i * width + (p + 1) * 128] = (grads[i] * factor).astype(bf16)


def attention(kernel, segs, scale, qkv, *more):
    seqs, n = segs.shape
    width = qkv.shape[1] // 3
    out_width = 3 * width if more else width
    rows = lambda w: pl.BlockSpec((n, w), lambda s: (s, 0))
    matmuls = (5 if more else 2) * 2 * seqs * n * n * width
    return pl.pallas_call(
        functools.partial(kernel, scale),
        grid=(seqs,),
        out_shape=jax.ShapeDtypeStruct((seqs * n, out_width), bf16),
        in_specs=[pl.BlockSpec((1, n, 1), lambda s: (s, 0, 0)), pl.BlockSpec((1, 1, n), lambda s: (s, 0, 0)), rows(3 * width)]
        + [rows(width)] * len(more),
        out_specs=rows(out_width),
        compiler_params=VMEM,
        cost_estimate=pl.CostEstimate(flops=10 * matmuls, transcendentals=seqs * HEADS * n * n, bytes_accessed=2 * seqs * n * (3 * width + out_width)),
        name="attention_backward" if more else "attention",
    )(segs[:, :, None], segs[:, None, :], qkv, *more)


def body(sizes, *args):
    tokens, cotangent, segment_ids, routed = args[:4]
    states = [args[4 + 4 * i : 8 + 4 * i] for i in range(6)]
    qkv_state, out_state, up_state, down_state, router_state, gains_state = states
    seqs, length, width = tokens.shape
    capacity = routed.shape[1]
    count = seqs * capacity
    rows = out_state[0].shape[0]
    hidden = up_state[0].shape[1]
    fold = down_state[0].shape[0] // rows
    scale = (width // HEADS) ** (-0.5)
    pos = jnp.stack([lax.axis_index(n) for n in ("y", "c", "a", "b")]).astype(jnp.int32)

    low = lambda v: v.astype(bf16)
    small = jnp.concatenate([router_state[0][:, None], gains_state[0].T, jnp.zeros((rows, SMALL - 3), f32)], axis=1)
    send_qkv = low(jnp.concatenate([qkv_state[0][0], qkv_state[0][1], qkv_state[0][2], small], axis=1))
    send_up = low(jnp.concatenate([out_state[0], up_state[0]], axis=1))
    send_down = low(down_state[0]).reshape(fold, rows, width).transpose(1, 0, 2).reshape(rows, fold * width)
    mine_up = lax.all_gather(send_up, ("y", "a", "b"), axis=0, tiled=False)
    way_qkv = gather_first(send_qkv, sizes)
    way_down = gather_first(send_down, sizes)

    here = routed[:, :, None] == jnp.arange(length, dtype=jnp.int32)[None, None, :]
    pick = here.astype(bf16)
    is_routed = jnp.any(here, axis=1)
    picked = dot(pick, tokens, "sct,std->scd").astype(bf16).reshape(count, width)
    way_qkv = gather_second(after(way_qkv, picked), sizes)
    picked_cot = dot(pick, cotangent, "sct,std->scd").astype(bf16).reshape(count, width)
    segs = jnp.sum(jnp.where(here, segment_ids[:, None, :], 0), axis=-1)
    way_qkv = after(way_qkv, picked_cot, way_down)
    way_down = gather_second(after(way_down, way_qkv), sizes)
    way_qkv = gather_third(way_qkv, sizes)
    got = gather_last(way_qkv, sizes)
    way_down, pos_qkv = lax.optimization_barrier((way_down, pos))
    way_down = gather_third(way_down, sizes)

    w_qkv, w_small = assemble(*got, pos_qkv, sizes, [(0, 3 * width), (3 * width, SMALL)])
    w_qkv = w_qkv.reshape(width, 3 * width)
    w_small = w_small.reshape(width, SMALL)
    router_low = w_small[:, 0]
    gain_one = w_small[:, 1].astype(f32)
    gain_two = w_small[:, 2].astype(f32)

    picked_f = picked.astype(f32)
    back_cot = picked_cot.astype(f32)
    score = jnp.dot(picked, router_low, preferred_element_type=f32)
    normed_one, pull_one = jax.vjp(norm_scale, picked_f, gain_one)
    hidden_one = low(normed_one)
    projected = low(dot(hidden_one, w_qkv, "rd,de->re"))
    mine_up = after(mine_up, projected)
    theirs_up = shifted(mine_up, "c", sizes, 1)
    mixed = attention(attend_kernel, segs, scale, projected)
    mixed, theirs_up, way_down = lax.optimization_barrier((mixed, theirs_up, way_down))
    got_down = gather_last(way_down, sizes)

    w_both = join_cores(mine_up, theirs_up, sizes).reshape(width, width + hidden)
    w_out, w_up = w_both[:, :width], w_both[:, width:]
    attended = dot(mixed, w_out, "rd,de->re")
    first = picked_f + score[:, None] * attended
    normed_two, pull_two = jax.vjp(norm_scale, first, gain_two)
    hidden_two = low(normed_two)
    inner_pre = dot(hidden_two, w_up, "rd,df->rf")
    activ, pull_gelu = jax.vjp(gelu_tanh, inner_pre)
    activ_low = low(activ)
    grad_down_out = low(score[:, None] * back_cot)

    grad_wdown = low(dot(activ_low, grad_down_out, "rf,re->fe"))
    own_1, other_1 = sum_start(grad_wdown.reshape(-1, fold * rows, width), sizes)
    came_1 = shifted(other_1, "c", sizes, 1)

    got_down, pos_down = lax.optimization_barrier((got_down, after(pos, other_1)))
    (w_down,) = assemble(*got_down, pos_down, sizes, [(i * width, width) for i in range(fold)], fold)
    w_down = w_down.reshape(hidden, width)
    grad_activ = dot(grad_down_out, w_down, "re,fe->rf")
    grad_pre = low(pull_gelu(grad_activ)[0])

    grad_pre, came_1 = lax.optimization_barrier((grad_pre, came_1))
    (own_1a, part_1a), (own_1b, part_1b) = sum_first(own_1, came_1, sizes)
    grad_pre, part_1a, part_1b = lax.optimization_barrier((grad_pre, part_1a, part_1b))
    came_1a, came_1b = send_parts(part_1a, "b", sizes), send_parts(part_1b, "y", sizes)
    grad_wup = low(dot(hidden_two, grad_pre, "rd,rf->df")).reshape(-1, rows, hidden)
    own_2, other_2 = sum_start(grad_wup, sizes)
    grad_pre, other_2 = lax.optimization_barrier((grad_pre, other_2))
    came_2 = shifted(other_2, "c", sizes, 1)

    grad_hidden_two = dot(grad_pre, w_up, "rf,df->rd")
    grad_first_norm, grad_gain_two = pull_two(grad_hidden_two)
    grad_first = back_cot + grad_first_norm
    grad_attended = low(score[:, None] * grad_first)

    grad_attended, came_1a, came_1b, came_2 = lax.optimization_barrier((grad_attended, came_1a, came_1b, came_2))
    (own_2a, part_2a), (own_2b, part_2b) = sum_first(own_2, came_2, sizes)
    (own_1a, part_1a), (own_1b, part_1b) = sum_second((own_1a, own_1b), (came_1a, came_1b), sizes)
    grad_attended, part_1a, part_1b, part_2a, part_2b = lax.optimization_barrier((grad_attended, part_1a, part_1b, part_2a, part_2b))
    came_1a, came_1b = send_parts(part_1a, "y", sizes), send_parts(part_1b, "b", sizes)
    came_2a, came_2b = send_parts(part_2a, "b", sizes), send_parts(part_2b, "y", sizes)

    grad_mixed = low(dot(grad_attended, w_out, "re,de->rd"))
    grad_projected = attention(attend_back_kernel, segs, scale, projected, grad_mixed)

    ready = lax.optimization_barrier((grad_projected, came_1a, came_1b, came_2a, came_2b))
    grad_projected, came_1a, came_1b, came_2a, came_2b = ready
    own_1, part_1 = sum_third((own_1a, own_1b), (came_1a, came_1b), sizes)
    (own_2a, part_2a), (own_2b, part_2b) = sum_second((own_2a, own_2b), (came_2a, came_2b), sizes)
    grad_projected, part_1, part_2a, part_2b = lax.optimization_barrier((grad_projected, part_1, part_2a, part_2b))
    came_1 = send_parts(part_1, "a", sizes)
    came_2a, came_2b = send_parts(part_2a, "y", sizes), send_parts(part_2b, "b", sizes)

    grad_wqkv = low(dot(hidden_one, grad_projected, "rd,re->de"))
    grad_wout = low(dot(mixed, after(grad_attended, grad_projected), "rd,re->de"))
    rest = jnp.concatenate([grad_wqkv, grad_wout], axis=1).reshape(-1, rows, 4 * width)
    own_3, other_3 = sum_start(rest, sizes)
    grad_projected, other_3, activ_late = lax.optimization_barrier((grad_projected, other_3, activ_low))
    came_3 = shifted(other_3, "c", sizes, 1)

    down_out = dot(activ_late, w_down, "rf,fe->re")
    second = low(first + score[:, None] * down_out).reshape(seqs, capacity, width)
    grad_score = jnp.sum(back_cot * down_out, axis=-1) + jnp.sum(grad_first * attended, axis=-1)
    grad_hidden_one = dot(grad_projected, w_qkv, "re,de->rd")
    grad_picked_norm, grad_gain_one = pull_one(grad_hidden_one)
    grad_rows = grad_first + grad_picked_norm + grad_score[:, None] * router_low.astype(f32)[None, :]
    grad_rows = low(grad_rows).reshape(seqs, capacity, width)
    grad_router = jnp.sum(grad_score[:, None] * picked_f, axis=0)
    grad_small = jnp.stack([grad_router, grad_gain_one, grad_gain_two], axis=1)
    grad_small = low(jnp.pad(grad_small, ((0, 0), (0, SMALL - 3)))).reshape(-1, rows, SMALL)
    own_s, other_s = sum_start(grad_small, sizes)
    came_s = shifted(other_s, "c", sizes, 1)
    came_3, came_s, second, grad_rows = lax.optimization_barrier((came_3, came_s, second, grad_rows))

    join = lambda a, b: jnp.concatenate([a, b], axis=-1)
    (own_3a, part_3a), (own_3b, part_3b) = sum_first(join(own_3, own_s), join(came_3, came_s), sizes)
    ready = lax.optimization_barrier((part_3a, part_3b, second, grad_rows, came_1, came_2a, came_2b))
    part_3a, part_3b, second, grad_rows, came_1, came_2a, came_2b = ready
    came_3a, came_3b = send_parts(part_3a, "b", sizes), send_parts(part_3b, "y", sizes)
    own_2, part_2 = sum_third((own_2a, own_2b), (came_2a, came_2b), sizes)
    part_2, second = lax.optimization_barrier((part_2, second))
    came_2 = send_parts(part_2, "a", sizes)

    block_out = jnp.where(is_routed[:, :, None], low(dot(pick, second, "sct,scd->std")), tokens)
    came_3a, came_3b, grad_rows, block_out = lax.optimization_barrier((came_3a, came_3b, grad_rows, block_out))
    (own_3a, part_3a), (own_3b, part_3b) = sum_second((own_3a, own_3b), (came_3a, came_3b), sizes)
    part_3a, part_3b, grad_rows, came_1 = lax.optimization_barrier((part_3a, part_3b, grad_rows, came_1))
    came_3a, came_3b = send_parts(part_3a, "y", sizes), send_parts(part_3b, "b", sizes)
    tokens_grad = jnp.where(is_routed[:, :, None], low(dot(pick, grad_rows, "sct,scd->std")), cotangent)
    sum_down = add_up(own_1, came_1)
    came_3a, came_3b, tokens_grad = lax.optimization_barrier((came_3a, came_3b, tokens_grad))
    own_3, part_3 = sum_third((own_3a, own_3b), (came_3a, came_3b), sizes)
    part_3, came_2 = lax.optimization_barrier((part_3, came_2))
    came_3 = send_parts(part_3, "a", sizes)
    sum_up = add_up(own_2, came_2)
    sum_rest = add_up(own_3, came_3)

    total_small = sum_rest[:, 4 * width :]
    grads = (
        jnp.stack([sum_rest[:, i * width : (i + 1) * width] for i in range(3)]),
        sum_rest[:, 3 * width : 4 * width],
        sum_up,
        sum_down,
        total_small[:, 0],
        total_small[:, 1:3].T,
    )
    decays = (decay_rate, decay_rate, decay_rate, decay_rate, 0.0, 0.0)
    results = [block_out, tokens_grad]
    for state, grad, decay, rate in zip(states, grads, decays, learn_rates):
        results = results + adamw(state, grad, decay, rate)
    return tuple(results)


def solution(mesh):
    lead = mesh.shape["dp"] // 2
    inner = mesh.shape["fsdp"] // 4
    names = ("y", "c", "a", "b")
    fine = Mesh(mesh.devices.reshape(lead, 2, 4, inner), names)
    sizes = dict(zip(names, (lead, 2, 4, inner)))
    head, second, only = P(names, None, None), P(None, names, None), P(names, None)
    weights = (second,) * 4 + (only,) * 12 + (P(names),) * 4 + (P(None, names),) * 4
    return jax.shard_map(
        functools.partial(body, sizes),
        mesh=fine,
        in_specs=(head, head, only, only) + weights,
        out_specs=(head, head) + weights,
        check_vma=False,
    )
```

time: 419 us -> 331 us (0.79)
  waiting for transfers between devices: 132 us -> 67.8 us
  local copies, waits for them, and re-layouts: 70.1 us -> 48.1 us
  matrix products: 85.2 us -> 66.2 us
  between operations: 2.31 us -> 16 us
  other arithmetic: 30.7 us -> 44.1 us
  starting transfers between devices: 62.2 us -> 52.4 us
    ppermute x60 -> x48, waiting for transfers between devices: 132 us -> 60.2 us  [shifted(): return lax.ppermute(value, axis, [(i, (i + step) % n) for i in range(n)])]
    reshape x8 -> x0, local copies, waits for them, and re-layouts: 27.3 us -> none  [the longest x3 11.2 us: body(): g.reshape(count, width)]
    dot_general x22 -> x16, matrix products: 84.9 us -> 66 us  [dot(): return jnp.einsum(spec, a, b, preferred_element_type=f32)]
    ppermute x60 -> x48, starting transfers between devices: 62.2 us -> 52.3 us  [shifted(): return lax.ppermute(value, axis, [(i, (i + step) % n) for i in range(n)])]
    add x18 -> x16, other arithmetic: 7.03 us -> 15 us  [the longest x3 7.89 us: sum_first(): total = own.astype(f32) + came.astype(f32)]
    all_gather x0 -> x1, waiting for transfers between devices: none -> 7.56 us  [body(): mine_up = lax.all_gather(send_up, ('y', 'a', 'b'), axis=0, tiled=False)]
    dynamic_slice x0 -> x5, local copies, waits for them, and re-layouts: none -> 7.1 us  [take(): return lax.dynamic_index_in_dim(value, index, axis, keepdims=False)]
    pallas_call x3 -> x2, Pallas kernels: 14.9 us -> 21 us  [attention(): pl.pallas_call(functools.partial(kernel, scale), grid=(seqs,), out_shape=...]
  transfers between devices with their start and end apart: 60 -> 49, of which waited for: 26 -> 18; matrix products, arithmetic and copies ran while one was open for 18% -> 26% of each run, Pallas kernels for 2% -> 9%
where the time goes in v3:
time: 331 us; the launch traced here: 325 us
  waiting for transfers between devices  67.8 us (20%)
  matrix products  66.2 us (20%)
  starting transfers between devices  52.4 us (16%)
  local copies, waits for them, and re-layouts  48.1 us (15%)
  other arithmetic  44.1 us (13%)
  Pallas kernels  30.1 us (9%)
  between operations  16 us (5%)
    dot_general x16, matrix products, dot(): return jnp.einsum(spec, a, b, preferred_element_type=f32)  66 us
    ppermute x48, waiting for transfers between devices, shifted(): return lax.ppermute(value, axis, [(i, (i + step) % n) for i in range(n)])  60.2 us
    ppermute x48, starting transfers between devices, shifted(): return lax.ppermute(value, axis, [(i, (i + step) % n) for i in range(n)])  52.3 us
    pallas_call x2, Pallas kernels, attention(): pl.pallas_call(functools.partial(kernel, scale), grid=(seqs,), out_shape=...  21 us
    unnamed x202, local copies, waits for them, and re-layouts  19.1 us
    pallas_call x2, Pallas kernels, assemble(): pl.pallas_call(kernel, out_shape=shapes, in_specs=[pl.BlockSpec(memory_sp...  9.16 us
    add x3, other arithmetic, sum_first(): total = own.astype(f32) + came.astype(f32)  7.89 us
    all_gather x1, waiting for transfers between devices, body(): mine_up = lax.all_gather(send_up, ('y', 'a', 'b'), axis=0, tiled=False)  7.56 us
  transfers between devices with their start and end apart: 49, of which 18 were waited for; matrix products, arithmetic and copies ran while one was open for 26% of the time, Pallas kernels for 9%

profile of v3, /device:TPU:0, one launch (start us, length us, event | category | flops | bytes accessed | tf_op | source)
XLA Modules:
  0.0 324.7 jit_solution(16141443423224472614)
XLA Ops:
  12.5 4.1 %collective-permute-start.4 = (bf16[24,2560]{1,0:T(8,128)(2,1)S(1)}, bf16[24,2560]{1,0:T(8,128)(2,1)S(1)}, u32[]{:S(2)}, u32[]{:S(2)}) collective-permute-start(bf16[24,2560]{1,0:T(8,128)(2,1)S(1)} %concatenate.57), channel_id=1, source_target_pairs={{0,4},{2,6},{4,0},{6,2},{1,5},{3,7},{5,1},{7,3},{8,12},{10,14},{12... | collective-permute-start | bytes 368648 | tf_op jit(solution)/shard_map/ppermute | solution.py:27
  20.8 2.9 collective-permute-start.2
  23.7 4.0 %fusion.20 = (f32[3,160]{1,0:T(4,128)S(1)}, bf16[3,160,768]{2,1,0:T(8,128)(2,1)S(1)}) fusion(bf16[3,1280,768]{2,1,0:T(8,128)(2,1)} %param.28, s32[3,160]{1,0:T(4,128)S(1)} %copy-done.62), kind=kOutput, calls=%fused_computation.82 | convolution fusion | flops 945806848 | bytes 6639360 | tf_op jit(solution)/shard_map/sct,std->scd/dot_general | solution.py:189
  27.6 2.2 fusion.31
  33.3 8.7 %collective-permute-done.1 = bf16[24,3072]{1,0:T(8,128)(2,1)S(1)} collective-permute-done((bf16[24,3072]{1,0:T(8,128)(2,1)S(1)}, bf16[24,3072]{1,0:T(8,128)(2,1)S(1)}, u32[]{:S(2)}, u32[]{:S(2)}) %collective-permute-start.1) | collective-permute-done | bytes 147488 | tf_op jit(solution)/shard_map/ppermute | solution.py:27
  47.9 15.0 %collective-permute-done.9 = bf16[2,24,3072]{2,1,0:T(8,128)(2,1)S(1)} collective-permute-done((bf16[2,24,3072]{2,1,0:T(8,128)(2,1)S(1)}, bf16[2,24,3072]{2,1,0:T(8,128)(2,1)S(1)}, u32[]{:S(2)}, u32[]{:S(2)}) %collective-permute-start.9) | collective-permute-done | bytes 294944 | tf_op jit(solution)/shard_map/ppermute | solution.py:27
  65.5 5.0 %collective-permute-done.8 = bf16[2,24,3072]{2,1,0:T(8,128)(2,1)S(1)} collective-permute-done((bf16[2,24,3072]{2,1,0:T(8,128)(2,1)S(1)}, bf16[2,24,3072]{2,1,0:T(8,128)(2,1)S(1)}, u32[]{:S(2)}, u32[]{:S(2)}) %collective-permute-start.8) | collective-permute-done | bytes 294944 | tf_op jit(solution)/shard_map/ppermute | solution.py:27
  73.1 4.3 %assemble.2 = (bf16[32,24,2304]{2,1,0:T(8,128)(2,1)}, bf16[32,24,256]{2,1,0:T(8,128)(2,1)}) custom-call(s32[4]{0:T(128)} %pad_add_fusion.pos_ref, bf16[2,2,24,2560]{3,2,1,0:T(8,128)(2,1)} %copy-done.28, bf16[2,2,24,2560]{3,2,1,0:T(8,128)(2,1)} %copy-done.43, bf16[2,2,24,2560]{3,2,1,0:T(8,128)(2,1)} %copy-done.27, bf16[2,2,24,2560]{3,2,1,0:T(8,128)(2,1)} %copy-done.44, ...), custom_call_target="tpu_custom_call" | custom-call | bytes 7864320 | tf_op jit(solution)/shard_map/assemble/pallas_call | solution.py:159
  77.4 2.1 slice_reduce_fusion
  79.9 5.3 %convolution_convert_fusion.3.qkv_ref = bf16[480,2304]{1,0:T(8,128)(2,1)} fusion(bf16[480,768]{1,0:T(8,128)(2,1)S(1)} %bitcast.245, bf16[768,2304]{1,0:T(8,128)(2,1)} %bitcast.275), kind=kOutput, calls=%fused_computation.20 | convolution fusion | flops 1699799040 | bytes 6488064 | tf_op jit(solution)/shard_map/rd,de->re/dot_general | solution.py:189
  85.2 7.6 %all-gather.2.cloned.1.call-done = bf16[16,24,3840]{2,1,0:T(8,128)(2,1)} async-done(((bf16[1,24,3840]{2,1,0:T(8,128)(2,1)}), bf16[16,24,3840]{2,1,0:T(8,128)(2,1)}) %all-gather.2.cloned.1.call-update) | async-done | bytes 2949136 | tf_op jit(solution)/shard_map/all_gather | solution.py:287
  96.3 6.8 %attention.1 = bf16[480,768]{1,0:T(8,128)(2,1)} custom-call(s32[3,160,1]{2,1,0:T(8,128)} %copy.244.col_ref, s32[3,1,160]{2,1,0:T(1,128)} %broadcast_in_dim.68.row_ref, bf16[480,2304]{1,0:T(8,128)(2,1)} %convolution_convert_fusion.3.qkv_ref), custom_call_target="tpu_custom_call" | custom-call | flops 2359296000 | bytes 2949120 | tf_op jit(solution)/shard_map/attention/pallas_call | solution.py:256
  103.4 5.4 %collective-permute-done.17.refs_1_ = bf16[2,2,24,3072]{3,2,1,0:T(8,128)(2,1)} collective-permute-done((bf16[2,2,24,3072]{3,2,1,0:T(8,128)(2,1)}, bf16[2,2,24,3072]{3,2,1,0:T(8,128)(2,1)}, u32[]{:S(2)}, u32[]{:S(2)}) %collective-permute-start.17) | collective-permute-done | bytes 589856 | tf_op jit(solution)/shard_map/ppermute | solution.py:27
  109.9 2.2 broadcast_select_fusion.1
  113.3 2.6 convert_add_fusion.3
  116.1 5.2 %multiply_convert_fusion = (bf16[480,3072]{1,0:T(8,128)(2,1)S(1)}, f32[480,3072]{1,0:T(8,128)}) fusion(bf16[768,3840]{1,0:T(8,128)(2,1)S(1)} %bitcast.223, f32[480,768]{1,0:T(8,128)S(1)} %get-tuple-element.446, f32[768]{0:T(1024)S(1)} %convert_reduce_fusion, f32[480]{0:T(512)S(1)} %fusion.100), kind=kOutput, calls=%fused_computation.12 | convolution fusion | flops 2279301120 | bytes 15046656 | tf_op jit(solution)/shard_map/rd,df->rf/dot_general | solution.py:189
  121.3 3.1 convolution_convert_fusion.2
  129.8 3.9 %collective-permute-done.19.refs_4_ = bf16[2,2,24,3072]{3,2,1,0:T(8,128)(2,1)S(1)} collective-permute-done((bf16[2,2,24,3072]{3,2,1,0:T(8,128)(2,1)}, bf16[2,2,24,3072]{3,2,1,0:T(8,128)(2,1)S(1)}, u32[]{:S(2)}, u32[]{:S(2)}) %collective-permute-start.19) | collective-permute-done | bytes 589856 | tf_op jit(solution)/shard_map/ppermute | solution.py:27
  135.9 4.8 %assemble.3 = bf16[128,24,768]{2,1,0:T(8,128)(2,1)} custom-call(s32[4]{0:T(128)} %pad_add_fusion.pos_ref, bf16[2,2,24,3072]{3,2,1,0:T(8,128)(2,1)} %pad_maximum_fusion.2.refs_0_, bf16[2,2,24,3072]{3,2,1,0:T(8,128)(2,1)} %collective-permute-done.17.refs_1_, bf16[2,2,24,3072]{3,2,1,0:T(8,128)(2,1)} %pad_maximum_fusion.3.refs_2_, ...), custom_call_target="tpu_custom_call" | custom-call | bytes 9437184 | tf_op jit(solution)/shard_map/assemble/pallas_call | solution.py:159
  140.7 8.6 %fusion.6 = bf16[480,3072]{1,0:T(8,128)(2,1)S(1)} fusion(f32[480,3072]{1,0:T(8,128)} %get-tuple-element.449, bf16[480,768]{1,0:T(8,128)(2,1)S(1)} %bitcast.244, bf16[3072,768]{1,0:T(8,128)(2,1)} %bitcast.226), kind=kOutput, calls=%fused_computation.8 | convolution fusion | flops 2294415360 | bytes 14303232 | tf_op jit(solution)/shard_map/re,fe->rf/dot_general | solution.py:189
  149.3 3.3 %convert_add_fusion.2 = f32[2,4,2,96,768]{4,3,1,2,0:T(8,128)S(1)} fusion(bf16[2,4,2,96,768]{4,3,1,2,0:T(8,128)(2,1)} %collective-permute-done.23, bf16[2,1,4,2,96,768]{5,4,3,2,1,0:T(8,128)(2,1)S(1)} %copy-done.4), kind=kLoop, calls=%fused_computation.19 | loop fusion | flops 3538944 | bytes 9437184 | tf_op jit(solution)/shard_map/add | solution.py:93
  155.8 3.2 convolution_convert_fusion.1
  169.0 6.5 %multiply_reduce_fusion.2 = (f32[480]{0:T(512)S(1)}, bf16[768]{0:T(1024)(128)(2,1)}, f32[480,768]{1,0:T(8,128)S(1)}) fusion(f32[480,768]{1,0:T(8,128)S(1)} %get-tuple-element.446, f32[768]{0:T(1024)S(1)} %copy-done.67, f32[480]{0:T(512)S(1)} %copy-done.71, bf16[480,3072]{1,0:T(8,128)(2,1)} %copy-done.86, bf16[768,3840]{1,0:T(8,128)(2,1)} %bitcast.224), kind=kOutput, calls=%fused_computation.96 | convolution fusion | flops 2267134720 | bytes 10625280 | tf_op jit(solution)/shard_map/rf,df->rd/dot_general | solution.py:189
  177.6 6.4 %collective-permute-done.24 = bf16[2,4,96,384]{3,2,1,0:T(8,128)(2,1)S(1)} collective-permute-done((bf16[2,4,96,384]{3,2,1,0:T(8,128)(2,1)}, bf16[2,4,96,384]{3,2,1,0:T(8,128)(2,1)S(1)}, u32[]{:S(2)}, u32[]{:S(2)}) %collective-permute-start.24) | collective-permute-done | bytes 589856 | tf_op jit(solution)/shard_map/ppermute | solution.py:27
  183.9 2.5 convert_add_fusion.1
  187.1 3.2 copy-done.9
  195.2 2.9 convolution_convert_fusion.5.grad_ref
  199.8 14.2 %attention_backward.1 = bf16[480,2304]{1,0:T(8,128)(2,1)} custom-call(s32[3,160,1]{2,1,0:T(8,128)} %copy.244.col_ref, s32[3,1,160]{2,1,0:T(1,128)} %broadcast_in_dim.68.row_ref, bf16[480,2304]{1,0:T(8,128)(2,1)} %convolution_convert_fusion.3.qkv_ref, bf16[480,768]{1,0:T(8,128)(2,1)} %convolution_convert_fusion.5.grad_ref), custom_call_target="tpu_custom_call" | custom-call | flops 5898240000 | bytes 4423680 | tf_op jit(solution)/shard_map/attention_backward/pallas_call | solution.py:256
  222.3 2.2 convolution_convert_fusion
  225.9 2.7 dynamic-slice_bitcast_fusion.1
  232.0 3.4 %add_convert_fusion = (bf16[480,768]{1,0:T(8,128)(2,1)}, f32[480]{0:T(512)S(1)}) fusion(f32[480,768]{1,0:T(8,128)S(1)} %copy-done.1, f32[480]{0:T(512)S(1)} %bitcast.270, bf16[480,768]{1,0:T(8,128)(2,1)S(1)} %bitcast.233, bf16[480,3072]{1,0:T(8,128)(2,1)S(1)} %copy-done.88, bf16[3072,768]{1,0:T(8,128)(2,1)S(1)} %bitcast.229), kind=kOutput, calls=%fused_computation.92 | convolution fusion | flops 2267135488 | bytes 10620672 | tf_op jit(solution)/shard_map/rf,fe->re/dot_general | solution.py:189
  235.8 6.4 %fusion.29 = (f32[480]{0:T(512)}, bf16[768]{0:T(1024)(128)(2,1)S(1)}, f32[480,768]{1,0:T(8,128)}) fusion(bf16[480,768]{1,0:T(8,128)(2,1)S(1)} %bitcast.219, f32[768]{0:T(1024)S(1)} %convert_reduce_fusion.1, f32[480]{0:T(512)} %copy-done.72, bf16[3,160,768]{2,1,0:T(8,128)(2,1)S(1)} %get-tuple-element.445, bf16[480,2304]{1,0:T(8,128)(2,1)} %attention_backward.1, ...), kind=kOutput, calls=%fused_computation.91 | convolution fusion | flops 1701640960 | bytes 8708352 | tf_op jit(solution)/shard_map/re,de->rd/dot_general | solution.py:189
  245.6 2.5 collective-permute-start.33
  250.8 2.3 collective-permute-start.34
  253.1 2.9 collective-permute-start.35
  256.0 2.1 convert_add_fusion
  258.7 2.9 collective-permute-done.34
  263.6 2.8 collective-permute-start.42
  266.3 2.5 collective-permute-start.43
  268.9 5.0 %convert_select_fusion.1 = bf16[3,1280,768]{2,1,0:T(8,128)(2,1)} fusion(bf16[3,1280,768]{2,1,0:T(8,128)(2,1)S(1)} %bitcast.272, pred[3,1280]{1,0:T(4,128)(4,1)S(1)} %copy-done.73, bf16[3,160,768]{2,1,0:T(8,128)(2,1)S(1)} %bitcast.277, s32[3,160]{1,0:T(4,128)S(1)} %copy-done.64), kind=kOutput, calls=%fused_computation.11 | convolution fusion | flops 950231040 | bytes 12539520 | tf_op jit(solution)/shard_map/sct,scd->std/dot_general | solution.py:189
  273.9 2.2 collective-permute-done.38
  278.7 4.7 %convert_select_fusion = bf16[3,1280,768]{2,1,0:T(8,128)(2,1)} fusion(bf16[3,1280,768]{2,1,0:T(8,128)(2,1)S(1)} %bitcast.274, pred[3,1280]{1,0:T(4,128)(4,1)S(1)} %copy-done.73, bf16[3,160,768]{2,1,0:T(8,128)(2,1)S(1)} %bitcast.243, s32[3,160]{1,0:T(4,128)S(1)} %copy-done.64), kind=kOutput, calls=%fused_computation.10 | convolution fusion | flops 950231040 | bytes 12539520 | tf_op jit(solution)/shard_map/sct,scd->std/dot_general | solution.py:189
  285.8 4.0 %collective-permute-start.45 = (bf16[24,3328]{1,0:T(8,128)(2,1)S(1)}, bf16[24,3328]{1,0:T(8,128)(2,1)}, u32[]{:S(2)}, u32[]{:S(2)}) collective-permute-start(bf16[24,3328]{1,0:T(8,128)(2,1)S(1)} %get-tuple-element.207), channel_id=1, source_target_pairs={{0,2},{2,4},{4,6},{6,0},{1,3},{3,5},{5,7},{7,1},{8,10},{10,12},{12... | collective-permute-start | bytes 479240 | tf_op jit(solution)/shard_map/ppermute | solution.py:27
  289.8 3.6 %collective-permute-start.46 = (bf16[24,3328]{1,0:T(8,128)(2,1)}, bf16[24,3328]{1,0:T(8,128)(2,1)}, u32[]{:S(2)}, u32[]{:S(2)}) collective-permute-start(bf16[24,3328]{1,0:T(8,128)(2,1)} %get-tuple-element.208), channel_id=1, source_target_pairs={{0,4},{2,6},{4,0},{6,2},{1,5},{3,7},{5,1},{7,3},{8,12},{10,14},{12... | collective-permute-start | bytes 479240 | tf_op jit(solution)/shard_map/ppermute | solution.py:27
  295.2 2.9 collective-permute-done.45
  299.5 2.4 collective-permute-done.46
  301.9 2.1 copy.249
  304.0 2.1 copy.250
  (387 shorter events, 101.2 us)
Async XLA Ops:
  7.2 85.5 %all-gather.2.cloned.1.call-start = ((), (), s32[]{:S(2)}) async-start(), calls=%async_computation | async-start | bytes 3133440 | tf_op jit(solution)/shard_map/all_gather | solution.py:287
  12.5 17.6 %collective-permute-start.4 = (bf16[24,2560]{1,0:T(8,128)(2,1)S(1)}, bf16[24,2560]{1,0:T(8,128)(2,1)S(1)}, u32[]{:S(2)}, u32[]{:S(2)}) collective-permute-start(bf16[24,2560]{1,0:T(8,128)(2,1)S(1)} %concatenate.57), channel_id=1, source_target_pairs={{0,4},{2,6},{4,0},{6,2},{1,5},{3,7},{5,1},{7,3},{8,12},{10,14},{12... | collective-permute-start | bytes 368648 | tf_op jit(solution)/shard_map/ppermute | solution.py:27
  16.6 13.6 %collective-permute-start.5 = (bf16[24,2560]{1,0:T(8,128)(2,1)S(1)}, bf16[24,2560]{1,0:T(8,128)(2,1)S(1)}, u32[]{:S(2)}, u32[]{:S(2)}) collective-permute-start(bf16[24,2560]{1,0:T(8,128)(2,1)S(1)} %concatenate.57), channel_id=1, source_target_pairs={{0,6},{2,0},{4,2},{6,4},{1,7},{3,1},{5,3},{7,5},{8,14},{10,8},{12,... | collective-permute-start | bytes 368648 | tf_op jit(solution)/shard_map/ppermute | solution.py:27
  17.9 12.3 %collective-permute-start.3 = (bf16[24,2560]{1,0:T(8,128)(2,1)S(1)}, bf16[24,2560]{1,0:T(8,128)(2,1)S(1)}, u32[]{:S(2)}, u32[]{:S(2)}) collective-permute-start(bf16[24,2560]{1,0:T(8,128)(2,1)S(1)} %concatenate.57), channel_id=1, source_target_pairs={{0,2},{2,4},{4,6},{6,0},{1,3},{3,5},{5,7},{7,1},{8,10},{10,12},{12... | collective-permute-start | bytes 368648 | tf_op jit(solution)/shard_map/ppermute | solution.py:27
  19.7 22.4 %collective-permute-start.1 = (bf16[24,3072]{1,0:T(8,128)(2,1)S(1)}, bf16[24,3072]{1,0:T(8,128)(2,1)S(1)}, u32[]{:S(2)}, u32[]{:S(2)}) collective-permute-start(bf16[24,3072]{1,0:T(8,128)(2,1)S(1)} %bitcast.254), channel_id=1, source_target_pairs={{0,4},{2,6},{4,0},{6,2},{1,5},{3,7},{5,1},{7,3},{8,12},{10,14},{12... | collective-permute-start | bytes 442376 | tf_op jit(solution)/shard_map/ppermute | solution.py:27
  20.8 21.3 %collective-permute-start.2 = (bf16[24,3072]{1,0:T(8,128)(2,1)S(1)}, bf16[24,3072]{1,0:T(8,128)(2,1)S(1)}, u32[]{:S(2)}, u32[]{:S(2)}) collective-permute-start(bf16[24,3072]{1,0:T(8,128)(2,1)S(1)} %bitcast.255), channel_id=1, source_target_pairs={{0,6},{2,0},{4,2},{6,4},{1,7},{3,1},{5,3},{7,5},{8,14},{10,8},{12,... | collective-permute-start | bytes 442376 | tf_op jit(solution)/shard_map/ppermute | solution.py:27
  30.1 12.0 %collective-permute-start = (bf16[24,3072]{1,0:T(8,128)(2,1)S(1)}, bf16[24,3072]{1,0:T(8,128)(2,1)S(1)}, u32[]{:S(2)}, u32[]{:S(2)}) collective-permute-start(bf16[24,3072]{1,0:T(8,128)(2,1)S(1)} %bitcast.256), channel_id=1, source_target_pairs={{0,2},{2,4},{4,6},{6,0},{1,3},{3,5},{5,7},{7,1},{8,10},{10,12},{12... | collective-permute-start | bytes 442376 | tf_op jit(solution)/shard_map/ppermute | solution.py:27
  30.3 11.9 %collective-permute-start.7 = (bf16[2,24,2560]{2,1,0:T(8,128)(2,1)S(1)}, bf16[2,24,2560]{2,1,0:T(8,128)(2,1)S(1)}, u32[]{:S(2)}, u32[]{:S(2)}) collective-permute-start(bf16[2,24,2560]{2,1,0:T(8,128)(2,1)S(1)} %pad_maximum_fusion.9), channel_id=1, source_target_pairs={{0,16},{16,0},{1,17},{17,1},{2,18},{18,2},{3,19},{19,3},{4,20},{20... | collective-permute-start | bytes 737288 | tf_op jit(solution)/shard_map/ppermute | solution.py:27
  31.9 10.4 %collective-permute-start.6 = (bf16[2,24,2560]{2,1,0:T(8,128)(2,1)S(1)}, bf16[2,24,2560]{2,1,0:T(8,128)(2,1)S(1)}, u32[]{:S(2)}, u32[]{:S(2)}) collective-permute-start(bf16[2,24,2560]{2,1,0:T(8,128)(2,1)S(1)} %pad_maximum_fusion.8), channel_id=1, source_target_pairs={{0,1},{1,0},{2,3},{3,2},{4,5},{5,4},{6,7},{7,6},{8,9},{9,8},{10,11... | collective-permute-start | bytes 737288 | tf_op jit(solution)/shard_map/ppermute | solution.py:27
  42.3 21.8 %collective-permute-start.10 = (bf16[2,2,24,2560]{3,2,1,0:T(8,128)(2,1)S(1)}, bf16[2,2,24,2560]{3,2,1,0:T(8,128)(2,1)S(1)}, u32[]{:S(2)}, u32[]{:S(2)}) collective-permute-start(bf16[2,2,24,2560]{3,2,1,0:T(8,128)(2,1)S(1)} %pad_maximum_fusion.4.refs_0_), channel_id=1, source_target_pairs={{0,16},{16,0},{1,17},{17,1},{2,18},{18,2},{3,19},{19,3},{4,20},{20... | collective-permute-start | bytes 1474568 | tf_op jit(solution)/shard_map/ppermute | solution.py:27
  44.2 19.9 %collective-permute-start.11 = (bf16[2,2,24,2560]{3,2,1,0:T(8,128)(2,1)S(1)}, bf16[2,2,24,2560]{3,2,1,0:T(8,128)(2,1)S(1)}, u32[]{:S(2)}, u32[]{:S(2)}) collective-permute-start(bf16[2,2,24,2560]{3,2,1,0:T(8,128)(2,1)S(1)} %pad_maximum_fusion.5.refs_2_), channel_id=1, source_target_pairs={{0,1},{1,0},{2,3},{3,2},{4,5},{5,4},{6,7},{7,6},{8,9},{9,8},{10,11... | collective-permute-start | bytes 1474568 | tf_op jit(solution)/shard_map/ppermute | solution.py:27
  45.7 17.2 %collective-permute-start.9 = (bf16[2,24,3072]{2,1,0:T(8,128)(2,1)S(1)}, bf16[2,24,3072]{2,1,0:T(8,128)(2,1)S(1)}, u32[]{:S(2)}, u32[]{:S(2)}) collective-permute-start(bf16[2,24,3072]{2,1,0:T(8,128)(2,1)S(1)} %pad_maximum_fusion.7), channel_id=1, source_target_pairs={{0,16},{16,0},{1,17},{17,1},{2,18},{18,2},{3,19},{19,3},{4,20},{20... | collective-permute-start | bytes 884744 | tf_op jit(solution)/shard_map/ppermute | solution.py:27
  47.4 24.0 %collective-permute-start.12 = (bf16[2,2,24,2560]{3,2,1,0:T(8,128)(2,1)S(1)}, bf16[2,2,24,2560]{3,2,1,0:T(8,128)(2,1)S(1)}, u32[]{:S(2)}, u32[]{:S(2)}) collective-permute-start(bf16[2,2,24,2560]{3,2,1,0:T(8,128)(2,1)S(1)} %pad_maximum_fusion.4.refs_0_), channel_id=1, source_target_pairs={{0,8},{8,0},{1,9},{9,1},{2,10},{10,2},{3,11},{11,3},{4,12},{12,4},... | collective-permute-start | bytes 1474568 | tf_op jit(solution)/shard_map/ppermute | solution.py:27
  47.4 24.0 %collective-permute-start.14 = (bf16[2,2,24,2560]{3,2,1,0:T(8,128)(2,1)S(1)}, bf16[2,2,24,2560]{3,2,1,0:T(8,128)(2,1)S(1)}, u32[]{:S(2)}, u32[]{:S(2)}) collective-permute-start(bf16[2,2,24,2560]{3,2,1,0:T(8,128)(2,1)S(1)} %pad_maximum_fusion.5.refs_2_), channel_id=1, source_target_pairs={{0,8},{8,0},{1,9},{9,1},{2,10},{10,2},{3,11},{11,3},{4,12},{12,4},... | collective-permute-start | bytes 1474568 | tf_op jit(solution)/shard_map/ppermute | solution.py:27
  62.9 7.6 %collective-permute-start.8 = (bf16[2,24,3072]{2,1,0:T(8,128)(2,1)S(1)}, bf16[2,24,3072]{2,1,0:T(8,128)(2,1)S(1)}, u32[]{:S(2)}, u32[]{:S(2)}) collective-permute-start(bf16[2,24,3072]{2,1,0:T(8,128)(2,1)S(1)} %pad_maximum_fusion.6), channel_id=1, source_target_pairs={{0,1},{1,0},{2,3},{3,2},{4,5},{5,4},{6,7},{7,6},{8,9},{9,8},{10,11... | collective-permute-start | bytes 884744 | tf_op jit(solution)/shard_map/ppermute | solution.py:27
  64.1 7.3 %collective-permute-start.13 = (bf16[2,2,24,2560]{3,2,1,0:T(8,128)(2,1)S(1)}, bf16[2,2,24,2560]{3,2,1,0:T(8,128)(2,1)S(1)}, u32[]{:S(2)}, u32[]{:S(2)}) collective-permute-start(bf16[2,2,24,2560]{3,2,1,0:T(8,128)(2,1)S(1)} %collective-permute-done.10.refs_1_), channel_id=1, source_target_pairs={{0,8},{8,0},{1,9},{9,1},{2,10},{10,2},{3,11},{11,3},{4,12},{12,4},... | collective-permute-start | bytes 1474568 | tf_op jit(solution)/shard_map/ppermute | solution.py:27
  64.2 8.9 %collective-permute-start.15 = (bf16[2,2,24,2560]{3,2,1,0:T(8,128)(2,1)S(1)}, bf16[2,2,24,2560]{3,2,1,0:T(8,128)(2,1)}, u32[]{:S(2)}, u32[]{:S(2)}) collective-permute-start(bf16[2,2,24,2560]{3,2,1,0:T(8,128)(2,1)S(1)} %collective-permute-done.11.refs_3_), channel_id=1, source_target_pairs={{0,8},{8,0},{1,9},{9,1},{2,10},{10,2},{3,11},{11,3},{4,12},{12,4},... | collective-permute-start | bytes 1474568 | tf_op jit(solution)/shard_map/ppermute | solution.py:27
  92.8 17.2 %collective-permute-start.16 = (bf16[16,24,3840]{2,1,0:T(8,128)(2,1)}, bf16[16,24,3840]{2,1,0:T(8,128)(2,1)}, u32[]{:S(2)}, u32[]{:S(2)}) collective-permute-start(bf16[16,24,3840]{2,1,0:T(8,128)(2,1)} %all-gather.2.cloned.1.call-done), channel_id=1, source_target_pairs={{0,8},{8,0},{1,9},{9,1},{2,10},{10,2},{3,11},{11,3},{4,12},{12,4},... | collective-permute-start | bytes 8847368 | tf_op jit(solution)/shard_map/ppermute | solution.py:27
  92.8 16.1 %collective-permute-start.17 = (bf16[2,2,24,3072]{3,2,1,0:T(8,128)(2,1)}, bf16[2,2,24,3072]{3,2,1,0:T(8,128)(2,1)}, u32[]{:S(2)}, u32[]{:S(2)}) collective-permute-start(bf16[2,2,24,3072]{3,2,1,0:T(8,128)(2,1)} %pad_maximum_fusion.2.refs_0_), channel_id=1, source_target_pairs={{0,16},{16,0},{1,17},{17,1},{2,18},{18,2},{3,19},{19,3},{4,20},{20... | collective-permute-start | bytes 1769480 | tf_op jit(solution)/shard_map/ppermute | solution.py:27
  94.2 15.8 %collective-permute-start.18 = (bf16[2,2,24,3072]{3,2,1,0:T(8,128)(2,1)}, bf16[2,2,24,3072]{3,2,1,0:T(8,128)(2,1)}, u32[]{:S(2)}, u32[]{:S(2)}) collective-permute-start(bf16[2,2,24,3072]{3,2,1,0:T(8,128)(2,1)} %pad_maximum_fusion.3.refs_2_), channel_id=1, source_target_pairs={{0,1},{1,0},{2,3},{3,2},{4,5},{5,4},{6,7},{7,6},{8,9},{9,8},{10,11... | collective-permute-start | bytes 1769480 | tf_op jit(solution)/shard_map/ppermute | solution.py:27
  127.6 21.7 %collective-permute-start.23 = (bf16[2,4,2,96,768]{4,3,1,2,0:T(8,128)(2,1)}, bf16[2,4,2,96,768]{4,3,1,2,0:T(8,128)(2,1)}, u32[]{:S(2)}, u32[]{:S(2)}) collective-permute-start(bf16[2,4,2,96,768]{4,3,1,2,0:T(8,128)(2,1)} %bitcast.214), channel_id=1, source_target_pairs={{0,8},{8,0},{1,9},{9,1},{2,10},{10,2},{3,11},{11,3},{4,12},{12,4},... | collective-permute-start | bytes 7077896 | tf_op jit(solution)/shard_map/ppermute | solution.py:27
  127.6 6.1 %collective-permute-start.19 = (bf16[2,2,24,3072]{3,2,1,0:T(8,128)(2,1)}, bf16[2,2,24,3072]{3,2,1,0:T(8,128)(2,1)S(1)}, u32[]{:S(2)}, u32[]{:S(2)}) collective-permute-start(bf16[2,2,24,3072]{3,2,1,0:T(8,128)(2,1)} %pad_maximum_fusion.2.refs_0_), channel_id=1, source_target_pairs={{0,8},{8,0},{1,9},{9,1},{2,10},{10,2},{3,11},{11,3},{4,12},{12,4},... | collective-permute-start | bytes 1769480 | tf_op jit(solution)/shard_map/ppermute | solution.py:27
  128.1 6.9 %collective-permute-start.21 = (bf16[2,2,24,3072]{3,2,1,0:T(8,128)(2,1)}, bf16[2,2,24,3072]{3,2,1,0:T(8,128)(2,1)}, u32[]{:S(2)}, u32[]{:S(2)}) collective-permute-start(bf16[2,2,24,3072]{3,2,1,0:T(8,128)(2,1)} %pad_maximum_fusion.3.refs_2_), channel_id=1, source_target_pairs={{0,8},{8,0},{1,9},{9,1},{2,10},{10,2},{3,11},{11,3},{4,12},{12,4},... | collective-permute-start | bytes 1769480 | tf_op jit(solution)/shard_map/ppermute | solution.py:27
  128.6 7.2 %collective-permute-start.22 = (bf16[2,2,24,3072]{3,2,1,0:T(8,128)(2,1)}, bf16[2,2,24,3072]{3,2,1,0:T(8,128)(2,1)}, u32[]{:S(2)}, u32[]{:S(2)}) collective-permute-start(bf16[2,2,24,3072]{3,2,1,0:T(8,128)(2,1)} %collective-permute-done.18.refs_3_), channel_id=1, source_target_pairs={{0,8},{8,0},{1,9},{9,1},{2,10},{10,2},{3,11},{11,3},{4,12},{12,4},... | collective-permute-start | bytes 1769480 | tf_op jit(solution)/shard_map/ppermute | solution.py:27
  162.5 21.4 %collective-permute-start.26 = (bf16[2,4,2,24,3072]{4,3,1,2,0:T(8,128)(2,1)}, bf16[2,4,2,24,3072]{4,3,1,2,0:T(8,128)(2,1)}, u32[]{:S(2)}, u32[]{:S(2)}) collective-permute-start(bf16[2,4,2,24,3072]{4,3,1,2,0:T(8,128)(2,1)} %bitcast.213), channel_id=1, source_target_pairs={{0,8},{8,0},{1,9},{9,1},{2,10},{10,2},{3,11},{11,3},{4,12},{12,4},... | collective-permute-start | bytes 7077896 | tf_op jit(solution)/shard_map/ppermute | solution.py:27
  168.1 15.8 %collective-permute-start.24 = (bf16[2,4,96,384]{3,2,1,0:T(8,128)(2,1)}, bf16[2,4,96,384]{3,2,1,0:T(8,128)(2,1)S(1)}, u32[]{:S(2)}, u32[]{:S(2)}) collective-permute-start(bf16[2,4,96,384]{3,2,1,0:T(8,128)(2,1)} %fusion.46), channel_id=1, source_target_pairs={{0,1},{1,0},{2,3},{3,2},{4,5},{5,4},{6,7},{7,6},{8,9},{9,8},{10,11... | collective-permute-start | bytes 1769480 | tf_op jit(solution)/shard_map/ppermute | solution.py:27
  168.4 15.5 %collective-permute-start.25 = (bf16[4,2,96,384]{3,2,0,1:T(8,128)(2,1)}, bf16[4,2,96,384]{3,2,0,1:T(8,128)(2,1)S(1)}, u32[]{:S(2)}, u32[]{:S(2)}) collective-permute-start(bf16[4,2,96,384]{3,2,0,1:T(8,128)(2,1)} %fusion.47), channel_id=1, source_target_pairs={{0,16},{16,0},{1,17},{17,1},{2,18},{18,2},{3,19},{19,3},{4,20},{20... | collective-permute-start | bytes 1769480 | tf_op jit(solution)/shard_map/ppermute | solution.py:27
  192.9 22.4 %collective-permute-start.29 = (bf16[2,4,24,1536]{3,2,1,0:T(8,128)(2,1)S(1)}, bf16[2,4,24,1536]{3,2,1,0:T(8,128)(2,1)}, u32[]{:S(2)}, u32[]{:S(2)}) collective-permute-start(bf16[2,4,24,1536]{3,2,1,0:T(8,128)(2,1)S(1)} %fusion.48), channel_id=1, source_target_pairs={{0,1},{1,0},{2,3},{3,2},{4,5},{5,4},{6,7},{7,6},{8,9},{9,8},{10,11... | collective-permute-start | bytes 1769480 | tf_op jit(solution)/shard_map/ppermute | solution.py:27
  194.6 20.6 %collective-permute-start.30 = (bf16[4,2,24,1536]{3,2,0,1:T(8,128)(2,1)S(1)}, bf16[4,2,24,1536]{3,2,0,1:T(8,128)(2,1)}, u32[]{:S(2)}, u32[]{:S(2)}) collective-permute-start(bf16[4,2,24,1536]{3,2,0,1:T(8,128)(2,1)S(1)} %fusion.49), channel_id=1, source_target_pairs={{0,16},{16,0},{1,17},{17,1},{2,18},{18,2},{3,19},{19,3},{4,20},{20... | collective-permute-start | bytes 1769480 | tf_op jit(solution)/shard_map/ppermute | solution.py:27
  198.1 17.1 %collective-permute-start.27 = (bf16[4,96,384]{2,1,0:T(8,128)(2,1)}, bf16[4,96,384]{2,1,0:T(8,128)(2,1)}, u32[]{:S(2)}, u32[]{:S(2)}) collective-permute-start(bf16[4,96,384]{2,1,0:T(8,128)(2,1)} %fusion.62), channel_id=1, source_target_pairs={{0,16},{16,0},{1,17},{17,1},{2,18},{18,2},{3,19},{19,3},{4,20},{20... | collective-permute-start | bytes 884744 | tf_op jit(solution)/shard_map/ppermute | solution.py:27
  199.6 15.7 %collective-permute-start.28 = (bf16[4,96,384]{2,1,0:T(8,128)(2,1)S(1)}, bf16[4,96,384]{2,1,0:T(8,128)(2,1)}, u32[]{:S(2)}, u32[]{:S(2)}) collective-permute-start(bf16[4,96,384]{2,1,0:T(8,128)(2,1)S(1)} %fusion.63), channel_id=1, source_target_pairs={{0,1},{1,0},{2,3},{3,2},{4,5},{5,4},{6,7},{7,6},{8,9},{9,8},{10,11... | collective-permute-start | bytes 884744 | tf_op jit(solution)/shard_map/ppermute | solution.py:27
  228.7 24.4 %collective-permute-start.31 = (bf16[2,4,2,24,3072]{4,3,2,1,0:T(8,128)(2,1)}, bf16[2,4,2,24,3072]{4,3,2,1,0:T(8,128)(2,1)}, u32[]{:S(2)}, u32[]{:S(2)}) collective-permute-start(bf16[2,4,2,24,3072]{4,3,2,1,0:T(8,128)(2,1)} %get-tuple-element.174), channel_id=1, source_target_pairs={{0,8},{8,0},{1,9},{9,1},{2,10},{10,2},{3,11},{11,3},{4,12},{12,4},... | collective-permute-start | bytes 7077896 | tf_op jit(solution)/shard_map/ppermute | solution.py:27
  244.1 6.7 %collective-permute-start.32 = (bf16[2,4,2,24,256]{4,3,2,1,0:T(8,128)(2,1)S(1)}, bf16[2,4,2,24,256]{4,3,2,1,0:T(8,128)(2,1)S(1)}, u32[]{:S(2)}, u32[]{:S(2)}) collective-permute-start(bf16[2,4,2,24,256]{4,3,2,1,0:T(8,128)(2,1)S(1)} %get-tuple-element.433), channel_id=1, source_target_pairs={{0,8},{8,0},{1,9},{9,1},{2,10},{10,2},{3,11},{11,3},{4,12},{12,4},... | collective-permute-start | bytes 589832 | tf_op jit(solution)/shard_map/ppermute | solution.py:27
  244.2 17.5 %collective-permute-start.36 = (bf16[4,24,1536]{2,1,0:T(8,128)(2,1)}, bf16[4,24,1536]{2,1,0:T(8,128)(2,1)S(1)}, u32[]{:S(2)}, u32[]{:S(2)}) collective-permute-start(bf16[4,24,1536]{2,1,0:T(8,128)(2,1)} %fusion.64), channel_id=1, source_target_pairs={{0,16},{16,0},{1,17},{17,1},{2,18},{18,2},{3,19},{19,3},{4,20},{20... | collective-permute-start | bytes 884744 | tf_op jit(solution)/shard_map/ppermute | solution.py:27
  244.9 16.8 %collective-permute-start.37 = (bf16[4,24,1536]{2,1,0:T(8,128)(2,1)}, bf16[4,24,1536]{2,1,0:T(8,128)(2,1)S(1)}, u32[]{:S(2)}, u32[]{:S(2)}) collective-permute-start(bf16[4,24,1536]{2,1,0:T(8,128)(2,1)} %fusion.65), channel_id=1, source_target_pairs={{0,1},{1,0},{2,3},{3,2},{4,5},{5,4},{6,7},{7,6},{8,9},{9,8},{10,11... | collective-permute-start | bytes 884744 | tf_op jit(solution)/shard_map/ppermute | solution.py:27
  245.6 13.1 %collective-permute-start.33 = (bf16[96,768]{1,0:T(8,128)(2,1)}, bf16[96,768]{1,0:T(8,128)(2,1)S(1)}, u32[]{:S(2)}, u32[]{:S(2)}) collective-permute-start(bf16[96,768]{1,0:T(8,128)(2,1)} %get-tuple-element.179), channel_id=1, source_target_pairs={{0,2},{2,4},{4,6},{6,0},{1,3},{3,5},{5,7},{7,1},{8,10},{10,12},{12... | collective-permute-start | bytes 442376 | tf_op jit(solution)/shard_map/ppermute | solution.py:27
  250.8 10.9 %collective-permute-start.34 = (bf16[96,768]{1,0:T(8,128)(2,1)S(1)}, bf16[96,768]{1,0:T(8,128)(2,1)S(1)}, u32[]{:S(2)}, u32[]{:S(2)}) collective-permute-start(bf16[96,768]{1,0:T(8,128)(2,1)S(1)} %copy-done.56), channel_id=1, source_target_pairs={{0,4},{2,6},{4,0},{6,2},{1,5},{3,7},{5,1},{7,3},{8,12},{10,14},{12... | collective-permute-start | bytes 442376 | tf_op jit(solution)/shard_map/ppermute | solution.py:27
  253.1 8.6 %collective-permute-start.35 = (bf16[96,768]{1,0:T(8,128)(2,1)S(1)}, bf16[96,768]{1,0:T(8,128)(2,1)S(1)}, u32[]{:S(2)}, u32[]{:S(2)}) collective-permute-start(bf16[96,768]{1,0:T(8,128)(2,1)S(1)} %get-tuple-element.181), channel_id=1, source_target_pairs={{0,6},{2,0},{4,2},{6,4},{1,7},{3,1},{5,3},{7,5},{8,14},{10,8},{12,... | collective-permute-start | bytes 442376 | tf_op jit(solution)/shard_map/ppermute | solution.py:27
  261.8 14.2 %collective-permute-start.38 = (bf16[2,4,24,1664]{3,2,1,0:T(8,128)(2,1)S(1)}, bf16[2,4,24,1664]{3,2,1,0:T(8,128)(2,1)S(1)}, u32[]{:S(2)}, u32[]{:S(2)}) collective-permute-start(bf16[2,4,24,1664]{3,2,1,0:T(8,128)(2,1)S(1)} %fusion.44), channel_id=1, source_target_pairs={{0,1},{1,0},{2,3},{3,2},{4,5},{5,4},{6,7},{7,6},{8,9},{9,8},{10,11... | collective-permute-start | bytes 1916936 | tf_op jit(solution)/shard_map/ppermute | solution.py:27
  262.7 14.1 %collective-permute-start.39 = (bf16[4,2,24,1664]{3,2,1,0:T(8,128)(2,1)S(1)}, bf16[4,2,24,1664]{3,2,1,0:T(8,128)(2,1)S(1)}, u32[]{:S(2)}, u32[]{:S(2)}) collective-permute-start(bf16[4,2,24,1664]{3,2,1,0:T(8,128)(2,1)S(1)} %fusion.45), channel_id=1, source_target_pairs={{0,16},{16,0},{1,17},{17,1},{2,18},{18,2},{3,19},{19,3},{4,20},{20... | collective-permute-start | bytes 1916936 | tf_op jit(solution)/shard_map/ppermute | solution.py:27
  263.6 22.2 %collective-permute-start.42 = (bf16[24,3072]{1,0:T(8,128)(2,1)S(1)}, bf16[24,3072]{1,0:T(8,128)(2,1)S(1)}, u32[]{:S(2)}, u32[]{:S(2)}) collective-permute-start(bf16[24,3072]{1,0:T(8,128)(2,1)S(1)} %get-tuple-element.204), channel_id=1, source_target_pairs={{0,2},{2,4},{4,6},{6,0},{1,3},{3,5},{5,7},{7,1},{8,10},{10,12},{12... | collective-permute-start | bytes 442376 | tf_op jit(solution)/shard_map/ppermute | solution.py:27
  266.3 19.4 %collective-permute-start.43 = (bf16[24,3072]{1,0:T(8,128)(2,1)S(1)}, bf16[24,3072]{1,0:T(8,128)(2,1)S(1)}, u32[]{:S(2)}, u32[]{:S(2)}) collective-permute-start(bf16[24,3072]{1,0:T(8,128)(2,1)S(1)} %get-tuple-element.205), channel_id=1, source_target_pairs={{0,4},{2,6},{4,0},{6,2},{1,5},{3,7},{5,1},{7,3},{8,12},{10,14},{12... | collective-permute-start | bytes 442376 | tf_op jit(solution)/shard_map/ppermute | solution.py:27
  268.8 16.9 %collective-permute-start.44 = (bf16[24,3072]{1,0:T(8,128)(2,1)S(1)}, bf16[24,3072]{1,0:T(8,128)(2,1)S(1)}, u32[]{:S(2)}, u32[]{:S(2)}) collective-permute-start(bf16[24,3072]{1,0:T(8,128)(2,1)S(1)} %get-tuple-element.206), channel_id=1, source_target_pairs={{0,6},{2,0},{4,2},{6,4},{1,7},{3,1},{5,3},{7,5},{8,14},{10,8},{12,... | collective-permute-start | bytes 442376 | tf_op jit(solution)/shard_map/ppermute | solution.py:27
  277.2 7.5 %collective-permute-start.40 = (bf16[4,24,1664]{2,1,0:T(8,128)(2,1)S(1)}, bf16[4,24,1664]{2,1,0:T(8,128)(2,1)S(1)}, u32[]{:S(2)}, u32[]{:S(2)}) collective-permute-start(bf16[4,24,1664]{2,1,0:T(8,128)(2,1)S(1)} %fusion.51), channel_id=1, source_target_pairs={{0,16},{16,0},{1,17},{17,1},{2,18},{18,2},{3,19},{19,3},{4,20},{20... | collective-permute-start | bytes 958472 | tf_op jit(solution)/shard_map/ppermute | solution.py:27
  277.9 7.0 %collective-permute-start.41 = (bf16[4,24,1664]{2,1,0:T(8,128)(2,1)S(1)}, bf16[4,24,1664]{2,1,0:T(8,128)(2,1)S(1)}, u32[]{:S(2)}, u32[]{:S(2)}) collective-permute-start(bf16[4,24,1664]{2,1,0:T(8,128)(2,1)S(1)} %fusion.52), channel_id=1, source_target_pairs={{0,1},{1,0},{2,3},{3,2},{4,5},{5,4},{6,7},{7,6},{8,9},{9,8},{10,11... | collective-permute-start | bytes 958472 | tf_op jit(solution)/shard_map/ppermute | solution.py:27
  285.8 12.3 %collective-permute-start.45 = (bf16[24,3328]{1,0:T(8,128)(2,1)S(1)}, bf16[24,3328]{1,0:T(8,128)(2,1)}, u32[]{:S(2)}, u32[]{:S(2)}) collective-permute-start(bf16[24,3328]{1,0:T(8,128)(2,1)S(1)} %get-tuple-element.207), channel_id=1, source_target_pairs={{0,2},{2,4},{4,6},{6,0},{1,3},{3,5},{5,7},{7,1},{8,10},{10,12},{12... | collective-permute-start | bytes 479240 | tf_op jit(solution)/shard_map/ppermute | solution.py:27
  289.8 12.0 %collective-permute-start.46 = (bf16[24,3328]{1,0:T(8,128)(2,1)}, bf16[24,3328]{1,0:T(8,128)(2,1)}, u32[]{:S(2)}, u32[]{:S(2)}) collective-permute-start(bf16[24,3328]{1,0:T(8,128)(2,1)} %get-tuple-element.208), channel_id=1, source_target_pairs={{0,4},{2,6},{4,0},{6,2},{1,5},{3,7},{5,1},{7,3},{8,12},{10,14},{12... | collective-permute-start | bytes 479240 | tf_op jit(solution)/shard_map/ppermute | solution.py:27
  293.5 10.6 %collective-permute-start.47 = (bf16[24,3328]{1,0:T(8,128)(2,1)S(1)}, bf16[24,3328]{1,0:T(8,128)(2,1)}, u32[]{:S(2)}, u32[]{:S(2)}) collective-permute-start(bf16[24,3328]{1,0:T(8,128)(2,1)S(1)} %get-tuple-element.209), channel_id=1, source_target_pairs={{0,6},{2,0},{4,2},{6,4},{1,7},{3,1},{5,3},{7,5},{8,14},{10,8},{12,... | collective-permute-start | bytes 479240 | tf_op jit(solution)/shard_map/ppermute | solution.py:27
  (96 other events, 720.9 us)
Sparse Core Ops, SparseCore 0:
  11.4 81.3 all-gather.1
